TPU v7x, 32 devices: a whole 2x2x4 slice. The times are simulated.
32 devices in a mesh: dp: 4 (over x, core), seq: 8 (over z, y).
Axes of the slice: x: 2, y: 2, z: 4, core: 2. Of those that a mesh axis runs over, the one named last changes fastest.
Arguments:
- queries: bfloat16 [4, 1536, 2048], P('dp', 'seq'), may hold values from -24 to 24
- key_rows: bfloat16 [4, 1536, 2048], P('dp', 'seq'), may hold values from -24 to 24
- value_rows: bfloat16 [4, 1536, 2048], P('dp', 'seq'), may hold values from -6 to 6
- out_weight: bfloat16 [2048, 3072], P('seq'), may hold values from -3 to 3
- cotangent: bfloat16 [4, 1536, 3072], P('dp', 'seq'), may hold values from -0.119628906 to 0.119628906
- tile_lists: int32 [16, 24, 16], replicated, may hold values from 0 to 23, as said below
- live_counts: int32 [16, 24], replicated, may hold values from 1 to 16, as said below
Outputs:
- block_out: bfloat16 [4, 1536, 3072], P('dp', 'seq')
- grad_queries: bfloat16 [4, 1536, 2048], P('dp', 'seq')
- grad_keys: bfloat16 [4, 1536, 2048], P('dp', 'seq')
- grad_values: bfloat16 [4, 1536, 2048], P('dp', 'seq')
- grad_weight: float32 [2048, 3072], P('seq')
Inputs may be any that keep to these rules, and one draw needn't show every extreme that they name: `tile_lists`: the 16 entries of a list are distinct tile numbers, and the first is the query tile itself. `live_counts`: every head has a query tile whose 16 entries are all live.
All inputs are finite; a program needn't handle non-finite values.
Results may differ from a plain program's by a relative error of at most 0.015.
Values may be sent and summed in bfloat16 or wider, within the bound.
No kernel may reach another device: no remote copies, remote signals or barrier semaphores. Data moves between devices by JAX's collectives and lax.ppermute only.
A program may use at most 256 MiB of HBM per device.

v0:
```python
import jax
import jax.numpy as jnp
from jax import lax
from jax.sharding import PartitionSpec as P

HEADS = 16
HDIM = 128
TILE = 64


def tile_weights(query_tiles, key_tiles, tile_list, live_count, score_scale):
    scores = (
        jnp.einsum("bie,bsje->bisj", query_tiles, key_tiles, preferred_element_type=jnp.float32)
        * score_scale
    )
    slot_index = lax.broadcasted_iota(jnp.int32, tile_list.shape, 1)
    live_mask = (slot_index < live_count[:, None])[:, None, :, None]
    masked = jnp.where(live_mask, scores, -jnp.inf)
    row_max = jnp.max(masked, axis=(2, 3), keepdims=True)
    weights = jnp.where(live_mask, jnp.exp(scores - row_max), 0.0)
    return weights / jnp.sum(weights, axis=(2, 3), keepdims=True)


def tile_onehot(tile_list, block_count):
    tile_number = lax.broadcasted_iota(jnp.int32, (1, 1, block_count), 2)
    return (tile_list[:, :, None] == tile_number).astype(jnp.bfloat16)


def select_tiles(matrix, onehot):
    block_count = matrix.shape[0] // TILE
    tiles = matrix.reshape(block_count, TILE, matrix.shape[1])
    picked = jnp.einsum("bst,tje->bsje", onehot, tiles, preferred_element_type=jnp.float32)
    return picked.astype(jnp.bfloat16)


def add_to_tiles(terms, onehot):
    return jnp.einsum(
        "bst,bsje->tje", onehot.astype(jnp.float32), terms, precision=lax.Precision.HIGHEST
    )


def head_forward(head_query, head_keys, head_values, tile_list, live_count):
    feature_width = head_query.shape[1]
    score_scale = feature_width ** (-0.5)
    query_tiles = head_query.reshape(-1, TILE, feature_width)
    onehot = tile_onehot(tile_list, query_tiles.shape[0])
    weights = tile_weights(
        query_tiles, select_tiles(head_keys, onehot), tile_list, live_count, score_scale
    )
    rounded = weights.astype(jnp.bfloat16)
    result = jnp.einsum(
        "bisj,bsje->bie",
        rounded,
        select_tiles(head_values, onehot),
        preferred_element_type=jnp.float32,
    )
    return result.astype(jnp.bfloat16).reshape(head_query.shape)


def head_backward(head_query, head_keys, head_values, head_grad, tile_list, live_count):
    feature_width = head_query.shape[1]
    score_scale = feature_width ** (-0.5)
    block_count = head_query.shape[0] // TILE
    query_tiles = head_query.reshape(block_count, TILE, feature_width)
    grad_tiles = head_grad.reshape(block_count, TILE, feature_width)
    onehot = tile_onehot(tile_list, block_count)
    key_tiles = select_tiles(head_keys, onehot)
    value_tiles = select_tiles(head_values, onehot)
    weights = tile_weights(query_tiles, key_tiles, tile_list, live_count, score_scale)
    rounded = weights.astype(jnp.bfloat16)
    grad_probs = jnp.einsum(
        "bie,bsje->bisj", grad_tiles, value_tiles, preferred_element_type=jnp.float32
    )
    row_dot = jnp.sum(weights * grad_probs, axis=(2, 3), keepdims=True)
    grad_scores = (weights * (grad_probs - row_dot)).astype(jnp.bfloat16)
    grad_query = (
        jnp.einsum("bisj,bsje->bie", grad_scores, key_tiles, preferred_element_type=jnp.float32)
        * score_scale
    )
    key_terms = (
        jnp.einsum("bisj,bie->bsje", grad_scores, query_tiles, preferred_element_type=jnp.float32)
        * score_scale
    )
    value_terms = jnp.einsum(
        "bisj,bie->bsje", rounded, grad_tiles, preferred_element_type=jnp.float32
    )
    grad_key = add_to_tiles(key_terms, onehot)
    grad_value = add_to_tiles(value_terms, onehot)
    return (
        grad_query.astype(jnp.bfloat16).reshape(head_query.shape),
        grad_key.astype(jnp.bfloat16).reshape(head_query.shape),
        grad_value.astype(jnp.bfloat16).reshape(head_query.shape),
    )


def column(matrix, head_index):
    return matrix[:, head_index * HDIM : (head_index + 1) * HDIM]


def shards(queries, key_rows, value_rows, out_weight, cotangent, tile_lists, live_counts):
    group_count = lax.axis_size("seq")
    seq_rank = lax.axis_index("seq")
    local_heads = HEADS // group_count
    head_q, head_k, head_v = (
        lax.all_to_all(queries, "seq", split_axis=2, concat_axis=1, tiled=True),
        lax.all_to_all(key_rows, "seq", split_axis=2, concat_axis=1, tiled=True),
        lax.all_to_all(value_rows, "seq", split_axis=2, concat_axis=1, tiled=True),
    )
    head_q, head_k, head_v = (head_q[0], head_k[0], head_v[0])
    my_tiles = lax.dynamic_slice_in_dim(tile_lists, seq_rank * local_heads, local_heads, 0)
    my_counts = lax.dynamic_slice_in_dim(live_counts, seq_rank * local_heads, local_heads, 0)
    attn_heads = jnp.concatenate(
        [
            head_forward(
                column(head_q, head_index),
                column(head_k, head_index),
                column(head_v, head_index),
                my_tiles[head_index],
                my_counts[head_index],
            )
            for head_index in range(local_heads)
        ],
        axis=1,
    )
    tok_rows = cotangent.shape[1]
    feature_width = out_weight.shape[1]
    group_cols = out_weight.shape[0]
    grad_rows_local = cotangent[0]
    attn_tokens = lax.all_to_all(attn_heads[None], "seq", split_axis=1, concat_axis=2, tiled=True)[
        0
    ]
    shard_rows = lax.all_gather(out_weight, "seq", axis=0, tiled=True)
    row_count = shard_rows.shape[0]
    block_count = row_count // group_cols
    partial_value = jnp.einsum(
        "tbc,bcd->btd",
        attn_tokens.reshape(tok_rows, block_count, group_cols),
        shard_rows.reshape(block_count, group_cols, feature_width),
        preferred_element_type=jnp.float32,
    )
    partial_value = lax.optimization_barrier(partial_value.astype(jnp.bfloat16))
    mixed_acc = jnp.sum(partial_value.astype(jnp.float32), axis=0)
    grad_cols = lax.dot_general(
        grad_rows_local, shard_rows, (((1,), (1,)), ((), ())), preferred_element_type=jnp.float32
    ).astype(jnp.bfloat16)
    grad_tokens = grad_cols
    mixed_rows, grad_tokens = (mixed_acc, grad_tokens)
    grad_heads = lax.all_to_all(grad_tokens[None], "seq", split_axis=2, concat_axis=1, tiled=True)[
        0
    ]
    partial_weight = lax.dot_general(
        attn_tokens, grad_rows_local, (((0,), (0,)), ((), ())), preferred_element_type=jnp.float32
    )
    weight_acc = lax.psum_scatter(
        partial_weight.astype(jnp.bfloat16), "seq", scatter_dimension=0, tiled=True
    )
    block_out = mixed_rows.astype(jnp.bfloat16)[None]
    grad_parts = [
        head_backward(
            column(head_q, head_index),
            column(head_k, head_index),
            column(head_v, head_index),
            column(grad_heads, head_index),
            my_tiles[head_index],
            my_counts[head_index],
        )
        for head_index in range(local_heads)
    ]
    grad_q = jnp.concatenate([entry[0] for entry in grad_parts], axis=1)
    grad_k = jnp.concatenate([entry[1] for entry in grad_parts], axis=1)
    grad_v = jnp.concatenate([entry[2] for entry in grad_parts], axis=1)
    back_q, back_k, back_v = (
        lax.all_to_all(grad_q[None], "seq", split_axis=1, concat_axis=2, tiled=True),
        lax.all_to_all(grad_k[None], "seq", split_axis=1, concat_axis=2, tiled=True),
        lax.all_to_all(grad_v[None], "seq", split_axis=1, concat_axis=2, tiled=True),
    )
    grad_weight = lax.psum(weight_acc, "dp").astype(jnp.float32)
    return (block_out, back_q, back_k, back_v, grad_weight)


def solution(mesh):
    in_specs = (
        P("dp", "seq", None),
        P("dp", "seq", None),
        P("dp", "seq", None),
        P("seq", None),
        P("dp", "seq", None),
        P(),
        P(),
    )
    out_specs = (
        P("dp", "seq", None),
        P("dp", "seq", None),
        P("dp", "seq", None),
        P("dp", "seq", None),
        P("seq", None),
    )
    return jax.shard_map(shards, mesh=mesh, in_specs=in_specs, out_specs=out_specs, check_vma=False)
```

profile of v0, /device:TPU:0, one launch (start us, length us, event | category | flops | bytes accessed | tf_op | source)
XLA Modules:
  0.0 595.4 jit_solution(10785377035378020788)
XLA Ops:
  7.9 4.5 copy.188
  13.0 12.6 %reduce.4 = bf16[2048,192]{1,0:T(8,128)(2,1)} reduce(bf16[2048,1,192]{2,1,0:T(2,128)(2,1)S(1)} %bitcast.260, bf16[]{:T(256)} %broadcast.83), dimensions={1}, to_apply=%bitcast.211.reduce_sub_computation | reduce | bytes 1572866
  29.1 7.3 %all-to-all-start.1 = ((bf16[8,2,24576]{2,1,0:T(2,128)(2,1)}), bf16[8,2,24576]{2,1,0:T(2,128)(2,1)}, u32[]{:S(2)}, u32[]{:S(2)}) async-start(bf16[8,2,24576]{2,1,0:T(2,128)(2,1)} %reshape.164), calls=%async_computation.1 | async-start | bytes 1572864 | tf_op jit(solution)/shard_map/all_to_all | solution.py:105
  36.4 4.5 copy.183
  41.0 12.6 %reduce.5 = bf16[2048,192]{1,0:T(8,128)(2,1)} reduce(bf16[2048,1,192]{2,1,0:T(2,128)(2,1)S(1)} %bitcast.266, bf16[]{:T(256)} %broadcast.83), dimensions={1}, to_apply=%bitcast.213.reduce_sub_computation | reduce | bytes 1572866
  57.1 21.1 %all-to-all-done.1 = bf16[8,2,24576]{2,1,0:T(2,128)(2,1)} async-done(((bf16[8,2,24576]{2,1,0:T(2,128)(2,1)}), bf16[8,2,24576]{2,1,0:T(2,128)(2,1)}, u32[]{:S(2)}, u32[]{:S(2)}) %all-to-all-start.1) | async-done | bytes 786464 | tf_op jit(solution)/shard_map/all_to_all | solution.py:105
  82.6 4.5 copy.192
  87.2 12.6 %reduce.3 = bf16[2048,192]{1,0:T(8,128)(2,1)} reduce(bf16[2048,1,192]{2,1,0:T(2,128)(2,1)S(1)} %bitcast.267, bf16[]{:T(256)} %broadcast.83), dimensions={1}, to_apply=%bitcast.209.reduce_sub_computation | reduce | bytes 1572866
  103.3 7.8 %all-to-all-done = bf16[8,2,24576]{2,1,0:T(2,128)(2,1)} async-done(((bf16[8,2,24576]{2,1,0:T(2,128)(2,1)}), bf16[8,2,24576]{2,1,0:T(2,128)(2,1)}, u32[]{:S(2)}, u32[]{:S(2)}) %all-to-all-start) | async-done | bytes 786464 | tf_op jit(solution)/shard_map/all_to_all | solution.py:106
  118.0 4.5 reshape.165
  138.5 16.9 %all-to-all-done.2 = bf16[8,2,24576]{2,1,0:T(2,128)(2,1)} async-done(((bf16[8,2,24576]{2,1,0:T(2,128)(2,1)}), bf16[8,2,24576]{2,1,0:T(2,128)(2,1)}, u32[]{:S(2)}, u32[]{:S(2)}) %all-to-all-start.2) | async-done | bytes 786464 | tf_op jit(solution)/shard_map/all_to_all | solution.py:107
  155.3 4.5 reshape.163
  168.6 4.5 convolution_convert_fusion.4
  175.1 6.7 %select_reduce_fusion.1 = (f32[24,64]{1,0:T(8,128)S(1)}, f32[24,16,64,64]{3,2,1,0:T(8,128)}) fusion(pred[24,16]{1,0:T(8,128)(4,1)S(1)} %get-tuple-element.28, bf16[24,64,128,1]{2,1,3,0:T(8,128)(2,1)S(1)} %bitcast.306, bf16[24,16,64,128]{3,1,2,0:T(8,128)(2,1)S(1)} %convolution_convert_fusion.5), kind=kOutput, calls=%fused_computation.19 | convolution fusion | flops 407370240 | bytes 12982656 | tf_op jit(solution)/shard_map/bie,bsje->bisj/dot_general | solution.py:13
  185.2 10.8 %bitcast_reduce_fusion.1 = f32[24,64]{1,0:T(8,128)S(1)} fusion(f32[24,16,64,64]{3,2,1,0:T(8,128)} %get-tuple-element.20, f32[24,64]{1,0:T(8,128)S(1)} %get-tuple-element.19, pred[24,16]{1,0:T(8,128)(4,1)S(1)} %get-tuple-element.28), kind=kLoop, calls=%fused_computation.3 | loop fusion | flops 6289920 | bytes 6304128 | tf_op jit(solution)/shard_map/reduce_sum | solution.py:21
  199.3 8.7 %fusion.88 = bf16[24,64,128]{2,1,0:T(8,128)(2,1)S(1)} fusion(bf16[24,16,64,128]{3,1,2,0:T(8,128)(2,1)} %convolution_convert_fusion.4, f32[24,16,64,64]{3,2,1,0:T(8,128)} %get-tuple-element.20, f32[24,64]{1,0:T(8,128)S(1)} %bitcast_reduce_fusion.1, f32[24,64]{1,0:T(8,128)S(1)} %get-tuple-element.19, pred[24,16]{1,0:T(8,128)(4,1)S(1)} %get-tuple-element.28), kind=kOutput, calls=%fused_computation.69 | convolution fusion | flops 410714112 | bytes 12988800 | tf_op jit(solution)/shard_map/bisj,bsje->bie/dot_general | solution.py:51
  208.1 5.1 fusion.83
  213.3 8.9 %copy.363 = bf16[1,1536,256]{2,0,1:T(2,128)(2,1)S(1)} copy(bf16[1,1536,256]{2,1,0:T(8,128)(2,1)S(1)} %maximum_bitcast_fusion) | data formatting | bytes 1572864 | tf_op jit(solution)/shard_map/broadcast_in_dim | solution.py:129
  222.2 8.1 %reduce.6 = bf16[1536,256]{1,0:T(8,128)(2,1)S(1)} reduce(bf16[1536,1,256]{2,1,0:T(2,128)(2,1)S(1)} %bitcast.273, bf16[]{:T(256)} %broadcast.83), dimensions={1}, to_apply=%bitcast.252.reduce_sub_computation | reduce | bytes 1572866
  230.5 23.2 %all_to_all.129 = bf16[8,2,24576]{2,1,0:T(2,128)(2,1)S(1)} all-to-all(bf16[8,2,24576]{2,1,0:T(2,128)(2,1)S(1)} %reshape.168), channel_id=1, replica_groups=mesh['dp'=4,'seq'=8] {'seq'}, dimensions={0} | all-to-all | bytes 1572864 | tf_op jit(solution)/shard_map/all_to_all | solution.py:129
  255.6 6.4 %convolution_convert_fusion = bf16[2048,3072]{1,0:T(8,128)(2,1)} fusion(bf16[192,2048]{1,0:T(8,128)(2,1)S(1)} %bitcast.280, bf16[1,192,3072]{2,1,0:T(8,128)(2,1)S(1)} %copy-done), kind=kOutput, calls=%fused_computation.20 | convolution fusion | flops 2422210560 | bytes 14548992 | tf_op jit(solution)/shard_map/dot_general | solution.py:151
  262.1 9.7 %fusion.30 = bf16[1,192,2048]{2,1,0:T(8,128)(2,1)} fusion(bf16[2048,3072]{1,0:T(8,128)(2,1)} %all-gather.2.cloned.1.call-done, bf16[1,192,3072]{2,1,0:T(8,128)(2,1)S(1)} %copy-done), kind=kOutput, calls=%fused_computation.51 | convolution fusion | flops 2416312320 | bytes 14548992 | tf_op jit(solution)/shard_map/dot_general | solution.py:143
  271.8 4.6 copy.207
  276.4 11.6 %reduce.7 = bf16[2048,192]{1,0:T(8,128)(2,1)S(1)} reduce(bf16[2048,1,192]{2,1,0:T(2,128)(2,1)S(1)} %bitcast.264, bf16[]{:T(256)} %broadcast.83), dimensions={1}, to_apply=%bitcast.217.reduce_sub_computation | reduce | bytes 1572866
  289.2 45.9 %all_to_all.130 = bf16[8,2,24576]{2,1,0:T(2,128)(2,1)S(1)} all-to-all(bf16[8,2,24576]{2,1,0:T(2,128)(2,1)S(1)} %reshape.170), channel_id=1, replica_groups=mesh['dp'=4,'seq'=8] {'seq'}, dimensions={0} | all-to-all | bytes 1572864 | tf_op jit(solution)/shard_map/all_to_all | solution.py:148
  342.4 7.4 %fusion.27 = f32[24,16,64,128]{3,2,1,0:T(8,128)S(1)} fusion(bf16[24,64,128,1]{2,1,3,0:T(8,128)(2,1)S(1)} %bitcast.315, f32[24,16,64,64]{3,2,1,0:T(8,128)} %get-tuple-element.20, f32[24,64]{1,0:T(8,128)S(1)} %copy-done.26, f32[24,64]{1,0:T(8,128)S(1)} %copy-done.24, pred[24,16]{1,0:T(8,128)(4,1)S(1)} %get-tuple-element.28), kind=kOutput, calls=%fused_computation.47 | convolution fusion | flops 410517504 | bytes 19280256 | tf_op jit(solution)/shard_map/bisj,bie->bsje/dot_general | solution.py:84
  349.8 10.0 %fusion.74 = bf16[24,64,128]{2,0,1:T(8,128)(2,1)S(1)} fusion(f32[24,16,64,128]{3,2,1,0:T(8,128)S(1)} %fusion.27, s32[24,16]{0,1:T(8,128)S(1)} %get-tuple-element.13), kind=kOutput, calls=%fused_computation.65 | convolution fusion | flops 906175488 | bytes 12977664 | tf_op jit(solution)/shard_map/bst,bsje->tje/dot_general | solution.py:37
  360.0 13.3 %multiply_reduce_fusion.1 = (f32[24,64]{1,0:T(8,128)S(1)}, f32[24,64,16,64]{1,3,2,0:T(8,128)}) fusion(f32[24,64]{1,0:T(8,128)S(1)} %copy-done.26, f32[24,64]{1,0:T(8,128)S(1)} %copy-done.24, f32[24,16,64,64]{3,2,1,0:T(8,128)} %get-tuple-element.20, pred[24,16]{1,0:T(8,128)(4,1)S(1)} %get-tuple-element.28, bf16[24,64,128,1]{2,1,3,0:T(8,128)(2,1)} %bitcast.316, ...), kind=kOutput, calls=%fused_computation.15 | convolution fusion | flops 412088832 | bytes 19286400 | tf_op jit(solution)/shard_map/bie,bsje->bisj/dot_general | solution.py:71
  373.2 13.4 %multiply_convert_fusion.1 = bf16[24,64,16,64]{1,3,2,0:T(8,128)(2,1)} fusion(f32[24,64,16,64]{1,3,2,0:T(8,128)} %get-tuple-element.24, f32[24,64]{1,0:T(8,128)S(1)} %get-tuple-element.23, f32[24,64]{1,0:T(8,128)S(1)} %copy-done.26, f32[24,64]{1,0:T(8,128)S(1)} %copy-done.24, f32[24,16,64,64]{3,2,1,0:T(8,128)} %get-tuple-element.20, ...), kind=kLoop, calls=%fused_computation.14 | loop fusion | flops 11010048 | bytes 15747456 | tf_op jit(solution)/shard_map/convert_element_type | solution.py:75
  386.6 7.4 %fusion.65 = bf16[24,64,128]{2,1,0:T(8,128)(2,1)S(1)} fusion(bf16[24,64,16,64]{1,3,2,0:T(8,128)(2,1)} %multiply_convert_fusion.1, bf16[24,16,64,128]{3,1,2,0:T(8,128)(2,1)} %copy-done.7), kind=kOutput, calls=%fused_computation.62 | convolution fusion | flops 403046400 | bytes 9830400 | tf_op jit(solution)/shard_map/bisj,bsje->bie/dot_general | solution.py:77
  394.1 9.9 %multiply_reduce_fusion = (f32[24,64]{1,0:T(8,128)S(1)}, f32[24,64,16,64]{1,3,2,0:T(8,128)}) fusion(f32[24,64]{1,0:T(8,128)S(1)} %copy-done.22, f32[24,64]{1,0:T(8,128)S(1)} %copy-done.20, f32[24,16,64,64]{3,2,1,0:T(8,128)S(1)} %bitcast.258, pred[24,16]{1,0:T(8,128)(4,1)S(1)} %get-tuple-element.27, bf16[24,64,128,1]{2,1,3,0:T(8,128)(2,1)S(1)} %bitcast.313, ...), kind=kOutput, calls=%fused_computation.13 | convolution fusion | flops 412088832 | bytes 19286400 | tf_op jit(solution)/shard_map/bie,bsje->bisj/dot_general | solution.py:71
  404.0 10.1 %multiply_convert_fusion = bf16[24,64,16,64]{1,3,2,0:T(8,128)(2,1)} fusion(f32[24,64,16,64]{1,3,2,0:T(8,128)} %get-tuple-element.22, f32[24,64]{1,0:T(8,128)S(1)} %get-tuple-element.21, f32[24,64]{1,0:T(8,128)S(1)} %copy-done.22, f32[24,64]{1,0:T(8,128)S(1)} %copy-done.20, f32[24,16,64,64]{3,2,1,0:T(8,128)S(1)} %bitcast.258, ...), kind=kLoop, calls=%fused_computation.12 | loop fusion | flops 11010048 | bytes 15747456 | tf_op jit(solution)/shard_map/convert_element_type | solution.py:75
  414.1 6.9 %fusion.68 = bf16[24,64,128]{2,1,0:T(8,128)(2,1)S(1)} fusion(bf16[24,64,16,64]{1,3,2,0:T(8,128)(2,1)} %multiply_convert_fusion, bf16[24,16,64,128]{3,1,2,0:T(8,128)(2,1)} %copy-done.6), kind=kOutput, calls=%fused_computation.63 | convolution fusion | flops 403046400 | bytes 9830400 | tf_op jit(solution)/shard_map/bisj,bsje->bie/dot_general | solution.py:77
  421.1 8.9 %copy.362 = bf16[1,1536,256]{2,0,1:T(2,128)(2,1)S(1)} copy(bf16[1,1536,256]{2,1,0:T(8,128)(2,1)S(1)} %maximum_bitcast_fusion.1) | data formatting | bytes 1572864 | tf_op jit(solution)/shard_map/broadcast_in_dim | solution.py:173
  430.0 8.1 %reduce.8 = bf16[1536,256]{1,0:T(8,128)(2,1)S(1)} reduce(bf16[1536,1,256]{2,1,0:T(2,128)(2,1)S(1)} %bitcast.275, bf16[]{:T(256)} %broadcast.83), dimensions={1}, to_apply=%bitcast.251.reduce_sub_computation | reduce | bytes 1572866
  446.9 6.9 %fusion.24 = f32[24,16,64,128]{3,2,1,0:T(8,128)S(1)} fusion(bf16[24,64,128,1]{2,1,3,0:T(8,128)(2,1)} %bitcast.312, f32[24,16,64,64]{3,2,1,0:T(8,128)} %copy-done.2, f32[24,64]{1,0:T(8,128)} %copy-done.21, f32[24,64]{1,0:T(8,128)} %copy-done.19, pred[24,16]{1,0:T(8,128)(4,1)S(1)} %get-tuple-element.27), kind=kOutput, calls=%fused_computation.44 | convolution fusion | flops 410517504 | bytes 19280256 | tf_op jit(solution)/shard_map/bisj,bie->bsje/dot_general | solution.py:84
  453.8 10.0 %fusion.80 = bf16[24,64,128]{2,0,1:T(8,128)(2,1)S(1)} fusion(f32[24,16,64,128]{3,2,1,0:T(8,128)S(1)} %broadcast_multiply_fusion.1, s32[24,16]{0,1:T(8,128)S(1)} %get-tuple-element.13), kind=kOutput, calls=%fused_computation.67 | convolution fusion | flops 906175488 | bytes 12977664 | tf_op jit(solution)/shard_map/bst,bsje->tje/dot_general | solution.py:37
  464.7 10.0 %fusion.71 = bf16[24,64,128]{2,0,1:T(8,128)(2,1)S(1)} fusion(f32[24,16,64,128]{3,2,1,0:T(8,128)S(1)} %fusion.24, s32[24,16]{0,1:T(8,128)S(1)} %copy-done.18), kind=kOutput, calls=%fused_computation.64 | convolution fusion | flops 906175488 | bytes 12977664 | tf_op jit(solution)/shard_map/bst,bsje->tje/dot_general | solution.py:37
  474.9 9.1 %copy.360 = bf16[1,1536,256]{2,0,1:T(2,128)(2,1)S(1)} copy(bf16[1,1536,256]{2,1,0:T(8,128)(2,1)S(1)} %maximum_bitcast_fusion.3) | data formatting | bytes 1572864 | tf_op jit(solution)/shard_map/broadcast_in_dim | solution.py:175
  484.0 8.1 %reduce.10 = bf16[1536,256]{1,0:T(8,128)(2,1)S(1)} reduce(bf16[1536,1,256]{2,1,0:T(2,128)(2,1)S(1)} %bitcast.276, bf16[]{:T(256)} %broadcast.83), dimensions={1}, to_apply=%bitcast.249.reduce_sub_computation | reduce | bytes 1572866
  493.2 6.0 %all-to-all-start.7 = ((bf16[8,2,24576]{2,1,0:T(2,128)(2,1)}), bf16[8,2,24576]{2,1,0:T(2,128)(2,1)}, u32[]{:S(2)}, u32[]{:S(2)}) async-start(bf16[8,2,24576]{2,1,0:T(2,128)(2,1)} %reshape.176), calls=%async_computation.7 | async-start | bytes 1572864 | tf_op jit(solution)/shard_map/all_to_all | solution.py:175
  503.3 10.0 %fusion.77 = bf16[24,64,128]{2,0,1:T(8,128)(2,1)S(1)} fusion(f32[24,16,64,128]{3,2,1,0:T(8,128)S(1)} %broadcast_multiply_fusion, s32[24,16]{0,1:T(8,128)S(1)} %copy-done.18), kind=kOutput, calls=%fused_computation.66 | convolution fusion | flops 906175488 | bytes 12977664 | tf_op jit(solution)/shard_map/bst,bsje->tje/dot_general | solution.py:37
  513.5 8.9 %copy.361 = bf16[1,1536,256]{2,0,1:T(2,128)(2,1)S(1)} copy(bf16[1,1536,256]{2,1,0:T(8,128)(2,1)S(1)} %maximum_bitcast_fusion.2) | data formatting | bytes 1572864 | tf_op jit(solution)/shard_map/broadcast_in_dim | solution.py:174
  522.4 8.1 %reduce.9 = bf16[1536,256]{1,0:T(8,128)(2,1)S(1)} reduce(bf16[1536,1,256]{2,1,0:T(2,128)(2,1)S(1)} %bitcast.272, bf16[]{:T(256)} %broadcast.83), dimensions={1}, to_apply=%bitcast.250.reduce_sub_computation | reduce | bytes 1572866
  531.6 6.0 all-to-all-start.6
  538.3 10.8 %convolution_convert_fusion.1 = bf16[8,192,3072]{2,1,0:T(8,128)(2,1)} fusion(bf16[192,8,256]{2,0,1:T(8,128)(2,1)S(1)} %bitcast.269, bf16[8,256,3072]{2,1,0:T(8,128)(2,1)} %bitcast.259), kind=kOutput, calls=%fused_computation.21 | convolution fusion | flops 2420637696 | bytes 22806528 | tf_op jit(solution)/shard_map/tbc,bcd->btd/dot_general | solution.py:135
  549.1 6.9 %reduce_sum.58 = bf16[192,3072]{1,0:T(8,128)(2,1)} reduce(bf16[8,192,3072]{2,1,0:T(8,128)(2,1)} %convolution_convert_fusion.1, bf16[]{:T(256)} %constant.7.clone.1), dimensions={0}, to_apply=%region_4.5 | reduce | flops 4128768 | bytes 10616834 | tf_op jit(solution)/shard_map/reduce_sum | solution.py:142
  568.3 16.6 %all-reduce.2.cloned.1.call-done = bf16[256,3072]{1,0:T(8,128)(2,1)} async-done(((bf16[256,3072]{1,0:T(8,128)(2,1)}), bf16[256,3072]{1,0:T(8,128)(2,1)}) %all-reduce.2.cloned.1.call-update) | async-done | bytes 1572880 | tf_op jit(solution)/shard_map/psum | solution.py:177
  (146 shorter events, 99.8 us)
Async XLA Ops:
  7.2 248.4 %copy-start = (bf16[1,192,3072]{2,1,0:T(8,128)(2,1)S(1)}, bf16[1,192,3072]{2,1,0:T(8,128)(2,1)}, u32[]{:S(2)}) copy-start(bf16[1,192,3072]{2,1,0:T(8,128)(2,1)} %param.11) | copy-start | bytes 3538948
  7.2 254.9 %all-gather.2.cloned.1.call-start = ((), (), s32[]{:S(2)}) async-start(), calls=%async_computation.9 | async-start | bytes 14155776 | tf_op jit(solution)/shard_map/all_gather | solution.py:132
  29.1 49.0 %all-to-all-start.1 = ((bf16[8,2,24576]{2,1,0:T(2,128)(2,1)}), bf16[8,2,24576]{2,1,0:T(2,128)(2,1)}, u32[]{:S(2)}, u32[]{:S(2)}) async-start(bf16[8,2,24576]{2,1,0:T(2,128)(2,1)} %reshape.164), calls=%async_computation.1 | async-start | bytes 1572864 | tf_op jit(solution)/shard_map/all_to_all | solution.py:105
  78.2 33.0 %all-to-all-start = ((bf16[8,2,24576]{2,1,0:T(2,128)(2,1)}), bf16[8,2,24576]{2,1,0:T(2,128)(2,1)}, u32[]{:S(2)}, u32[]{:S(2)}) async-start(bf16[8,2,24576]{2,1,0:T(2,128)(2,1)} %reshape.166), calls=%async_computation | async-start | bytes 1572864 | tf_op jit(solution)/shard_map/all_to_all | solution.py:106
  111.2 44.1 %all-to-all-start.2 = ((bf16[8,2,24576]{2,1,0:T(2,128)(2,1)}), bf16[8,2,24576]{2,1,0:T(2,128)(2,1)}, u32[]{:S(2)}, u32[]{:S(2)}) async-start(bf16[8,2,24576]{2,1,0:T(2,128)(2,1)} %reshape.162), calls=%async_computation.2 | async-start | bytes 1572864 | tf_op jit(solution)/shard_map/all_to_all | solution.py:107
  115.4 422.4 %reduce-scatter.2.cloned.1.call-start = ((), (), s32[]{:S(2)}) async-start(), calls=%async_computation.10 | async-start | bytes 14155776 | tf_op jit(solution)/shard_map/reduce_scatter | solution.py:154
  116.2 0.6 copy-start.17
  163.2 3.6 copy-start.9
  164.9 10.1 %copy-start.8 = (bf16[1,8,192,256]{3,2,1,0:T(8,128)(2,1)S(1)}, bf16[1,8,192,256]{3,2,1,0:T(8,128)(2,1)}, u32[]{:S(2)}) copy-start(bf16[1,8,192,256]{3,2,1,0:T(8,128)(2,1)} %copy.190) | copy-start | bytes 2359300
  166.7 41.4 %copy-start.5 = (bf16[24,16,64,128]{3,1,2,0:T(8,128)(2,1)}, bf16[24,16,64,128]{3,1,2,0:T(8,128)(2,1)S(1)}, u32[]{:S(2)}) copy-start(bf16[24,16,64,128]{3,1,2,0:T(8,128)(2,1)S(1)} %convolution_convert_fusion.2) | copy-start | bytes 18874372
  168.6 13.2 %copy-start.6 = (bf16[24,16,64,128]{3,1,2,0:T(8,128)(2,1)}, bf16[24,16,64,128]{3,1,2,0:T(8,128)(2,1)S(1)}, u32[]{:S(2)}) copy-start(bf16[24,16,64,128]{3,1,2,0:T(8,128)(2,1)S(1)} %convolution_convert_fusion.3) | copy-start | bytes 18874372
  175.0 6.8 %copy-start.7 = (bf16[24,16,64,128]{3,1,2,0:T(8,128)(2,1)}, bf16[24,16,64,128]{3,1,2,0:T(8,128)(2,1)S(1)}, u32[]{:S(2)}) copy-start(bf16[24,16,64,128]{3,1,2,0:T(8,128)(2,1)S(1)} %convolution_convert_fusion.5) | copy-start | bytes 18874372
  175.1 6.7 %copy-start.14 = (bf16[1536,128]{1,0:T(8,128)(2,1)}, bf16[1536,128]{1,0:T(8,128)(2,1)S(1)}, u32[]{:S(2)}) copy-start(bf16[1536,128]{1,0:T(8,128)(2,1)S(1)} %get-tuple-element.9) | copy-start | bytes 1179652
  175.1 6.7 %copy-start.13 = (bf16[1536,128]{1,0:T(8,128)(2,1)}, bf16[1536,128]{1,0:T(8,128)(2,1)S(1)}, u32[]{:S(2)}) copy-start(bf16[1536,128]{1,0:T(8,128)(2,1)S(1)} %get-tuple-element.10) | copy-start | bytes 1179652
  181.8 17.5 %copy-start.23 = (f32[24,64]{1,0:T(8,128)}, f32[24,64]{1,0:T(8,128)S(1)}, u32[]{:S(2)}) copy-start(f32[24,64]{1,0:T(8,128)S(1)} %get-tuple-element.19) | copy-start | bytes 18436
  185.2 22.9 %copy-start.2 = (f32[24,16,64,64]{3,2,1,0:T(8,128)}, f32[24,16,64,64]{3,2,1,0:T(8,128)S(1)}, u32[]{:S(2)}) copy-start(f32[24,16,64,64]{3,2,1,0:T(8,128)S(1)} %get-tuple-element.18) | copy-start | bytes 18874372
  185.2 22.9 %copy-start.19 = (f32[24,64]{1,0:T(8,128)}, f32[24,64]{1,0:T(8,128)S(1)}, u32[]{:S(2)}) copy-start(f32[24,64]{1,0:T(8,128)S(1)} %get-tuple-element.17) | copy-start | bytes 18436
  196.0 3.3 copy-start.25
  199.3 8.8 %copy-start.21 = (f32[24,64]{1,0:T(8,128)}, f32[24,64]{1,0:T(8,128)S(1)}, u32[]{:S(2)}) copy-start(f32[24,64]{1,0:T(8,128)S(1)} %bitcast_reduce_fusion) | copy-start | bytes 18436
  254.6 0.9 copy-start.3
  271.8 70.5 %copy-start.24 = (f32[24,64]{1,0:T(8,128)S(1)}, f32[24,64]{1,0:T(8,128)}, u32[]{:S(2)}) copy-start(f32[24,64]{1,0:T(8,128)} %copy-done.23) | copy-start | bytes 18436
  271.8 70.5 %copy-start.26 = (f32[24,64]{1,0:T(8,128)S(1)}, f32[24,64]{1,0:T(8,128)}, u32[]{:S(2)}) copy-start(f32[24,64]{1,0:T(8,128)} %copy-done.25) | copy-start | bytes 18436
  341.3 18.6 %slice-start.3 = ((s8[6291456]{0:T(1024)(128)(4,1)}), s8[4194304]{0:T(1024)(128)(4,1)S(1)}, s32[]{:S(2)}) async-start(s8[6291456]{0:T(1024)(128)(4,1)} %bitcast.270), calls=%async_computation.15 | async-start | bytes 8388608
  342.4 7.4 %copy-start.16 = (bf16[1536,128]{1,0:T(8,128)(2,1)}, bf16[1536,128]{1,0:T(8,128)(2,1)S(1)}, u32[]{:S(2)}) copy-start(bf16[1536,128]{1,0:T(8,128)(2,1)S(1)} %get-tuple-element.5) | copy-start | bytes 1179652
  342.4 17.6 %slice-start.4 = ((s8[6291456]{0:T(1024)(128)(4,1)}), s8[2097152]{0:T(1024)(128)(4,1)S(1)}, s32[]{:S(2)}) async-start(s8[6291456]{0:T(1024)(128)(4,1)} %bitcast.270), calls=%async_computation.16 | async-start | bytes 4194304
  359.9 34.1 %slice-start = ((s8[12582912]{0:T(1024)(128)(4,1)}), s8[4194304]{0:T(1024)(128)(4,1)S(1)}, s32[]{:S(2)}) async-start(s8[12582912]{0:T(1024)(128)(4,1)} %bitcast.257), calls=%async_computation.12 | async-start | bytes 8388608
  360.0 34.1 %slice-start.1 = ((s8[12582912]{0:T(1024)(128)(4,1)}), s8[4194304]{0:T(1024)(128)(4,1)S(1)}, s32[]{:S(2)}) async-start(s8[12582912]{0:T(1024)(128)(4,1)} %bitcast.257), calls=%async_computation.13 | async-start | bytes 8388608
  373.2 20.8 %slice-start.2 = ((s8[12582912]{0:T(1024)(128)(4,1)}), s8[4194304]{0:T(1024)(128)(4,1)S(1)}, s32[]{:S(2)}) async-start(s8[12582912]{0:T(1024)(128)(4,1)} %bitcast.257), calls=%async_computation.14 | async-start | bytes 8388608
  386.6 7.5 %copy-start.15 = (bf16[1536,128]{1,0:T(8,128)(2,1)S(1)}, bf16[1536,128]{1,0:T(8,128)(2,1)}, u32[]{:S(2)}) copy-start(bf16[1536,128]{1,0:T(8,128)(2,1)} %get-tuple-element.6) | copy-start | bytes 1179652
  386.6 7.5 %copy-start.20 = (f32[24,64]{1,0:T(8,128)S(1)}, f32[24,64]{1,0:T(8,128)}, u32[]{:S(2)}) copy-start(f32[24,64]{1,0:T(8,128)} %copy-done.19) | copy-start | bytes 18436
  386.6 7.5 %copy-start.22 = (f32[24,64]{1,0:T(8,128)S(1)}, f32[24,64]{1,0:T(8,128)}, u32[]{:S(2)}) copy-start(f32[24,64]{1,0:T(8,128)} %copy-done.21) | copy-start | bytes 18436
  439.1 54.1 %all-to-all-start.5 = ((bf16[8,2,24576]{2,1,0:T(2,128)(2,1)}), bf16[8,2,24576]{2,1,0:T(2,128)(2,1)S(1)}, u32[]{:S(2)}, u32[]{:S(2)}) async-start(bf16[8,2,24576]{2,1,0:T(2,128)(2,1)} %reshape.172), calls=%async_computation.5 | async-start | bytes 1572864 | tf_op jit(solution)/shard_map/all_to_all | solution.py:173
  453.8 10.9 %copy-start.18 = (s32[24,16]{0,1:T(8,128)S(1)}, s32[24,16]{0,1:T(8,128)}, u32[]{:S(2)}) copy-start(s32[24,16]{0,1:T(8,128)} %copy-done.17) | copy-start | bytes 4612
  493.2 20.2 %copy-start.10 = (bf16[8,2,24576]{2,1,0:T(2,128)(2,1)}, bf16[8,2,24576]{2,1,0:T(2,128)(2,1)S(1)}, u32[]{:S(2)}) copy-start(bf16[8,2,24576]{2,1,0:T(2,128)(2,1)S(1)} %all-to-all-done.5) | copy-start | bytes 2359300
  493.2 38.4 %all-to-all-start.7 = ((bf16[8,2,24576]{2,1,0:T(2,128)(2,1)}), bf16[8,2,24576]{2,1,0:T(2,128)(2,1)}, u32[]{:S(2)}, u32[]{:S(2)}) async-start(bf16[8,2,24576]{2,1,0:T(2,128)(2,1)} %reshape.176), calls=%async_computation.7 | async-start | bytes 1572864 | tf_op jit(solution)/shard_map/all_to_all | solution.py:175
  499.2 14.3 %copy-start.12 = (bf16[24,64,128]{2,1,0:T(8,128)(2,1)S(1)}, bf16[24,64,128]{2,1,0:T(8,128)(2,1)}, u32[]{:S(2)}) copy-start(bf16[24,64,128]{2,1,0:T(8,128)(2,1)} %copy.219) | copy-start | bytes 1179652
  503.3 35.0 %copy-start.4 = (bf16[1,1536,256]{2,1,0:T(8,128)(2,1)S(1)}, bf16[1,1536,256]{2,1,0:T(8,128)(2,1)}, u32[]{:S(2)}) copy-start(bf16[1,1536,256]{2,1,0:T(8,128)(2,1)} %copy-done.3) | copy-start | bytes 2359300
  531.6 31.6 %all-to-all-start.6 = ((bf16[8,2,24576]{2,1,0:T(2,128)(2,1)}), bf16[8,2,24576]{2,1,0:T(2,128)(2,1)}, u32[]{:S(2)}, u32[]{:S(2)}) async-start(bf16[8,2,24576]{2,1,0:T(2,128)(2,1)} %reshape.174), calls=%async_computation.6 | async-start | bytes 1572864 | tf_op jit(solution)/shard_map/all_to_all | solution.py:174
  537.5 47.5 %all-reduce.2.cloned.1.call-start = ((), (), s32[]{:S(2)}) async-start(), calls=%async_computation.11 | async-start | bytes 3145728 | tf_op jit(solution)/shard_map/psum | solution.py:177
  538.3 17.7 %copy-start.11 = (bf16[8,2,24576]{2,1,0:T(2,128)(2,1)S(1)}, bf16[8,2,24576]{2,1,0:T(2,128)(2,1)}, u32[]{:S(2)}) copy-start(bf16[8,2,24576]{2,1,0:T(2,128)(2,1)} %copy-done.10) | copy-start | bytes 2359300
  549.1 39.3 %copy-start.1 = (bf16[1,192,3072]{2,1,0:T(8,128)(2,1)S(1)}, bf16[1,192,3072]{2,1,0:T(8,128)(2,1)}, u32[]{:S(2)}) copy-start(bf16[1,192,3072]{2,1,0:T(8,128)(2,1)} %param.11) | copy-start | bytes 3538948
Sparse Core Ops, SparseCore 0:
  10.2 224.5 all-gather.1
  262.2 250.3 reduce-scatter.1
  540.7 44.2 all-reduce.1
where the time goes:
time: 605 us; the launch traced here: 595 us
  matrix products  161 us (27%)
  other arithmetic  130 us (21%)
  local copies, waits for them, and re-layouts  124 us (20%)
  blocking collectives  69.1 us (11%)
  waiting for transfers between devices  63.6 us (11%)
  starting transfers between devices  32 us (5%)
  between operations  15.1 us (2%)
    unnamed x10, other arithmetic  81.8 us
    unnamed x93, local copies, waits for them, and re-layouts  61.8 us
    all_to_all x1, blocking collectives, shards(): lax.all_to_all(grad_tokens[None], 'seq', split_axis=2, concat_axis=1, til...  45.9 us
    dot_general x4, matrix products, add_to_tiles(): jnp.einsum('bst,bsje->tje', onehot.astype(jnp.float32), terms, precision=...  40.2 us
    convert_element_type x2, other arithmetic, head_backward(): grad_scores = (weights * (grad_probs - row_dot)).astype(jnp.bfloat16)  23.5 us
    all_to_all x1, blocking collectives, shards(): lax.all_to_all(attn_heads[None], 'seq', split_axis=1, concat_axis=2, tile...  23.2 us
    dot_general x2, matrix products, head_backward(): jnp.einsum('bie,bsje->bisj', grad_tiles, value_tiles, preferred_element_t...  23.1 us
    all_to_all x1, waiting for transfers between devices, shards(): lax.all_to_all(queries, 'seq', split_axis=2, concat_axis=1, tiled=True)  21.1 us
  transfers between devices with their start and end apart: 9, of which 4 were waited for; matrix products, arithmetic and copies ran while one was open for 69% of the time, Pallas kernels for 0%

commit v1 on v0

v1 whole, which is shorter than its diff:
```python
import jax
import jax.numpy as jnp
from jax import lax
from jax.experimental import pallas as pl
from jax.experimental.pallas import tpu as pltpu
from jax.sharding import PartitionSpec as P

HDIM = 128
TILE = 64
SCALE = HDIM**-0.5
EXP2_SCALE = SCALE * 1.4426950408889634
NEG = -1e30
VMEM_LIMIT = 48 * 1024 * 1024
BF16 = jnp.bfloat16
F32 = jnp.float32


def params(**kw):
    return pltpu.CompilerParams(vmem_limit_bytes=VMEM_LIMIT, **kw)


def dot_nt(a, b):
    return lax.dot_general(a, b, (((1,), (1,)), ((), ())), preferred_element_type=F32)


def dot_nn(a, b):
    return lax.dot_general(a, b, (((1,), (0,)), ((), ())), preferred_element_type=F32)


def pack_heads(arrays, n):
    rows, width = arrays[0].shape
    cols = width // n
    count = len(arrays)

    def body(*refs):
        out, sem = refs[count], refs[count + 1]
        copies = [
            pltpu.make_async_copy(
                refs[a].at[:, pl.ds(j * cols, cols)], out.at[j, a], sem.at[j * count + a]
            )
            for j in range(n)
            for a in range(count)
        ]
        for copy in copies:
            copy.start()
        for copy in copies:
            copy.wait()

    return pl.pallas_call(
        body,
        out_shape=jax.ShapeDtypeStruct((n, count, rows, cols), arrays[0].dtype),
        in_specs=[pl.BlockSpec(memory_space=pl.ANY)] * count,
        out_specs=pl.BlockSpec(memory_space=pl.ANY),
        scratch_shapes=[pltpu.SemaphoreType.DMA((n * count,))],
        name="pack_heads",
    )(*arrays)


def unpack_heads(packed):
    n, count, rows, cols = packed.shape

    def body(*refs):
        src, outs, sem = refs[0], refs[1 : 1 + count], refs[1 + count]
        copies = [
            pltpu.make_async_copy(
                src.at[j, a], outs[a].at[:, pl.ds(j * cols, cols)], sem.at[j * count + a]
            )
            for j in range(n)
            for a in range(count)
        ]
        for copy in copies:
            copy.start()
        for copy in copies:
            copy.wait()

    return pl.pallas_call(
        body,
        out_shape=[jax.ShapeDtypeStruct((rows, n * cols), packed.dtype)] * count,
        in_specs=[pl.BlockSpec(memory_space=pl.ANY)],
        out_specs=[pl.BlockSpec(memory_space=pl.ANY)] * count,
        scratch_shapes=[pltpu.SemaphoreType.DMA((n * count,))],
        name="unpack_heads",
    )(packed)


def masked_scores(q, k, bias):
    s = dot_nt(q, k)
    tiles = bias.shape[0]
    s = s.reshape(tiles, TILE, s.shape[1]) + bias[:, None, :]
    return s.reshape(tiles * TILE, s.shape[2])


def masked_probs(q, k, bias):
    s = masked_scores(q, k, bias)
    e = jnp.exp2((s - jnp.max(s, axis=1, keepdims=True)) * EXP2_SCALE)
    return e * (1.0 / jnp.sum(e, axis=1, keepdims=True))


def attention_forward(packed, bias, half):
    n, _, rows, cols = packed.shape
    heads = cols // HDIM
    tokens = n * rows
    q_rows = 2 * rows
    steps = n // 2
    half_steps = steps // 2
    tiles = q_rows // TILE

    def body(half_ref, q_ref, k_ref, v_ref, bias_ref, o_ref):
        q = q_ref[...].reshape(q_rows, HDIM)
        k = k_ref[...].reshape(tokens, HDIM)
        v = v_ref[...].reshape(tokens, HDIM)
        probs = masked_probs(q, k, bias_ref[0, 0]).astype(BF16)
        o_ref[0] = dot_nn(probs, v).astype(BF16)

    return pl.pallas_call(
        body,
        out_shape=jax.ShapeDtypeStruct((2, tokens // 2, cols), BF16),
        grid_spec=pltpu.PrefetchScalarGridSpec(
            num_scalar_prefetch=1,
            grid=(heads, steps),
            in_specs=[
                pl.BlockSpec((2, 1, rows, HDIM), lambda h, i, r: (i, 0, 0, h)),
                pl.BlockSpec((n, 1, rows, HDIM), lambda h, i, r: (0, 1, 0, h)),
                pl.BlockSpec((n, 1, rows, HDIM), lambda h, i, r: (0, 2, 0, h)),
                pl.BlockSpec((1, 1, tiles, tokens), lambda h, i, r: (h, i, 0, 0)),
            ],
            out_specs=pl.BlockSpec(
                (1, q_rows, HDIM), lambda h, i, r: ((i // half_steps) ^ r[0], i % half_steps, h)
            ),
        ),
        compiler_params=params(),
        name="attention_forward",
    )(half, packed, packed, packed, bias)


def attention_backward(packed, bias, half, grad_own, grad_mirror):
    n, _, rows, cols = packed.shape
    heads = cols // HDIM
    tokens = n * rows
    q_rows = 2 * rows
    steps = n // 2
    half_steps = steps // 2
    tiles = q_rows // TILE

    def body(half_ref, q_ref, k_ref, v_ref, bias_ref, g0_ref, g1_ref, out_ref, dk_ref, dv_ref):
        i = pl.program_id(1)
        q = q_ref[...].reshape(q_rows, HDIM)
        k = k_ref[...].reshape(tokens, HDIM)
        v = v_ref[...].reshape(tokens, HDIM)
        own = (i // half_steps) == half_ref[0]
        grad = jnp.where(own, g0_ref[...], g1_ref[...])
        probs = masked_probs(q, k, bias_ref[0, 0])
        grad_probs = dot_nt(grad, v)
        row_dot = jnp.sum(probs * grad_probs, axis=1, keepdims=True)
        grad_scores = (probs * (grad_probs - row_dot)).astype(BF16)
        grad_q = dot_nn(grad_scores, k) * SCALE
        out_ref[pl.ds(2 * i, 2), 0] = grad_q.astype(BF16).reshape(2, rows, HDIM)
        dk_t = dot_nn(q.T, grad_scores)
        dv_t = dot_nn(grad.T, probs.astype(BF16))

        @pl.when(i == 0)
        def _():
            dk_ref[...] = dk_t
            dv_ref[...] = dv_t

        @pl.when(i > 0)
        def _():
            dk_ref[...] += dk_t
            dv_ref[...] += dv_t

        @pl.when(i == steps - 1)
        def _():
            out_ref[:, 1] = (dk_ref[...] * SCALE).T.astype(BF16).reshape(n, rows, HDIM)
            out_ref[:, 2] = dv_ref[...].T.astype(BF16).reshape(n, rows, HDIM)

    return pl.pallas_call(
        body,
        out_shape=jax.ShapeDtypeStruct((n, 3, rows, cols), BF16),
        grid_spec=pltpu.PrefetchScalarGridSpec(
            num_scalar_prefetch=1,
            grid=(heads, steps),
            in_specs=[
                pl.BlockSpec((2, 1, rows, HDIM), lambda h, i, r: (i, 0, 0, h)),
                pl.BlockSpec((n, 1, rows, HDIM), lambda h, i, r: (0, 1, 0, h)),
                pl.BlockSpec((n, 1, rows, HDIM), lambda h, i, r: (0, 2, 0, h)),
                pl.BlockSpec((1, 1, tiles, tokens), lambda h, i, r: (h, i, 0, 0)),
                pl.BlockSpec((q_rows, HDIM), lambda h, i, r: (i % half_steps, h)),
                pl.BlockSpec((q_rows, HDIM), lambda h, i, r: (i % half_steps, h)),
            ],
            out_specs=pl.BlockSpec((n, 3, rows, HDIM), lambda h, i, r: (0, 0, 0, h)),
            scratch_shapes=[pltpu.VMEM((HDIM, tokens), F32), pltpu.VMEM((HDIM, tokens), F32)],
        ),
        compiler_params=params(),
        name="attention_backward",
    )(half, packed, packed, packed, bias, grad_own, grad_mirror)


def attention_grad(cot_blocks, w_own, w_mirror, rank):
    m = len(cot_blocks)
    rows, width = cot_blocks[0].shape
    cols = w_own.shape[0]

    def body(rank_ref, *refs):
        cots, w0_ref, w1_ref, g0_ref, g1_ref = refs[:m], *refs[m:]
        for j in range(m):
            start = pl.multiple_of((rank_ref[0] ^ j) * rows, rows)
            g0_ref[pl.ds(start, rows), :] = dot_nt(cots[j][...], w0_ref[...]).astype(BF16)
            g1_ref[pl.ds(start, rows), :] = dot_nt(cots[j][...], w1_ref[...]).astype(BF16)

    full = lambda shape: pl.BlockSpec(shape, lambda i, r: (0, 0))
    return pl.pallas_call(
        body,
        out_shape=[jax.ShapeDtypeStruct((m * rows, cols), BF16)] * 2,
        grid_spec=pltpu.PrefetchScalarGridSpec(
            num_scalar_prefetch=1,
            grid=(1,),
            in_specs=[full((rows, width))] * m + [full((cols, width))] * 2,
            out_specs=[full((m * rows, cols))] * 2,
        ),
        compiler_params=params(),
        name="attention_grad",
    )(rank, *cot_blocks, w_own, w_mirror)


def output_partial(attn_own, attn_mirror, w_own, w_mirror, m):
    tokens, cols = attn_own.shape
    width = w_own.shape[1]
    rows = tokens // m
    step = 512

    def body(a0_ref, a1_ref, w0_ref, w1_ref, o_ref):
        total = dot_nn(a0_ref[...], w0_ref[...]) + dot_nn(a1_ref[...], w1_ref[...])
        o_ref[...] = total.astype(BF16).reshape(m, rows, step)

    return pl.pallas_call(
        body,
        out_shape=jax.ShapeDtypeStruct((m, rows, width), BF16),
        grid=(width // step,),
        in_specs=[
            pl.BlockSpec((tokens, cols), lambda i: (0, 0)),
            pl.BlockSpec((tokens, cols), lambda i: (0, 0)),
            pl.BlockSpec((cols, step), lambda i: (0, i)),
            pl.BlockSpec((cols, step), lambda i: (0, i)),
        ],
        out_specs=pl.BlockSpec((m, rows, step), lambda i: (0, 0, i)),
        compiler_params=params(),
        name="output_partial",
    )(attn_own, attn_mirror, w_own, w_mirror)


def weight_grad_partial(attn_own, attn_mirror, cot_blocks, rank, parts):
    m = len(cot_blocks)
    rows, width = cot_blocks[0].shape
    tokens, cols = attn_own.shape
    step = 512
    piece = cols // parts

    def body(rank_ref, *refs):
        a0_ref, a1_ref, cots, o_ref, at_ref = refs[0], refs[1], refs[2 : 2 + m], *refs[2 + m :]

        @pl.when(pl.program_id(0) == 0)
        def _():
            for j in range(m):
                start = pl.multiple_of((rank_ref[0] ^ j) * rows, rows)
                at_ref[j, :cols] = a0_ref[pl.ds(start, rows), :].T
                at_ref[j, cols:] = a1_ref[pl.ds(start, rows), :].T

        total = dot_nn(at_ref[0], cots[0][...])
        for j in range(1, m):
            total += dot_nn(at_ref[j], cots[j][...])
        total = total.astype(BF16).reshape(2, parts, piece, step)
        o_ref[:, 0] = total[0]
        o_ref[:, 1] = total[1]

    return pl.pallas_call(
        body,
        out_shape=jax.ShapeDtypeStruct((parts, 2, piece, width), BF16),
        grid_spec=pltpu.PrefetchScalarGridSpec(
            num_scalar_prefetch=1,
            grid=(width // step,),
            in_specs=[pl.BlockSpec((tokens, cols), lambda i, r: (0, 0))] * 2
            + [pl.BlockSpec((rows, step), lambda i, r: (0, i))] * m,
            out_specs=pl.BlockSpec((parts, 2, piece, step), lambda i, r: (0, 0, 0, i)),
            scratch_shapes=[pltpu.VMEM((m, 2 * cols, rows), BF16)],
        ),
        compiler_params=params(),
        name="weight_grad_partial",
    )(rank, attn_own, attn_mirror, *cot_blocks)


def mask_bias(my_tiles, my_counts, tokens, q_rows):
    heads, blocks, slots = my_tiles.shape
    key_tile = lax.broadcasted_iota(jnp.int32, (1, 1, tokens, 1), 2) // TILE
    slot = lax.broadcasted_iota(jnp.int32, (1, 1, 1, slots), 3)
    seen = (my_tiles[:, :, None, :] == key_tile) & (slot < my_counts[:, :, None, None])
    bias = jnp.where(jnp.any(seen, axis=3), F32(0.0), F32(NEG))
    tiles = q_rows // TILE
    return bias.reshape(heads, blocks // tiles, tiles, tokens)


def shards(queries, key_rows, value_rows, out_weight, cotangent, tile_lists, live_counts):
    n = lax.axis_size("seq")
    dp = lax.axis_size("dp")
    m = n // 2
    s = lax.axis_index("seq")
    d = lax.axis_index("dp")
    half = (s // m).astype(jnp.int32).reshape(1)
    rank = (s % m).astype(jnp.int32).reshape(1)
    rows = queries.shape[1]
    cols, width = out_weight.shape
    heads = cols // HDIM
    xor = lambda x, bit: lax.ppermute(x, "seq", [(i, i ^ bit) for i in range(n)])

    my_tiles = lax.dynamic_slice_in_dim(tile_lists, s * heads, heads, 0)
    my_counts = lax.dynamic_slice_in_dim(live_counts, s * heads, heads, 0)
    bias = mask_bias(my_tiles, my_counts, n * rows, 2 * rows)

    packed = pack_heads([queries[0], key_rows[0], value_rows[0]], n)
    packed = lax.all_to_all(packed, "seq", split_axis=0, concat_axis=0, tiled=True)

    piece = cols // dp
    w_piece = lax.dynamic_slice_in_dim(out_weight, d * piece, piece, 0)
    w_mirror = lax.all_gather(xor(w_piece, m), "dp", axis=0, tiled=True)

    cot_at = {0: cotangent[0]}
    bit = m // 2
    while bit:
        cot_at.update({j | bit: xor(block, bit) for j, block in list(cot_at.items())})
        bit //= 2
    cot_blocks = [cot_at[j] for j in range(m)]

    grad_own, grad_send = attention_grad(cot_blocks, out_weight, w_mirror, rank)
    grad_mirror = xor(grad_send, m)

    attn = attention_forward(packed, bias, half)
    attn_own = attn[0]
    attn_mirror = xor(attn[1], m)

    grads = attention_backward(packed, bias, half, grad_own, grad_mirror)
    grads = lax.all_to_all(grads, "seq", split_axis=0, concat_axis=0, tiled=True)
    back_q, back_k, back_v = unpack_heads(grads)

    partial = output_partial(attn_own, attn_mirror, out_weight, w_mirror, m)
    groups = [list(range(m)), list(range(m, n))]
    partial = lax.all_to_all(
        partial, "seq", split_axis=0, concat_axis=0, tiled=True, axis_index_groups=groups
    )
    block_out = jnp.sum(partial.astype(F32), axis=0).astype(BF16)

    gw = weight_grad_partial(attn_own, attn_mirror, cot_blocks, rank, dp)
    gw = lax.all_to_all(gw, "dp", split_axis=0, concat_axis=0, tiled=True)
    gw = jnp.sum(gw.astype(F32), axis=0)
    gw = (gw[0] + xor(gw[1].astype(BF16), m).astype(F32)).astype(BF16)
    grad_weight = lax.all_gather(gw, "dp", axis=0, tiled=True).astype(F32)
    return (block_out[None], back_q[None], back_k[None], back_v[None], grad_weight)


def solution(mesh):
    token_spec = P("dp", "seq", None)
    in_specs = (
        token_spec,
        token_spec,
        token_spec,
        P("seq", None),
        token_spec,
        P(),
        P(),
    )
    out_specs = (token_spec,) * 4 + (P("seq", None),)
    return jax.shard_map(shards, mesh=mesh, in_specs=in_specs, out_specs=out_specs, check_vma=False)
```

time: 605 us -> 478 us (0.79); the launches traced: 595 us -> 476 us
  Pallas kernels: 0 us -> 203 us
  matrix products: 161 us -> 0 us
  waiting for transfers between devices: 63.6 us -> 207 us
  other arithmetic: 130 us -> 12.8 us
  local copies, waits for them, and re-layouts: 124 us -> 9.82 us
  blocking collectives: 69.1 us -> 0 us
    pallas_call x0 -> x7, Pallas kernels: none -> 203 us  [the longest x1 72.8 us: unpack_heads(): pl.pallas_call(body, out_shape=[jax.ShapeDtypeStruct((rows, n * cols), pa...]
    dot_general x23 -> x0, matrix products: 161 us -> none  [the longest x4 40.2 us: add_to_tiles(): jnp.einsum('bst,bsje->tje', onehot.astype(jnp.float32), terms, precision=...]
    ppermute x0 -> x7, waiting for transfers between devices: none -> 160 us  [shards(): lax.ppermute(x, 'seq', [(i, i ^ bit) for i in range(n)])]
    unnamed x10 -> x0, other arithmetic: 81.8 us -> none
    all_to_all x2 -> x0, blocking collectives: 69.1 us -> none  [the longest x1 45.9 us: shards(): lax.all_to_all(grad_tokens[None], 'seq', split_axis=2, concat_axis=1, til...]
    unnamed x93 -> x14, local copies, waits for them, and re-layouts: 61.8 us -> 6.13 us
    broadcast_in_dim x5 -> x0, local copies, waits for them, and re-layouts: 40.2 us -> none  [the longest x1 9.06 us: shards(): grad_v[None]]
    convert_element_type x3 -> x2, other arithmetic: 26.9 us -> 4.25 us  [the longest x1 3.44 us: shards(): grad_weight = lax.all_gather(gw, 'dp', axis=0, tiled=True).astype(F32)]
  transfers between devices with their start and end apart: 9 -> 13, of which waited for: 4 -> 6; matrix products, arithmetic and copies ran while one was open for 69% -> 3% of each run, Pallas kernels for 0% -> 27%
where the time goes in v1:
time: 478 us; the launch traced here: 476 us
  waiting for transfers between devices  207 us (43%)
  Pallas kernels  203 us (42%)
  starting transfers between devices  29.6 us (6%)
  between operations  14.3 us (3%)
  other arithmetic  12.8 us (3%)
  local copies, waits for them, and re-layouts  9.82 us (2%)
    ppermute x7, waiting for transfers between devices, shards(): lax.ppermute(x, 'seq', [(i, i ^ bit) for i in range(n)])  160 us
    pallas_call x1, Pallas kernels, unpack_heads(): pl.pallas_call(body, out_shape=[jax.ShapeDtypeStruct((rows, n * cols), pa...  72.8 us
    pallas_call x1, Pallas kernels, pack_heads(): pl.pallas_call(body, out_shape=jax.ShapeDtypeStruct((n, count, rows, cols...  72.8 us
    all_to_all x1, waiting for transfers between devices, shards(): lax.all_to_all(grads, 'seq', split_axis=0, concat_axis=0, tiled=True)  46.7 us
    pallas_call x1, Pallas kernels, attention_backward(): pl.pallas_call(body, out_shape=jax.ShapeDtypeStruct((n, 3, rows, cols), B...  20.3 us
    pallas_call x1, Pallas kernels, attention_forward(): pl.pallas_call(body, out_shape=jax.ShapeDtypeStruct((2, tokens // 2, cols...  15.7 us
  transfers between devices with their start and end apart: 13, of which 6 were waited for; matrix products, arithmetic and copies ran while one was open for 3% of the time, Pallas kernels for 27%

profile of v1, /device:TPU:0, one launch (start us, length us, event | category | flops | bytes accessed | tf_op | source)
XLA Modules:
  0.0 476.2 jit_solution(3350924939560113956)
XLA Ops:
  7.2 0.0 copy-start
  7.2 72.8 %pack_heads.1 = bf16[8,3,192,256]{3,2,1,0:T(8,128)(2,1)} custom-call(bf16[192,2048]{1,0:T(8,128)(2,1)} %bitcast.29, bf16[192,2048]{1,0:T(8,128)(2,1)} %bitcast.30, bf16[192,2048]{1,0:T(8,128)(2,1)} %bitcast.31), custom_call_target="tpu_custom_call" | custom-call | tf_op jit(solution)/shard_map/pack_heads/pallas_call | solution.py:49
  80.0 7.3 %all-to-all-start = ((bf16[8,3,192,256]{3,2,1,0:T(8,128)(2,1)}), bf16[8,3,192,256]{3,2,1,0:T(8,128)(2,1)S(1)}, u32[]{:S(2)}, u32[]{:S(2)}) async-start(bf16[8,3,192,256]{3,2,1,0:T(8,128)(2,1)} %pack_heads.1), calls=%async_computation | async-start | bytes 4718592 | tf_op jit(solution)/shard_map/all_to_all | solution.py:319
  87.3 0.0 all-gather.3.cloned.1.call-start
  87.3 2.0 collective-permute-start.3
  89.3 1.5 collective-permute-start.2
  90.8 1.8 constant_dynamic-slice_fusion
  92.5 2.4 collective-permute-start.1
  94.9 0.1 copy.16
  95.0 0.7 constant_dynamic-slice_fusion.1
  95.7 0.1 iota_compare_fusion
  95.7 65.7 %collective-permute-done.3.refs_2_.refs_4_ = bf16[192,3072]{1,0:T(8,128)(2,1)} collective-permute-done((bf16[192,3072]{1,0:T(8,128)(2,1)}, bf16[192,3072]{1,0:T(8,128)(2,1)}, u32[]{:S(2)}, u32[]{:S(2)}) %collective-permute-start.3) | collective-permute-done | bytes 1179680 | tf_op jit(solution)/shard_map/ppermute | solution.py:312
  161.4 1.5 collective-permute-start.4
  162.9 1.4 and_reduce_fusion
  164.3 0.2 copy.17
  164.5 0.1 copy.18.bias_ref
  164.6 0.7 copy-done.6
  165.4 0.0 all-gather.3.cloned.1.call-update
  165.4 15.7 %attention_forward.1 = bf16[2,768,256]{2,1,0:T(8,128)(2,1)S(1)} custom-call(s32[1]{0:T(128)} %bitcast.half_ref, bf16[8,3,192,256]{3,2,1,0:T(8,128)(2,1)S(1)} %all-to-all-done.q_ref.k_ref.v_ref, bf16[8,3,192,256]{3,2,1,0:T(8,128)(2,1)S(1)} %all-to-all-done.q_ref.k_ref.v_ref, bf16[8,3,192,256]{3,2,1,0:T(8,128)(2,1)S(1)} %all-to-all-done.q_ref.k_ref.v_ref, ...), custom_call_target="tpu_custom_call" | custom-call | tf_op jit(solution)/shard_map/attention_forward/pallas_call | solution.py:115
  181.1 0.8 slice_bitcast_fusion.1
  181.9 0.4 collective-permute-start
  182.3 6.0 %collective-permute-done.4.refs_3_.refs_5_ = bf16[192,3072]{1,0:T(8,128)(2,1)} collective-permute-done((bf16[192,3072]{1,0:T(8,128)(2,1)}, bf16[192,3072]{1,0:T(8,128)(2,1)}, u32[]{:S(2)}, u32[]{:S(2)}) %collective-permute-start.4) | collective-permute-done | bytes 1179680 | tf_op jit(solution)/shard_map/ppermute | solution.py:312
  188.4 12.4 %collective-permute-done.a1_ref.refs_1_ = bf16[768,256]{1,0:T(8,128)(2,1)} collective-permute-done((bf16[768,256]{1,0:T(8,128)(2,1)}, bf16[768,256]{1,0:T(8,128)(2,1)}, u32[]{:S(2)}, u32[]{:S(2)}) %collective-permute-start) | collective-permute-done | bytes 393248 | tf_op jit(solution)/shard_map/ppermute | solution.py:312
  200.7 1.3 copy-done.4
  202.0 7.9 %weight_grad_partial.1 = bf16[4,2,64,3072]{3,2,1,0:T(8,128)(2,1)} custom-call(s32[1]{0:T(128)} %bitcast.8.rank_ref, bf16[768,256]{1,0:T(8,128)(2,1)S(1)} %get-tuple-element.16.a0_ref.refs_0_, bf16[768,256]{1,0:T(8,128)(2,1)} %collective-permute-done.a1_ref.refs_1_, bf16[192,3072]{1,0:T(8,128)(2,1)S(1)} %bitcast.25, ...), custom_call_target="tpu_custom_call" | custom-call | tf_op jit(solution)/shard_map/weight_grad_partial/pallas_call | solution.py:275
  209.9 4.6 all-to-all-start.3
  214.6 0.0 all-gather.3.cloned.1.call-done.w1_ref.refs_5_
  214.6 1.3 copy-done.5
  215.9 7.2 %attention_grad.1 = (bf16[768,256]{1,0:T(8,128)(2,1)S(1)}, bf16[768,256]{1,0:T(8,128)(2,1)S(1)}) custom-call(s32[1]{0:T(128)} %bitcast.8.rank_ref, bf16[192,3072]{1,0:T(8,128)(2,1)S(1)} %bitcast.26, bf16[192,3072]{1,0:T(8,128)(2,1)} %collective-permute-done.2.refs_1_.refs_3_, bf16[192,3072]{1,0:T(8,128)(2,1)} %collective-permute-done.3.refs_2_.refs_4_, ...), custom_call_target="tpu_custom_call" | custom-call | tf_op jit(solution)/shard_map/attention_grad/pallas_call | solution.py:211
  223.1 0.1 collective-permute-start.5
  223.2 19.9 %collective-permute-done.5.g1_ref = bf16[768,256]{1,0:T(8,128)(2,1)S(1)} collective-permute-done((bf16[768,256]{1,0:T(8,128)(2,1)S(1)}, bf16[768,256]{1,0:T(8,128)(2,1)S(1)}, u32[]{:S(2)}, u32[]{:S(2)}) %collective-permute-start.5) | collective-permute-done | bytes 393248 | tf_op jit(solution)/shard_map/ppermute | solution.py:312
  243.1 20.3 %attention_backward.1 = bf16[8,3,192,256]{3,2,1,0:T(8,128)(2,1)S(1)} custom-call(s32[1]{0:T(128)} %bitcast.half_ref, bf16[8,3,192,256]{3,2,1,0:T(8,128)(2,1)S(1)} %all-to-all-done.q_ref.k_ref.v_ref, bf16[8,3,192,256]{3,2,1,0:T(8,128)(2,1)S(1)} %all-to-all-done.q_ref.k_ref.v_ref, bf16[8,3,192,256]{3,2,1,0:T(8,128)(2,1)S(1)} %all-to-all-done.q_ref.k_ref.v_ref, ...), custom_call_target="tpu_custom_call" | custom-call | tf_op jit(solution)/shard_map/attention_backward/pallas_call | solution.py:176
  263.4 1.4 copy-done.1
  264.9 4.5 all-to-all-start.2
  269.4 1.4 copy-done.2
  270.8 6.3 %output_partial.1 = bf16[4,192,3072]{2,1,0:T(8,128)(2,1)} custom-call(bf16[768,256]{1,0:T(8,128)(2,1)S(1)} %get-tuple-element.16.a0_ref.refs_0_, bf16[768,256]{1,0:T(8,128)(2,1)} %collective-permute-done.a1_ref.refs_1_, bf16[256,3072]{1,0:T(8,128)(2,1)S(1)} %copy-done.2, bf16[256,3072]{1,0:T(8,128)(2,1)S(1)} %copy-done.3), custom_call_target="tpu_custom_call" | custom-call | tf_op jit(solution)/shard_map/output_partial/pallas_call | solution.py:235
  277.1 46.7 %all-to-all-done.2.refs_0_ = bf16[8,3,192,256]{3,2,1,0:T(8,128)(2,1)} async-done(((bf16[8,3,192,256]{3,2,1,0:T(8,128)(2,1)}), bf16[8,3,192,256]{3,2,1,0:T(8,128)(2,1)}, u32[]{:S(2)}, u32[]{:S(2)}) %all-to-all-start.2) | async-done | bytes 2359328 | tf_op jit(solution)/shard_map/all_to_all | solution.py:340
  323.8 5.1 %all-to-all-start.1 = ((bf16[4,192,3072]{2,1,0:T(8,128)(2,1)}), bf16[4,192,3072]{2,1,0:T(8,128)(2,1)}, u32[]{:S(2)}, u32[]{:S(2)}) async-start(bf16[4,192,3072]{2,1,0:T(8,128)(2,1)} %output_partial.1), calls=%async_computation.1 | async-start | bytes 9437184 | tf_op jit(solution)/shard_map/all_to_all | solution.py:345
  328.9 0.0 all-gather.5.cloned.1.call-start
  329.0 2.6 convert_reduce_fusion
  331.6 0.1 collective-permute-start.6
  331.7 56.1 %collective-permute-done.6 = bf16[64,3072]{1,0:T(8,128)(2,1)S(1)} collective-permute-done((bf16[64,3072]{1,0:T(8,128)(2,1)S(1)}, bf16[64,3072]{1,0:T(8,128)(2,1)S(1)}, u32[]{:S(2)}, u32[]{:S(2)}) %collective-permute-start.6) | collective-permute-done | bytes 393248 | tf_op jit(solution)/shard_map/ppermute | solution.py:312
  387.8 0.8 fusion.1
  388.6 0.0 all-gather.5.cloned.1.call-update
  388.6 72.8 %unpack_heads.1 = (bf16[192,2048]{1,0:T(8,128)(2,1)}, bf16[192,2048]{1,0:T(8,128)(2,1)}, bf16[192,2048]{1,0:T(8,128)(2,1)}) custom-call(bf16[8,3,192,256]{3,2,1,0:T(8,128)(2,1)} %all-to-all-done.2.refs_0_), custom_call_target="tpu_custom_call" | custom-call | tf_op jit(solution)/shard_map/unpack_heads/pallas_call | solution.py:76
  461.4 0.0 all-gather.5.cloned.1.call-done
  461.4 3.4 convert_element_type.22
  464.9 4.5 reduce_sum.21
  (17 shorter events, 0.1 us)
Async XLA Ops:
  7.2 87.7 %copy-start = (s32[16,24,16]{1,2,0:T(8,128)S(1)}, s32[16,24,16]{1,2,0:T(8,128)}, u32[]{:S(2)}) copy-start(s32[16,24,16]{1,2,0:T(8,128)} %param.12) | copy-start | bytes 73732
  80.0 85.4 %all-to-all-start = ((bf16[8,3,192,256]{3,2,1,0:T(8,128)(2,1)}), bf16[8,3,192,256]{3,2,1,0:T(8,128)(2,1)S(1)}, u32[]{:S(2)}, u32[]{:S(2)}) async-start(bf16[8,3,192,256]{3,2,1,0:T(8,128)(2,1)} %pack_heads.1), calls=%async_computation | async-start | bytes 4718592 | tf_op jit(solution)/shard_map/all_to_all | solution.py:319
  87.3 127.3 %all-gather.3.cloned.1.call-start = ((), (), s32[]{:S(2)}) async-start(), calls=%async_computation.4 | async-start | bytes 1966080 | tf_op jit(solution)/shard_map/all_gather | solution.py:323
  87.3 74.1 %collective-permute-start.3 = (bf16[192,3072]{1,0:T(8,128)(2,1)}, bf16[192,3072]{1,0:T(8,128)(2,1)}, u32[]{:S(2)}, u32[]{:S(2)}) collective-permute-start(bf16[192,3072]{1,0:T(8,128)(2,1)} %bitcast.23), channel_id=1, source_target_pairs={{0,2},{1,3},{2,0},{3,1},{4,6},{5,7},{6,4},{7,5},{8,10},{9,11},{10,... | collective-permute-start | bytes 3538952 | tf_op jit(solution)/shard_map/ppermute | solution.py:312
  89.3 93.1 %collective-permute-start.2 = (bf16[192,3072]{1,0:T(8,128)(2,1)}, bf16[192,3072]{1,0:T(8,128)(2,1)}, u32[]{:S(2)}, u32[]{:S(2)}) collective-permute-start(bf16[192,3072]{1,0:T(8,128)(2,1)} %bitcast.24), channel_id=1, source_target_pairs={{0,1},{1,0},{2,3},{3,2},{4,5},{5,4},{6,7},{7,6},{8,9},{9,8},{10,11... | collective-permute-start | bytes 3538952 | tf_op jit(solution)/shard_map/ppermute | solution.py:312
  92.5 72.1 %collective-permute-start.1 = (bf16[64,3072]{1,0:T(8,128)(2,1)}, bf16[64,3072]{1,0:T(8,128)(2,1)S(1)}, u32[]{:S(2)}, u32[]{:S(2)}) collective-permute-start(bf16[64,3072]{1,0:T(8,128)(2,1)} %constant_dynamic-slice_fusion), channel_id=1, source_target_pairs={{0,4},{1,5},{2,6},{3,7},{4,0},{5,1},{6,2},{7,3},{8,12},{9,13},{10,... | collective-permute-start | bytes 1179656 | tf_op jit(solution)/shard_map/ppermute | solution.py:312
  161.4 27.0 %collective-permute-start.4 = (bf16[192,3072]{1,0:T(8,128)(2,1)}, bf16[192,3072]{1,0:T(8,128)(2,1)}, u32[]{:S(2)}, u32[]{:S(2)}) collective-permute-start(bf16[192,3072]{1,0:T(8,128)(2,1)} %collective-permute-done.3.refs_2_.refs_4_), channel_id=1, source_target_pairs={{0,1},{1,0},{2,3},{3,2},{4,5},{5,4},{6,7},{7,6},{8,9},{9,8},{10,11... | collective-permute-start | bytes 3538952 | tf_op jit(solution)/shard_map/ppermute | solution.py:312
  164.6 0.7 copy-start.6
  181.9 18.8 %collective-permute-start = (bf16[768,256]{1,0:T(8,128)(2,1)}, bf16[768,256]{1,0:T(8,128)(2,1)}, u32[]{:S(2)}, u32[]{:S(2)}) collective-permute-start(bf16[768,256]{1,0:T(8,128)(2,1)} %get-tuple-element.15), channel_id=1, source_target_pairs={{0,4},{1,5},{2,6},{3,7},{4,0},{5,1},{6,2},{7,3},{8,12},{9,13},{10,... | collective-permute-start | bytes 1179656 | tf_op jit(solution)/shard_map/ppermute | solution.py:312
  200.7 1.3 copy-start.4
  209.9 54.9 %all-to-all-start.3 = ((bf16[4,2,64,3072]{3,2,1,0:T(8,128)(2,1)}), bf16[4,2,64,3072]{3,2,1,0:T(8,128)(2,1)}, u32[]{:S(2)}, u32[]{:S(2)}) async-start(bf16[4,2,64,3072]{3,2,1,0:T(8,128)(2,1)} %weight_grad_partial.1), calls=%async_computation.3 | async-start | bytes 6291456 | tf_op jit(solution)/shard_map/all_to_all | solution.py:351
  214.6 1.3 copy-start.5
  223.1 20.0 %collective-permute-start.5 = (bf16[768,256]{1,0:T(8,128)(2,1)S(1)}, bf16[768,256]{1,0:T(8,128)(2,1)S(1)}, u32[]{:S(2)}, u32[]{:S(2)}) collective-permute-start(bf16[768,256]{1,0:T(8,128)(2,1)S(1)} %get-tuple-element.11), channel_id=1, source_target_pairs={{0,4},{1,5},{2,6},{3,7},{4,0},{5,1},{6,2},{7,3},{8,12},{9,13},{10,... | collective-permute-start | bytes 1179656 | tf_op jit(solution)/shard_map/ppermute | solution.py:312
  263.4 1.4 copy-start.1
  264.8 4.6 copy-start.3
  264.9 58.9 %all-to-all-start.2 = ((bf16[8,3,192,256]{3,2,1,0:T(8,128)(2,1)}), bf16[8,3,192,256]{3,2,1,0:T(8,128)(2,1)}, u32[]{:S(2)}, u32[]{:S(2)}) async-start(bf16[8,3,192,256]{3,2,1,0:T(8,128)(2,1)} %copy-done.1), calls=%async_computation.2 | async-start | bytes 4718592 | tf_op jit(solution)/shard_map/all_to_all | solution.py:340
  269.4 1.4 copy-start.2
  323.8 141.1 %all-to-all-start.1 = ((bf16[4,192,3072]{2,1,0:T(8,128)(2,1)}), bf16[4,192,3072]{2,1,0:T(8,128)(2,1)}, u32[]{:S(2)}, u32[]{:S(2)}) async-start(bf16[4,192,3072]{2,1,0:T(8,128)(2,1)} %output_partial.1), calls=%async_computation.1 | async-start | bytes 9437184 | tf_op jit(solution)/shard_map/all_to_all | solution.py:345
  328.9 132.5 %all-gather.5.cloned.1.call-start = ((), (), s32[]{:S(2)}) async-start(), calls=%async_computation.5 | async-start | bytes 1966080 | tf_op jit(solution)/shard_map/all_gather | solution.py:354
  331.6 56.1 %collective-permute-start.6 = (bf16[64,3072]{1,0:T(8,128)(2,1)S(1)}, bf16[64,3072]{1,0:T(8,128)(2,1)S(1)}, u32[]{:S(2)}, u32[]{:S(2)}) collective-permute-start(bf16[64,3072]{1,0:T(8,128)(2,1)S(1)} %fusion.2), channel_id=1, source_target_pairs={{0,4},{1,5},{2,6},{3,7},{4,0},{5,1},{6,2},{7,3},{8,12},{9,13},{10,... | collective-permute-start | bytes 1179656 | tf_op jit(solution)/shard_map/ppermute | solution.py:312
Sparse Core Ops, SparseCore 0:
  165.5 18.7 all-gather.2
  388.7 20.9 all-gather.4

commit v2 on v1

v2 whole, which is shorter than its diff:
```python
import jax
import jax.numpy as jnp
from jax import lax
from jax.experimental import pallas as pl
from jax.experimental.pallas import tpu as pltpu
from jax.sharding import PartitionSpec as P

HDIM = 128
TILE = 64
SCALE = HDIM**-0.5
EXP2_SCALE = SCALE * 1.4426950408889634
NEG = -1e30
VMEM_LIMIT = 48 * 1024 * 1024
BF16 = jnp.bfloat16
F32 = jnp.float32


def params(**kw):
    return pltpu.CompilerParams(vmem_limit_bytes=VMEM_LIMIT, **kw)


def cost(flops, nbytes, exps=0):
    return pl.CostEstimate(flops=flops, bytes_accessed=nbytes, transcendentals=exps)


def dot_nt(a, b):
    return lax.dot_general(a, b, (((1,), (1,)), ((), ())), preferred_element_type=F32)


def dot_nn(a, b):
    return lax.dot_general(a, b, (((1,), (0,)), ((), ())), preferred_element_type=F32)


def pack_heads(arrays, n):
    rows, width = arrays[0].shape
    cols = width // n
    count = len(arrays)

    def body(*refs):
        for a in range(count):
            refs[count][0, a] = refs[a][...]

    return pl.pallas_call(
        body,
        out_shape=jax.ShapeDtypeStruct((n, count, rows, cols), arrays[0].dtype),
        grid=(n,),
        in_specs=[pl.BlockSpec((rows, cols), lambda j: (0, j))] * count,
        out_specs=pl.BlockSpec((1, count, rows, cols), lambda j: (j, 0, 0, 0)),
        compiler_params=params(),
        cost_estimate=cost(0, 4 * n * count * rows * cols),
        name="pack_heads",
    )(*arrays)


def unpack_heads(packed):
    heads = len(packed)
    n, count, rows, width = packed[0].shape
    cols = heads * width

    def body(*refs):
        for a in range(count):
            for h in range(heads):
                refs[heads + a][:, h * width : (h + 1) * width] = refs[h][0, a]

    return pl.pallas_call(
        body,
        out_shape=[jax.ShapeDtypeStruct((rows, n * cols), BF16)] * count,
        grid=(n,),
        in_specs=[pl.BlockSpec((1, count, rows, width), lambda j: (j, 0, 0, 0))] * heads,
        out_specs=[pl.BlockSpec((rows, cols), lambda j: (0, j))] * count,
        compiler_params=params(),
        cost_estimate=cost(0, 4 * n * count * rows * cols),
        name="unpack_heads",
    )(*packed)


def masked_scores(q, k, bias):
    s = dot_nt(q, k)
    tiles = bias.shape[0]
    s = s.reshape(tiles, TILE, s.shape[1]) + bias[:, None, :]
    return s.reshape(tiles * TILE, s.shape[2])


def masked_probs(q, k, bias):
    s = masked_scores(q, k, bias)
    e = jnp.exp2((s - jnp.max(s, axis=1, keepdims=True)) * EXP2_SCALE)
    return e * (1.0 / jnp.sum(e, axis=1, keepdims=True))


def attention_forward(packed, bias, half):
    n, _, rows, cols = packed.shape
    heads = cols // HDIM
    tokens = n * rows
    q_rows = 2 * rows
    steps = n // 2
    half_steps = steps // 2
    tiles = q_rows // TILE

    def body(half_ref, q_ref, k_ref, v_ref, bias_ref, own_ref, send_ref):
        q = q_ref[...].reshape(q_rows, HDIM)
        k = k_ref[...].reshape(tokens, HDIM)
        v = v_ref[...].reshape(tokens, HDIM)
        probs = masked_probs(q, k, bias_ref[0, 0]).astype(BF16)
        attn = dot_nn(probs, v).astype(BF16)
        own = (pl.program_id(1) // half_steps) == half_ref[0]

        @pl.when(own)
        def _():
            own_ref[...] = attn

        @pl.when(jnp.logical_not(own))
        def _():
            send_ref[...] = attn

    return pl.pallas_call(
        body,
        out_shape=[jax.ShapeDtypeStruct((tokens // 2, cols), BF16)] * 2,
        grid_spec=pltpu.PrefetchScalarGridSpec(
            num_scalar_prefetch=1,
            grid=(heads, steps),
            in_specs=[
                pl.BlockSpec((2, 1, rows, HDIM), lambda h, i, r: (i, 0, 0, h)),
                pl.BlockSpec((n, 1, rows, HDIM), lambda h, i, r: (0, 1, 0, h)),
                pl.BlockSpec((n, 1, rows, HDIM), lambda h, i, r: (0, 2, 0, h)),
                pl.BlockSpec((1, 1, tiles, tokens), lambda h, i, r: (h, i, 0, 0)),
            ],
            out_specs=[
                pl.BlockSpec(
                    (q_rows, HDIM),
                    lambda h, i, r: (jnp.clip(i - r[0] * half_steps, 0, half_steps - 1), h),
                ),
                pl.BlockSpec(
                    (q_rows, HDIM),
                    lambda h, i, r: (jnp.clip(i - (1 - r[0]) * half_steps, 0, half_steps - 1), h),
                ),
            ],
        ),
        compiler_params=params(),
        cost_estimate=cost(4 * tokens**2 * cols, 8 * tokens * cols, heads * tokens**2),
        name="attention_forward",
    )(half, packed, packed, packed, bias)


def attention_backward(packed, bias, half, grad_own, grad_mirror, head):
    n, _, rows, cols = packed.shape
    tokens = n * rows
    q_rows = 2 * rows
    steps = n // 2
    half_steps = steps // 2
    tiles = q_rows // TILE

    def body(half_ref, q_ref, k_ref, v_ref, bias_ref, g0_ref, g1_ref, out_ref, dk_ref, dv_ref):
        i = pl.program_id(0)
        q = q_ref[...].reshape(q_rows, HDIM)
        k = k_ref[...].reshape(tokens, HDIM)
        v = v_ref[...].reshape(tokens, HDIM)
        own = (i // half_steps) == half_ref[0]
        grad = jnp.where(own, g0_ref[...], g1_ref[...])
        probs = masked_probs(q, k, bias_ref[0, 0])
        grad_probs = dot_nt(grad, v)
        row_dot = jnp.sum(probs * grad_probs, axis=1, keepdims=True)
        grad_scores = (probs * (grad_probs - row_dot)).astype(BF16)
        grad_q = dot_nn(grad_scores, k) * SCALE
        out_ref[pl.ds(2 * i, 2), 0] = grad_q.astype(BF16).reshape(2, rows, HDIM)
        dk_t = dot_nn(q.T, grad_scores)
        dv_t = dot_nn(grad.T, probs.astype(BF16))

        @pl.when(i == 0)
        def _():
            dk_ref[...] = dk_t
            dv_ref[...] = dv_t

        @pl.when(i > 0)
        def _():
            dk_ref[...] += dk_t
            dv_ref[...] += dv_t

        @pl.when(i == steps - 1)
        def _():
            out_ref[:, 1] = (dk_ref[...] * SCALE).T.astype(BF16).reshape(n, rows, HDIM)
            out_ref[:, 2] = dv_ref[...].T.astype(BF16).reshape(n, rows, HDIM)

    return pl.pallas_call(
        body,
        out_shape=jax.ShapeDtypeStruct((n, 3, rows, HDIM), BF16),
        grid_spec=pltpu.PrefetchScalarGridSpec(
            num_scalar_prefetch=1,
            grid=(steps,),
            in_specs=[
                pl.BlockSpec((2, 1, rows, HDIM), lambda i, r: (i, 0, 0, head)),
                pl.BlockSpec((n, 1, rows, HDIM), lambda i, r: (0, 1, 0, head)),
                pl.BlockSpec((n, 1, rows, HDIM), lambda i, r: (0, 2, 0, head)),
                pl.BlockSpec((1, 1, tiles, tokens), lambda i, r: (head, i, 0, 0)),
                pl.BlockSpec((q_rows, HDIM), lambda i, r: (i % half_steps, head)),
                pl.BlockSpec((q_rows, HDIM), lambda i, r: (i % half_steps, head)),
            ],
            out_specs=pl.BlockSpec((n, 3, rows, HDIM), lambda i, r: (0, 0, 0, 0)),
            scratch_shapes=[pltpu.VMEM((HDIM, tokens), F32), pltpu.VMEM((HDIM, tokens), F32)],
        ),
        compiler_params=params(),
        cost_estimate=cost(10 * tokens**2 * HDIM, 14 * tokens * HDIM, tokens**2),
        name="attention_backward",
    )(half, packed, packed, packed, bias, grad_own, grad_mirror)


def attention_grad(cot_blocks, w_own, w_mirror, rank):
    m = len(cot_blocks)
    rows, width = cot_blocks[0].shape
    cols = w_own.shape[0]

    def body(rank_ref, *refs):
        cots, w0_ref, w1_ref, g0_ref, g1_ref = refs[:m], *refs[m:]
        for w_ref, g_ref in ((w1_ref, g1_ref), (w0_ref, g0_ref)):
            for j in range(m):
                start = pl.multiple_of((rank_ref[0] ^ j) * rows, rows)
                g_ref[pl.ds(start, rows), :] = dot_nt(cots[j][...], w_ref[...]).astype(BF16)

    full = lambda shape: pl.BlockSpec(shape, lambda i, r: (0, 0))
    return pl.pallas_call(
        body,
        out_shape=[jax.ShapeDtypeStruct((m * rows, cols), BF16)] * 2,
        grid_spec=pltpu.PrefetchScalarGridSpec(
            num_scalar_prefetch=1,
            grid=(1,),
            in_specs=[full((rows, width))] * m + [full((cols, width))] * 2,
            out_specs=[full((m * rows, cols))] * 2,
        ),
        compiler_params=params(),
        cost_estimate=cost(4 * m * rows * width * cols, 2 * width * (m * rows + 2 * cols)),
        name="attention_grad",
    )(rank, *cot_blocks, w_own, w_mirror)


def output_partial(attn_own, attn_mirror, w_own, w_mirror, rank, m):
    tokens, cols = attn_own.shape
    width = w_own.shape[1]
    rows = tokens // m
    step = 512

    def body(rank_ref, a0_ref, a1_ref, w0_ref, w1_ref, *o_refs):
        for j in range(m):
            at = pl.ds(pl.multiple_of((rank_ref[0] ^ j) * rows, rows), rows)
            total = dot_nn(a0_ref[at, :], w0_ref[...]) + dot_nn(a1_ref[at, :], w1_ref[...])
            o_refs[j][...] = total.astype(BF16)

    return pl.pallas_call(
        body,
        out_shape=[jax.ShapeDtypeStruct((rows, width), BF16)] * m,
        grid_spec=pltpu.PrefetchScalarGridSpec(
            num_scalar_prefetch=1,
            grid=(width // step,),
            in_specs=[pl.BlockSpec((tokens, cols), lambda i, r: (0, 0))] * 2
            + [pl.BlockSpec((cols, step), lambda i, r: (0, i))] * 2,
            out_specs=[pl.BlockSpec((rows, step), lambda i, r: (0, i))] * m,
        ),
        compiler_params=params(),
        cost_estimate=cost(4 * tokens * cols * width, 2 * (2 * cols + tokens) * width),
        name="output_partial",
    )(rank, attn_own, attn_mirror, w_own, w_mirror)


def weight_grad_partial(attn_own, attn_mirror, cot_blocks, rank, place, parts):
    m = len(cot_blocks)
    rows, width = cot_blocks[0].shape
    tokens, cols = attn_own.shape
    step = 512
    piece = cols // parts

    def body(rank_ref, place_ref, *refs):
        a0_ref, a1_ref, cots = refs[0], refs[1], refs[2 : 2 + m]
        keep_ref, send_ref, at_ref, sum_ref = refs[2 + m :]

        @pl.when(pl.program_id(0) == 0)
        def _():
            for j in range(m):
                start = pl.multiple_of((rank_ref[0] ^ j) * rows, rows)
                at_ref[j, :cols] = a0_ref[pl.ds(start, rows), :].T
                at_ref[j, cols:] = a1_ref[pl.ds(start, rows), :].T

        total = dot_nn(at_ref[0], cots[0][...])
        for j in range(1, m):
            total += dot_nn(at_ref[j], cots[j][...])
        sum_ref[...] = total.astype(BF16).reshape(2 * parts, piece, step)
        for j in range(parts):
            out_ref = send_ref if j % 2 else keep_ref
            out_ref[j // 2, 0] = sum_ref[place_ref[0] ^ j]
            out_ref[j // 2, 1] = sum_ref[parts + (place_ref[0] ^ j)]

    shape = (parts // 2, 2, piece, width)
    return pl.pallas_call(
        body,
        out_shape=[jax.ShapeDtypeStruct(shape, BF16)] * 2,
        grid_spec=pltpu.PrefetchScalarGridSpec(
            num_scalar_prefetch=2,
            grid=(width // step,),
            in_specs=[pl.BlockSpec((tokens, cols), lambda i, r, p: (0, 0))] * 2
            + [pl.BlockSpec((rows, step), lambda i, r, p: (0, i))] * m,
            out_specs=[pl.BlockSpec(shape[:3] + (step,), lambda i, r, p: (0, 0, 0, i))] * 2,
            scratch_shapes=[
                pltpu.VMEM((m, 2 * cols, rows), BF16),
                pltpu.VMEM((2 * parts, piece, step), BF16),
            ],
        ),
        compiler_params=params(),
        cost_estimate=cost(4 * tokens * cols * width, 2 * (2 * cols + tokens) * width),
        name="weight_grad_partial",
    )(rank, place, attn_own, attn_mirror, *cot_blocks)


def join_parts(pieces, place, dtype):
    parts = len(pieces)
    rows, width = pieces[0].shape
    step = 1024

    def body(place_ref, *refs):
        for j in range(parts):
            refs[parts][place_ref[0] ^ j] = refs[j][...].astype(dtype)

    joined = pl.pallas_call(
        body,
        out_shape=jax.ShapeDtypeStruct((parts, rows, width), dtype),
        grid_spec=pltpu.PrefetchScalarGridSpec(
            num_scalar_prefetch=1,
            grid=(width // step,),
            in_specs=[pl.BlockSpec((rows, step), lambda i, p: (0, i))] * parts,
            out_specs=pl.BlockSpec((parts, rows, step), lambda i, p: (0, 0, i)),
        ),
        compiler_params=params(),
        cost_estimate=cost(0, 6 * parts * rows * width),
        name="join_parts",
    )(place, *pieces)
    return joined.reshape(parts * rows, width)


def mask_bias(my_tiles, my_counts, tokens, q_rows):
    heads, blocks, slots = my_tiles.shape
    key_tile = lax.broadcasted_iota(jnp.int32, (1, 1, tokens, 1), 2) // TILE
    slot = lax.broadcasted_iota(jnp.int32, (1, 1, 1, slots), 3)
    seen = (my_tiles[:, :, None, :] == key_tile) & (slot < my_counts[:, :, None, None])
    bias = jnp.where(jnp.any(seen, axis=3), F32(0.0), F32(NEG))
    tiles = q_rows // TILE
    return bias.reshape(heads, blocks // tiles, tiles, tokens)


def shards(queries, key_rows, value_rows, out_weight, cotangent, tile_lists, live_counts):
    n = lax.axis_size("seq")
    dp = lax.axis_size("dp")
    m = n // 2
    s = lax.axis_index("seq")
    d = lax.axis_index("dp")
    half = (s // m).astype(jnp.int32).reshape(1)
    rank = (s % m).astype(jnp.int32).reshape(1)
    rows = queries.shape[1]
    cols, width = out_weight.shape
    heads = cols // HDIM
    place = d.astype(jnp.int32).reshape(1)
    xor = lambda x, bit: lax.ppermute(x, "seq", [(i, i ^ bit) for i in range(n)])

    def gather_parts(x):
        pieces = {0: x}
        bit = dp // 2
        while bit:
            pieces.update({j | bit: dp_xor(x, bit) for j, x in list(pieces.items())})
            bit //= 2
        return [pieces[j] for j in range(dp)]

    dp_xor = lambda x, bit: lax.ppermute(x, "dp", [(i, i ^ bit) for i in range(dp)])

    my_tiles = lax.dynamic_slice_in_dim(tile_lists, s * heads, heads, 0)
    my_counts = lax.dynamic_slice_in_dim(live_counts, s * heads, heads, 0)
    bias = mask_bias(my_tiles, my_counts, n * rows, 2 * rows)

    packed = pack_heads([queries[0], key_rows[0], value_rows[0]], n)
    packed = lax.all_to_all(packed, "seq", split_axis=0, concat_axis=0, tiled=True)

    attn_own, attn_send = attention_forward(packed, bias, half)

    piece = cols // dp
    w_piece = xor(lax.dynamic_slice_in_dim(out_weight, d * piece, piece, 0), m)
    bit = m // 2
    cot_at = {0: cotangent[0], bit: xor(cotangent[0], bit)}
    if bit > 1:
        cot_at[1] = xor(cotangent[0], 1)
    attn_send, w_piece, cot_at[bit] = lax.optimization_barrier(
        (attn_send, w_piece, cot_at[bit])
    )
    attn_mirror = xor(attn_send, m)
    w_pieces = gather_parts(w_piece)

    while bit > 1:
        bit //= 2
        for j in list(cot_at):
            if j | bit not in cot_at:
                cot_at[j | bit] = xor(cot_at[j], bit)
    cot_blocks = [cot_at[j] for j in range(m)]

    w_mirror = join_parts(w_pieces, place, BF16)
    grad_own, grad_send = attention_grad(cot_blocks, out_weight, w_mirror, rank)
    grad_mirror = xor(grad_send, m)
    attn_mirror, grad_send = lax.optimization_barrier((attn_mirror, grad_send))
    partials = output_partial(attn_own, attn_mirror, out_weight, w_mirror, rank, m)
    keep, send = weight_grad_partial(attn_own, attn_mirror, cot_blocks, rank, place, dp)
    grad_mirror, partials, keep, send = lax.optimization_barrier(
        (grad_mirror, partials, keep, send)
    )
    sums = [partials[0]] + [xor(partials[j], j) for j in range(1, m)]

    gw = keep.astype(F32) + dp_xor(send, 1).astype(F32)
    bit = 2
    while bit < dp:
        gw = gw[0::2].astype(F32) + dp_xor(gw[1::2].astype(BF16), bit).astype(F32)
        bit *= 2
    gw_own, gw_send = gw[0, 0], gw[0, 1].astype(BF16)

    grads = []
    for head in range(heads):
        if head == 1:
            gw_send, grad_own = lax.optimization_barrier((gw_send, grad_own))
        got = attention_backward(packed, bias, half, grad_own, grad_mirror, head)
        if head == 0:
            got, sums[1:3] = lax.optimization_barrier((got, sums[1:3]))
        else:
            got, sums[3:] = lax.optimization_barrier((got, sums[3:]))
        grads.append(got)
    gw = (gw_own + xor(gw_send, m).astype(F32)).astype(BF16)
    grads = [lax.all_to_all(x, "seq", split_axis=0, concat_axis=0, tiled=True) for x in grads]
    back_q, back_k, back_v = unpack_heads(grads)

    block_out = sum(x.astype(F32) for x in sums).astype(BF16)
    pieces = gather_parts(gw)
    grad_weight = join_parts(pieces, place, F32)
    return (block_out[None], back_q[None], back_k[None], back_v[None], grad_weight)


def solution(mesh):
    token_spec = P("dp", "seq", None)
    in_specs = (
        token_spec,
        token_spec,
        token_spec,
        P("seq", None),
        token_spec,
        P(),
        P(),
    )
    out_specs = (token_spec,) * 4 + (P("seq", None),)
    return jax.shard_map(shards, mesh=mesh, in_specs=in_specs, out_specs=out_specs, check_vma=False)
```

time: 478 us -> 268 us (0.56)
  Pallas kernels: 203 us -> 68.9 us
  waiting for transfers between devices: 207 us -> 133 us
  between operations: 14.3 us -> 0.87 us
  starting transfers between devices: 29.6 us -> 38.5 us
  local copies, waits for them, and re-layouts: 9.82 us -> 14.7 us
    ppermute x7 -> x10, waiting for transfers between devices: 160 us -> 58.1 us  [shards(): lax.ppermute(x, 'seq', [(i, i ^ bit) for i in range(n)])]
    pallas_call x1, Pallas kernels: 72.8 us -> 3.26 us  [pack_heads(): pl.pallas_call(body, out_shape=jax.ShapeDtypeStruct((n, count, rows, cols...]
    pallas_call x5 -> x8, Pallas kernels: 123 us -> 58.4 us  [the longest x2 19.7 us: attention_backward(): pl.pallas_call(body, out_shape=jax.ShapeDtypeStruct((n, 3, rows, HDIM), B...]
    all_to_all x1, waiting for transfers between devices: 0.01 us -> 45.1 us  [shards(): lax.all_to_all(packed, 'seq', split_axis=0, concat_axis=0, tiled=True)]
    all_to_all x3 -> x2, waiting for transfers between devices: 46.7 us -> 10.6 us  [shards(): lax.all_to_all(x, 'seq', split_axis=0, concat_axis=0, tiled=True)]
    ppermute x0 -> x8, waiting for transfers between devices: none -> 19.5 us  [shards(): lax.ppermute(x, 'dp', [(i, i ^ bit) for i in range(dp)])]
    ppermute x7 -> x10, starting transfers between devices: 7.86 us -> 18.6 us  [shards(): lax.ppermute(x, 'seq', [(i, i ^ bit) for i in range(n)])]
    reduce_sum x2 -> x0, other arithmetic: 7.13 us -> none  [the longest x1 4.55 us: shards(): block_out = jnp.sum(partial.astype(F32), axis=0).astype(BF16)]
  transfers between devices with their start and end apart: 13 -> 21, of which waited for: 6 -> 13; matrix products, arithmetic and copies ran while one was open for 3% -> 6% of each run, Pallas kernels for 27% -> 23%
where the time goes in v2:
time: 268 us; the launch traced here: 267 us
  waiting for transfers between devices  133 us (50%)
  Pallas kernels  68.9 us (26%)
  starting transfers between devices  38.5 us (14%)
  local copies, waits for them, and re-layouts  14.7 us (5%)
  other arithmetic  10.3 us (4%)
    ppermute x10, waiting for transfers between devices, shards(): lax.ppermute(x, 'seq', [(i, i ^ bit) for i in range(n)])  58.1 us
    all_to_all x1, waiting for transfers between devices, shards(): lax.all_to_all(packed, 'seq', split_axis=0, concat_axis=0, tiled=True)  45.1 us
    pallas_call x2, Pallas kernels, attention_backward(): pl.pallas_call(body, out_shape=jax.ShapeDtypeStruct((n, 3, rows, HDIM), B...  19.7 us
    ppermute x8, waiting for transfers between devices, shards(): lax.ppermute(x, 'dp', [(i, i ^ bit) for i in range(dp)])  19.5 us
    ppermute x10, starting transfers between devices, shards(): lax.ppermute(x, 'seq', [(i, i ^ bit) for i in range(n)])  18.6 us
    pallas_call x1, Pallas kernels, attention_forward(): pl.pallas_call(body, out_shape=[jax.ShapeDtypeStruct((tokens // 2, cols),...  16.3 us
    all_to_all x2, waiting for transfers between devices, shards(): lax.all_to_all(x, 'seq', split_axis=0, concat_axis=0, tiled=True)  10.6 us
    unnamed x38, local copies, waits for them, and re-layouts  9.95 us
  transfers between devices with their start and end apart: 21, of which 13 were waited for; matrix products, arithmetic and copies ran while one was open for 6% of the time, Pallas kernels for 23%

profile of v2, /device:TPU:0, one launch (start us, length us, event | category | flops | bytes accessed | tf_op | source)
XLA Modules:
  0.0 266.7 jit_solution(14731186545089503547)
XLA Ops:
  0.7 1.2 copy-done.8
  1.8 1.1 copy-done.9
  3.0 1.1 copy-done.10
  4.1 3.3 %pack_heads.1 = bf16[8,3,192,256]{3,2,1,0:T(8,128)(2,1)} custom-call(bf16[192,2048]{1,0:T(8,128)(2,1)S(1)} %bitcast.25, bf16[192,2048]{1,0:T(8,128)(2,1)S(1)} %bitcast.26, bf16[192,2048]{1,0:T(8,128)(2,1)S(1)} %bitcast.27), custom_call_target="tpu_custom_call" | custom-call | bytes 4718592 | tf_op jit(solution)/shard_map/pack_heads/pallas_call | solution.py:43
  7.3 7.3 %all-to-all-start = ((bf16[8,3,192,256]{3,2,1,0:T(8,128)(2,1)}), bf16[8,3,192,256]{3,2,1,0:T(8,128)(2,1)S(1)}, u32[]{:S(2)}, u32[]{:S(2)}) async-start(bf16[8,3,192,256]{3,2,1,0:T(8,128)(2,1)} %pack_heads.1), calls=%async_computation | async-start | bytes 4718592 | tf_op jit(solution)/shard_map/all_to_all | solution.py:374
  14.6 2.0 collective-permute-start.2
  16.6 1.5 collective-permute-start
  18.1 1.8 constant_dynamic-slice_fusion
  19.9 2.4 collective-permute-start.1
  23.1 1.4 and_reduce_fusion
  24.9 45.1 %all-to-all-done.q_ref.k_ref.v_ref = bf16[8,3,192,256]{3,2,1,0:T(8,128)(2,1)S(1)} async-done(((bf16[8,3,192,256]{3,2,1,0:T(8,128)(2,1)}), bf16[8,3,192,256]{3,2,1,0:T(8,128)(2,1)S(1)}, u32[]{:S(2)}, u32[]{:S(2)}) %all-to-all-start) | async-done | bytes 2359328 | tf_op jit(solution)/shard_map/all_to_all | solution.py:374
  70.0 16.3 %attention_forward.1 = (bf16[768,256]{1,0:T(8,128)(2,1)S(1)}, bf16[768,256]{1,0:T(8,128)(2,1)}) custom-call(s32[1]{0:T(128)} %bitcast.2.half_ref, bf16[8,3,192,256]{3,2,1,0:T(8,128)(2,1)S(1)} %all-to-all-done.q_ref.k_ref.v_ref, bf16[8,3,192,256]{3,2,1,0:T(8,128)(2,1)S(1)} %all-to-all-done.q_ref.k_ref.v_ref, ...), custom_call_target="tpu_custom_call" | custom-call | flops 2415919104 | bytes 3145728 | tf_op jit(solution)/shard_map/attention_forward/pallas_call | solution.py:115
  87.6 1.1 collective-permute-done.2.refs_2_.refs_4_
  88.8 1.5 collective-permute-start.3
  90.2 1.5 collective-permute-start.5
  91.7 8.4 %collective-permute-done.5.refs_2_ = bf16[64,3072]{1,0:T(8,128)(2,1)} collective-permute-done((bf16[64,3072]{1,0:T(8,128)(2,1)S(1)}, bf16[64,3072]{1,0:T(8,128)(2,1)}, u32[]{:S(2)}, u32[]{:S(2)}) %collective-permute-start.5) | collective-permute-done | bytes 393248 | tf_op jit(solution)/shard_map/ppermute | solution.py:367
  100.1 1.5 collective-permute-start.8
  102.2 2.4 join_parts.2
  104.6 1.1 copy-done.3
  105.7 10.0 %collective-permute-done.3.refs_3_.refs_5_ = bf16[192,3072]{1,0:T(8,128)(2,1)} collective-permute-done((bf16[192,3072]{1,0:T(8,128)(2,1)}, bf16[192,3072]{1,0:T(8,128)(2,1)}, u32[]{:S(2)}, u32[]{:S(2)}) %collective-permute-start.3) | collective-permute-done | bytes 1179680 | tf_op jit(solution)/shard_map/ppermute | solution.py:357
  115.7 7.2 %attention_grad.1 = (bf16[768,256]{1,0:T(8,128)(2,1)S(1)}, bf16[768,256]{1,0:T(8,128)(2,1)S(1)}) custom-call(s32[1]{0:T(128)} %bitcast.rank_ref, bf16[192,3072]{1,0:T(8,128)(2,1)S(1)} %bitcast.30, bf16[192,3072]{1,0:T(8,128)(2,1)} %collective-permute-done.refs_1_.refs_3_, bf16[192,3072]{1,0:T(8,128)(2,1)} %collective-permute-done.2.refs_2_.refs_4_, ...), custom_call_target="tpu_custom_call" | custom-call | flops 2415919104 | bytes 7864320 | tf_op jit(solution)/shard_map/attention_grad/pallas_call | solution.py:219
  123.0 2.4 collective-permute-start.7
  125.4 6.7 %output_partial.1 = (bf16[192,3072]{1,0:T(8,128)(2,1)S(1)}, bf16[192,3072]{1,0:T(8,128)(2,1)S(1)}, bf16[192,3072]{1,0:T(8,128)(2,1)S(1)}, bf16[192,3072]{1,0:T(8,128)(2,1)}) custom-call(s32[1]{0:T(128)} %bitcast.rank_ref, bf16[768,256]{1,0:T(8,128)(2,1)S(1)} %copy-done.15, bf16[768,256]{1,0:T(8,128)(2,1)} %collective-permute-done.8.a1_ref.refs_1_, ...), custom_call_target="tpu_custom_call" | custom-call | flops 2415919104 | bytes 7864320 | tf_op jit(solution)/shard_map/output_partial/pallas_call | solution.py:246
  132.1 1.0 copy-done.6
  133.1 8.1 %weight_grad_partial.1 = (bf16[2,2,64,3072]{3,2,1,0:T(8,128)(2,1)}, bf16[2,2,64,3072]{3,2,1,0:T(8,128)(2,1)}) custom-call(s32[1]{0:T(128)} %bitcast.rank_ref, s32[1]{0:T(128)} %bitcast.7.place_ref, bf16[768,256]{1,0:T(8,128)(2,1)S(1)} %copy-done.15, bf16[768,256]{1,0:T(8,128)(2,1)} %collective-permute-done.8.a1_ref.refs_1_, bf16[192,3072]{1,0:T(8,128)(2,1)S(1)} %bitcast.31, ...), custom_call_target="tpu_custom_call" | custom-call | flops 2415919104 | bytes 7864320 | tf_op jit(solution)/shard_map/weight_grad_partial/pallas_call | solution.py:290
  141.3 1.6 collective-permute-start.10
  143.3 1.6 collective-permute-done.11
  144.9 1.9 convert_add_fusion
  146.8 1.1 slice.34
  147.9 1.5 collective-permute-start.12
  149.4 9.9 %attention_backward.2 = bf16[8,3,192,128]{3,2,1,0:T(8,128)(2,1)S(1)} custom-call(s32[1]{0:T(128)} %bitcast.2.half_ref, bf16[8,3,192,256]{3,2,1,0:T(8,128)(2,1)S(1)} %all-to-all-done.q_ref.k_ref.v_ref, bf16[8,3,192,256]{3,2,1,0:T(8,128)(2,1)S(1)} %all-to-all-done.q_ref.k_ref.v_ref, bf16[8,3,192,256]{3,2,1,0:T(8,128)(2,1)S(1)} %all-to-all-done.q_ref.k_ref.v_ref, ...), custom_call_target="tpu_custom_call" | custom-call | flops 3019898880 | bytes 2752512 | tf_op jit(solution)/shard_map/attention_backward/pallas_call | solution.py:183
  159.3 1.1 copy-done.5
  160.4 9.2 %collective-permute-done.10 = bf16[192,3072]{1,0:T(8,128)(2,1)S(1)} collective-permute-done((bf16[192,3072]{1,0:T(8,128)(2,1)S(1)}, bf16[192,3072]{1,0:T(8,128)(2,1)S(1)}, u32[]{:S(2)}, u32[]{:S(2)}) %collective-permute-start.10) | collective-permute-done | bytes 1179680 | tf_op jit(solution)/shard_map/ppermute | solution.py:357
  171.0 4.5 %all-to-all-start.1 = ((bf16[8,3,192,128]{3,2,1,0:T(8,128)(2,1)}), bf16[8,3,192,128]{3,2,1,0:T(8,128)(2,1)S(1)}, u32[]{:S(2)}, u32[]{:S(2)}) async-start(bf16[8,3,192,128]{3,2,1,0:T(8,128)(2,1)} %copy-done.5), calls=%async_computation.1 | async-start | bytes 2359296 | tf_op jit(solution)/shard_map/all_to_all | solution.py:426
  175.4 2.9 %collective-permute-start.13 = (bf16[192,3072]{1,0:T(8,128)(2,1)}, bf16[192,3072]{1,0:T(8,128)(2,1)}, u32[]{:S(2)}, u32[]{:S(2)}) collective-permute-start(bf16[192,3072]{1,0:T(8,128)(2,1)} %get-tuple-element.59), channel_id=1, source_target_pairs={{0,3},{1,2},{2,1},{3,0},{4,7},{5,6},{6,5},{7,4},{8,11},{9,10},{10,... | collective-permute-start | bytes 3538952 | tf_op jit(solution)/shard_map/ppermute | solution.py:357
  178.3 1.8 slice_add_fusion
  181.4 2.4 collective-permute-start.14
  183.8 9.9 %attention_backward.3 = bf16[8,3,192,128]{3,2,1,0:T(8,128)(2,1)S(1)} custom-call(s32[1]{0:T(128)} %bitcast.2.half_ref, bf16[8,3,192,256]{3,2,1,0:T(8,128)(2,1)S(1)} %copy-done.2, bf16[8,3,192,256]{3,2,1,0:T(8,128)(2,1)S(1)} %copy-done.2, bf16[8,3,192,256]{3,2,1,0:T(8,128)(2,1)S(1)} %copy-done.2, f32[2,4,6,1536]{3,2,1,0:T(8,128)S(1)} %copy.19.bias_ref, ...), custom_call_target="tpu_custom_call" | custom-call | flops 3019898880 | bytes 2752512 | tf_op jit(solution)/shard_map/attention_backward/pallas_call | solution.py:183
  193.7 1.0 copy-done.4
  194.7 36.8 %collective-permute-done.13 = bf16[192,3072]{1,0:T(8,128)(2,1)} collective-permute-done((bf16[192,3072]{1,0:T(8,128)(2,1)}, bf16[192,3072]{1,0:T(8,128)(2,1)}, u32[]{:S(2)}, u32[]{:S(2)}) %collective-permute-start.13) | collective-permute-done | bytes 1179680 | tf_op jit(solution)/shard_map/ppermute | solution.py:357
  231.4 3.6 %all-to-all-start.2 = ((bf16[8,3,192,128]{3,2,1,0:T(8,128)(2,1)}), bf16[8,3,192,128]{3,2,1,0:T(8,128)(2,1)S(1)}, u32[]{:S(2)}, u32[]{:S(2)}) async-start(bf16[8,3,192,128]{3,2,1,0:T(8,128)(2,1)} %copy-done.4), calls=%async_computation.2 | async-start | bytes 2359296 | tf_op jit(solution)/shard_map/all_to_all | solution.py:426
  235.1 1.4 fusion.2.refs_0_
  236.5 1.6 collective-permute-start.16
  238.0 9.0 %collective-permute-done.16.refs_2_ = bf16[64,3072]{1,0:T(8,128)(2,1)S(1)} collective-permute-done((bf16[64,3072]{1,0:T(8,128)(2,1)S(1)}, bf16[64,3072]{1,0:T(8,128)(2,1)S(1)}, u32[]{:S(2)}, u32[]{:S(2)}) %collective-permute-start.16) | collective-permute-done | bytes 393248 | tf_op jit(solution)/shard_map/ppermute | solution.py:367
  247.1 3.7 %fusion = bf16[1,192,3072]{2,1,0:T(8,128)(2,1)} fusion(bf16[192,3072]{1,0:T(8,128)(2,1)} %collective-permute-done.13, bf16[192,3072]{1,0:T(8,128)(2,1)} %copy-done.18, bf16[192,3072]{1,0:T(8,128)(2,1)} %collective-permute-done.9, bf16[192,3072]{1,0:T(8,128)(2,1)S(1)} %copy-done.7), kind=kLoop, calls=%fused_computation.5 | loop fusion | flops 4718592 | bytes 5898240 | tf_op jit(solution)/shard_map/broadcast_in_dim | solution.py:432
  250.8 2.2 join_parts.3
  253.0 10.6 %all-to-all-done.2.refs_1_ = bf16[8,3,192,128]{3,2,1,0:T(8,128)(2,1)S(1)} async-done(((bf16[8,3,192,128]{3,2,1,0:T(8,128)(2,1)}), bf16[8,3,192,128]{3,2,1,0:T(8,128)(2,1)S(1)}, u32[]{:S(2)}, u32[]{:S(2)}) %all-to-all-start.2) | async-done | bytes 1179680 | tf_op jit(solution)/shard_map/all_to_all | solution.py:426
  263.6 3.1 %unpack_heads.1 = (bf16[192,2048]{1,0:T(8,128)(2,1)}, bf16[192,2048]{1,0:T(8,128)(2,1)}, bf16[192,2048]{1,0:T(8,128)(2,1)}) custom-call(bf16[8,3,192,128]{3,2,1,0:T(8,128)(2,1)S(1)} %all-to-all-done.1.refs_0_, bf16[8,3,192,128]{3,2,1,0:T(8,128)(2,1)S(1)} %all-to-all-done.2.refs_1_), custom_call_target="tpu_custom_call" | custom-call | bytes 4718592 | tf_op jit(solution)/shard_map/unpack_heads/pallas_call | solution.py:65
  (58 shorter events, 6.3 us)
Async XLA Ops:
  0.6 21.6 %copy-start = (s32[16,24,16]{1,2,0:T(8,128)S(1)}, s32[16,24,16]{1,2,0:T(8,128)}, u32[]{:S(2)}) copy-start(s32[16,24,16]{1,2,0:T(8,128)} %param.12) | copy-start | bytes 73732
  0.6 1.2 copy-start.8
  1.8 1.1 copy-start.9
  3.0 1.1 copy-start.10
  7.3 62.7 %all-to-all-start = ((bf16[8,3,192,256]{3,2,1,0:T(8,128)(2,1)}), bf16[8,3,192,256]{3,2,1,0:T(8,128)(2,1)S(1)}, u32[]{:S(2)}, u32[]{:S(2)}) async-start(bf16[8,3,192,256]{3,2,1,0:T(8,128)(2,1)} %pack_heads.1), calls=%async_computation | async-start | bytes 4718592 | tf_op jit(solution)/shard_map/all_to_all | solution.py:374
  14.6 74.1 %collective-permute-start.2 = (bf16[192,3072]{1,0:T(8,128)(2,1)}, bf16[192,3072]{1,0:T(8,128)(2,1)}, u32[]{:S(2)}, u32[]{:S(2)}) collective-permute-start(bf16[192,3072]{1,0:T(8,128)(2,1)} %bitcast.28), channel_id=1, source_target_pairs={{0,2},{1,3},{2,0},{3,1},{4,6},{5,7},{6,4},{7,5},{8,10},{9,11},{10,... | collective-permute-start | bytes 3538952 | tf_op jit(solution)/shard_map/ppermute | solution.py:357
  16.6 89.1 %collective-permute-start = (bf16[192,3072]{1,0:T(8,128)(2,1)}, bf16[192,3072]{1,0:T(8,128)(2,1)}, u32[]{:S(2)}, u32[]{:S(2)}) collective-permute-start(bf16[192,3072]{1,0:T(8,128)(2,1)} %bitcast.29), channel_id=1, source_target_pairs={{0,1},{1,0},{2,3},{3,2},{4,5},{5,4},{6,7},{7,6},{8,9},{9,8},{10,11... | collective-permute-start | bytes 3538952 | tf_op jit(solution)/shard_map/ppermute | solution.py:357
  19.9 67.7 %collective-permute-start.1 = (bf16[64,3072]{1,0:T(8,128)(2,1)}, bf16[64,3072]{1,0:T(8,128)(2,1)S(1)}, u32[]{:S(2)}, u32[]{:S(2)}) collective-permute-start(bf16[64,3072]{1,0:T(8,128)(2,1)} %constant_dynamic-slice_fusion), channel_id=1, source_target_pairs={{0,4},{1,5},{2,6},{3,7},{4,0},{5,1},{6,2},{7,3},{8,12},{9,13},{10,... | collective-permute-start | bytes 1179656 | tf_op jit(solution)/shard_map/ppermute | solution.py:357
  70.0 79.4 %copy-start.1 = (bf16[8,3,192,256]{3,2,1,0:T(8,128)(2,1)}, bf16[8,3,192,256]{3,2,1,0:T(8,128)(2,1)S(1)}, u32[]{:S(2)}) copy-start(bf16[8,3,192,256]{3,2,1,0:T(8,128)(2,1)S(1)} %all-to-all-done.q_ref.k_ref.v_ref) | copy-start | bytes 7077892
  86.3 0.7 copy-start.14
  88.8 27.0 %collective-permute-start.3 = (bf16[192,3072]{1,0:T(8,128)(2,1)}, bf16[192,3072]{1,0:T(8,128)(2,1)}, u32[]{:S(2)}, u32[]{:S(2)}) collective-permute-start(bf16[192,3072]{1,0:T(8,128)(2,1)} %collective-permute-done.2.refs_2_.refs_4_), channel_id=1, source_target_pairs={{0,1},{1,0},{2,3},{3,2},{4,5},{5,4},{6,7},{7,6},{8,9},{9,8},{10,11... | collective-permute-start | bytes 3538952 | tf_op jit(solution)/shard_map/ppermute | solution.py:357
  90.2 9.9 %collective-permute-start.5 = (bf16[64,3072]{1,0:T(8,128)(2,1)S(1)}, bf16[64,3072]{1,0:T(8,128)(2,1)}, u32[]{:S(2)}, u32[]{:S(2)}) collective-permute-start(bf16[64,3072]{1,0:T(8,128)(2,1)S(1)} %collective-permute-done.1.refs_0_), channel_id=1, source_target_pairs={{0,16},{8,24},{16,0},{24,8},{1,17},{9,25},{17,1},{25,9},{2,18},{10... | collective-permute-start | bytes 1179656 | tf_op jit(solution)/shard_map/ppermute | solution.py:367
  91.7 10.0 %collective-permute-start.4 = (bf16[64,3072]{1,0:T(8,128)(2,1)S(1)}, bf16[64,3072]{1,0:T(8,128)(2,1)}, u32[]{:S(2)}, u32[]{:S(2)}) collective-permute-start(bf16[64,3072]{1,0:T(8,128)(2,1)S(1)} %collective-permute-done.1.refs_0_), channel_id=1, source_target_pairs={{0,8},{8,0},{16,24},{24,16},{1,9},{9,1},{17,25},{25,17},{2,10},{10... | collective-permute-start | bytes 1179656 | tf_op jit(solution)/shard_map/ppermute | solution.py:367
  100.1 2.1 collective-permute-start.6
  100.1 25.3 %collective-permute-start.8 = (bf16[768,256]{1,0:T(8,128)(2,1)}, bf16[768,256]{1,0:T(8,128)(2,1)}, u32[]{:S(2)}, u32[]{:S(2)}) collective-permute-start(bf16[768,256]{1,0:T(8,128)(2,1)} %get-tuple-element.41), channel_id=1, source_target_pairs={{0,4},{1,5},{2,6},{3,7},{4,0},{5,1},{6,2},{7,3},{8,12},{9,13},{10,... | collective-permute-start | bytes 1179656 | tf_op jit(solution)/shard_map/ppermute | solution.py:357
  102.2 13.5 %copy-start.11 = (bf16[1,192,3072]{2,1,0:T(8,128)(2,1)S(1)}, bf16[1,192,3072]{2,1,0:T(8,128)(2,1)}, u32[]{:S(2)}) copy-start(bf16[1,192,3072]{2,1,0:T(8,128)(2,1)} %param.11) | copy-start | bytes 3538948
  104.6 1.1 copy-start.3
  115.7 9.7 %copy-start.15 = (bf16[768,256]{1,0:T(8,128)(2,1)S(1)}, bf16[768,256]{1,0:T(8,128)(2,1)}, u32[]{:S(2)}) copy-start(bf16[768,256]{1,0:T(8,128)(2,1)} %copy-done.14) | copy-start | bytes 1179652
  123.0 26.4 %copy-start.12 = (bf16[768,256]{1,0:T(8,128)(2,1)}, bf16[768,256]{1,0:T(8,128)(2,1)S(1)}, u32[]{:S(2)}) copy-start(bf16[768,256]{1,0:T(8,128)(2,1)S(1)} %get-tuple-element.58.g0_ref) | copy-start | bytes 1179652
  123.0 18.3 %collective-permute-start.7 = (bf16[768,256]{1,0:T(8,128)(2,1)S(1)}, bf16[768,256]{1,0:T(8,128)(2,1)S(1)}, u32[]{:S(2)}, u32[]{:S(2)}) collective-permute-start(bf16[768,256]{1,0:T(8,128)(2,1)S(1)} %get-tuple-element.39), channel_id=1, source_target_pairs={{0,4},{1,5},{2,6},{3,7},{4,0},{5,1},{6,2},{7,3},{8,12},{9,13},{10,... | collective-permute-start | bytes 1179656 | tf_op jit(solution)/shard_map/ppermute | solution.py:357
  132.1 1.0 copy-start.6
  141.3 3.6 %collective-permute-start.11 = (bf16[2,2,64,3072]{3,2,1,0:T(8,128)(2,1)}, bf16[2,2,64,3072]{3,2,1,0:T(8,128)(2,1)S(1)}, u32[]{:S(2)}, u32[]{:S(2)}) collective-permute-start(bf16[2,2,64,3072]{3,2,1,0:T(8,128)(2,1)} %get-tuple-element.57), channel_id=1, source_target_pairs={{0,8},{8,0},{16,24},{24,16},{1,9},{9,1},{17,25},{25,17},{2,10},{10... | collective-permute-start | bytes 4718600 | tf_op jit(solution)/shard_map/ppermute | solution.py:367
  141.3 28.4 %collective-permute-start.10 = (bf16[192,3072]{1,0:T(8,128)(2,1)S(1)}, bf16[192,3072]{1,0:T(8,128)(2,1)S(1)}, u32[]{:S(2)}, u32[]{:S(2)}) collective-permute-start(bf16[192,3072]{1,0:T(8,128)(2,1)S(1)} %get-tuple-element.53), channel_id=1, source_target_pairs={{0,2},{1,3},{2,0},{3,1},{4,6},{5,7},{6,4},{7,5},{8,10},{9,11},{10,... | collective-permute-start | bytes 3538952 | tf_op jit(solution)/shard_map/ppermute | solution.py:357
  142.8 28.1 %collective-permute-start.9 = (bf16[192,3072]{1,0:T(8,128)(2,1)S(1)}, bf16[192,3072]{1,0:T(8,128)(2,1)}, u32[]{:S(2)}, u32[]{:S(2)}) collective-permute-start(bf16[192,3072]{1,0:T(8,128)(2,1)S(1)} %get-tuple-element.52), channel_id=1, source_target_pairs={{0,1},{1,0},{2,3},{3,2},{4,5},{5,4},{6,7},{7,6},{8,9},{9,8},{10,11... | collective-permute-start | bytes 3538952 | tf_op jit(solution)/shard_map/ppermute | solution.py:357
  146.8 2.6 copy-start.16
  147.9 30.4 %collective-permute-start.12 = (bf16[1,2,64,3072]{3,2,1,0:T(8,128)(2,1)}, bf16[1,2,64,3072]{3,2,1,0:T(8,128)(2,1)}, u32[]{:S(2)}, u32[]{:S(2)}) collective-permute-start(bf16[1,2,64,3072]{3,2,1,0:T(8,128)(2,1)} %slice.34), channel_id=1, source_target_pairs={{0,16},{8,24},{16,0},{24,8},{1,17},{9,25},{17,1},{25,9},{2,18},{10... | collective-permute-start | bytes 2359304 | tf_op jit(solution)/shard_map/ppermute | solution.py:367
  159.3 1.1 copy-start.5
  169.7 1.0 copy-start.18
  171.0 60.5 %all-to-all-start.1 = ((bf16[8,3,192,128]{3,2,1,0:T(8,128)(2,1)}), bf16[8,3,192,128]{3,2,1,0:T(8,128)(2,1)S(1)}, u32[]{:S(2)}, u32[]{:S(2)}) async-start(bf16[8,3,192,128]{3,2,1,0:T(8,128)(2,1)} %copy-done.5), calls=%async_computation.1 | async-start | bytes 2359296 | tf_op jit(solution)/shard_map/all_to_all | solution.py:426
  175.4 8.3 %copy-start.2 = (bf16[8,3,192,256]{3,2,1,0:T(8,128)(2,1)S(1)}, bf16[8,3,192,256]{3,2,1,0:T(8,128)(2,1)}, u32[]{:S(2)}) copy-start(bf16[8,3,192,256]{3,2,1,0:T(8,128)(2,1)} %copy-done.1) | copy-start | bytes 7077892
  175.4 8.3 %copy-start.13 = (bf16[768,256]{1,0:T(8,128)(2,1)S(1)}, bf16[768,256]{1,0:T(8,128)(2,1)}, u32[]{:S(2)}) copy-start(bf16[768,256]{1,0:T(8,128)(2,1)} %copy-done.12) | copy-start | bytes 1179652
  175.4 56.0 %collective-permute-start.13 = (bf16[192,3072]{1,0:T(8,128)(2,1)}, bf16[192,3072]{1,0:T(8,128)(2,1)}, u32[]{:S(2)}, u32[]{:S(2)}) collective-permute-start(bf16[192,3072]{1,0:T(8,128)(2,1)} %get-tuple-element.59), channel_id=1, source_target_pairs={{0,3},{1,2},{2,1},{3,0},{4,7},{5,6},{6,5},{7,4},{8,11},{9,10},{10,... | collective-permute-start | bytes 3538952 | tf_op jit(solution)/shard_map/ppermute | solution.py:357
  180.1 1.3 copy-start.17
  181.4 53.7 %collective-permute-start.14 = (bf16[64,3072]{1,0:T(8,128)(2,1)}, bf16[64,3072]{1,0:T(8,128)(2,1)}, u32[]{:S(2)}, u32[]{:S(2)}) collective-permute-start(bf16[64,3072]{1,0:T(8,128)(2,1)} %fusion.3), channel_id=1, source_target_pairs={{0,4},{1,5},{2,6},{3,7},{4,0},{5,1},{6,2},{7,3},{8,12},{9,13},{10,... | collective-permute-start | bytes 1179656 | tf_op jit(solution)/shard_map/ppermute | solution.py:357
  193.6 1.0 copy-start.4
  231.4 32.2 %all-to-all-start.2 = ((bf16[8,3,192,128]{3,2,1,0:T(8,128)(2,1)}), bf16[8,3,192,128]{3,2,1,0:T(8,128)(2,1)S(1)}, u32[]{:S(2)}, u32[]{:S(2)}) async-start(bf16[8,3,192,128]{3,2,1,0:T(8,128)(2,1)} %copy-done.4), calls=%async_computation.2 | async-start | bytes 2359296 | tf_op jit(solution)/shard_map/all_to_all | solution.py:426
  235.1 12.0 %copy-start.7 = (bf16[192,3072]{1,0:T(8,128)(2,1)S(1)}, bf16[192,3072]{1,0:T(8,128)(2,1)}, u32[]{:S(2)}) copy-start(bf16[192,3072]{1,0:T(8,128)(2,1)} %copy-done.6) | copy-start | bytes 3538948
  236.5 10.6 %collective-permute-start.16 = (bf16[64,3072]{1,0:T(8,128)(2,1)S(1)}, bf16[64,3072]{1,0:T(8,128)(2,1)S(1)}, u32[]{:S(2)}, u32[]{:S(2)}) collective-permute-start(bf16[64,3072]{1,0:T(8,128)(2,1)S(1)} %fusion.2.refs_0_), channel_id=1, source_target_pairs={{0,16},{8,24},{16,0},{24,8},{1,17},{9,25},{17,1},{25,9},{2,18},{10... | collective-permute-start | bytes 1179656 | tf_op jit(solution)/shard_map/ppermute | solution.py:367
  238.0 12.8 %collective-permute-start.15 = (bf16[64,3072]{1,0:T(8,128)(2,1)S(1)}, bf16[64,3072]{1,0:T(8,128)(2,1)S(1)}, u32[]{:S(2)}, u32[]{:S(2)}) collective-permute-start(bf16[64,3072]{1,0:T(8,128)(2,1)S(1)} %fusion.2.refs_0_), channel_id=1, source_target_pairs={{0,8},{8,0},{16,24},{24,16},{1,9},{9,1},{17,25},{25,17},{2,10},{10... | collective-permute-start | bytes 1179656 | tf_op jit(solution)/shard_map/ppermute | solution.py:367
  247.1 3.8 %collective-permute-start.17 = (bf16[64,3072]{1,0:T(8,128)(2,1)S(1)}, bf16[64,3072]{1,0:T(8,128)(2,1)S(1)}, u32[]{:S(2)}, u32[]{:S(2)}) collective-permute-start(bf16[64,3072]{1,0:T(8,128)(2,1)S(1)} %collective-permute-done.16.refs_2_), channel_id=1, source_target_pairs={{0,8},{8,0},{16,24},{24,16},{1,9},{9,1},{17,25},{25,17},{2,10},{10... | collective-permute-start | bytes 1179656 | tf_op jit(solution)/shard_map/ppermute | solution.py:367

commit v3 on v2

--- a/solution.py
+++ b/solution.py
@@ -10,6 +10,7 @@
 SCALE = HDIM**-0.5
 EXP2_SCALE = SCALE * 1.4426950408889634
 NEG = -1e30
+EXTRA = HDIM - 3
 VMEM_LIMIT = 48 * 1024 * 1024
 BF16 = jnp.bfloat16
 F32 = jnp.float32
@@ -74,20 +75,22 @@
     )(*packed)
 
 
-def masked_scores(q, k, bias):
-    s = dot_nt(q, k)
-    tiles = bias.shape[0]
-    s = s.reshape(tiles, TILE, s.shape[1]) + bias[:, None, :]
-    return s.reshape(tiles * TILE, s.shape[2])
-
-
-def masked_probs(q, k, bias):
-    s = masked_scores(q, k, bias)
-    e = jnp.exp2((s - jnp.max(s, axis=1, keepdims=True)) * EXP2_SCALE)
-    return e * (1.0 / jnp.sum(e, axis=1, keepdims=True))
-
-
-def attention_forward(packed, bias, half):
+def split3(x):
+    high = x.astype(BF16)
+    rest = x - high.astype(F32)
+    mid = rest.astype(BF16)
+    low = (rest - mid.astype(F32)).astype(BF16)
+    return high, mid, low
+
+
+def put_columns(base, columns):
+    lane = lax.broadcasted_iota(jnp.int32, base.shape, 1)
+    for at, column in enumerate(columns):
+        base = jnp.where(lane == EXTRA + at, column.astype(F32), base)
+    return base
+
+
+def attention_forward(packed, mask, half):
     n, _, rows, cols = packed.shape
     heads = cols // HDIM
     tokens = n * rows
@@ -96,13 +99,27 @@
     half_steps = steps // 2
     tiles = q_rows // TILE
 
-    def body(half_ref, q_ref, k_ref, v_ref, bias_ref, own_ref, send_ref):
-        q = q_ref[...].reshape(q_rows, HDIM)
-        k = k_ref[...].reshape(tokens, HDIM)
-        v = v_ref[...].reshape(tokens, HDIM)
-        probs = masked_probs(q, k, bias_ref[0, 0]).astype(BF16)
-        attn = dot_nn(probs, v).astype(BF16)
-        own = (pl.program_id(1) // half_steps) == half_ref[0]
+    def body(half_ref, q_ref, k_ref, v_ref, mask_ref, own_ref, send_ref, extra_ref, wide_ref):
+        i = pl.program_id(1)
+
+        @pl.when(i == 0)
+        def _():
+            wide_ref[:, :HDIM] = k_ref[...].reshape(tokens, HDIM)
+            wide_ref[:, HDIM:] = mask_ref[0]
+
+        shape = (q_rows, HDIM)
+        tile = lax.broadcasted_iota(jnp.int32, shape, 0) // TILE + i * tiles
+        ones = jnp.where(tile == lax.broadcasted_iota(jnp.int32, shape, 1), F32(1), F32(0))
+        q = jnp.concatenate([q_ref[...].reshape(shape), ones.astype(BF16)], axis=1)
+        s = dot_nt(q, wide_ref[...])
+        top = jnp.max(s, axis=1, keepdims=True)
+        e = jnp.exp2((s - top) * EXP2_SCALE)
+        total = jnp.sum(e, axis=1, keepdims=True)
+        attn = dot_nn(e.astype(BF16), v_ref[...].reshape(tokens, HDIM)) * (1.0 / total)
+        attn = attn.astype(BF16)
+        log_sum = top + jnp.log2(total) * (1.0 / EXP2_SCALE)
+        extra_ref[...] = put_columns(ones, split3(log_sum)).astype(BF16)
+        own = (i // half_steps) == half_ref[0]
 
         @pl.when(own)
         def _():
@@ -114,7 +131,8 @@
 
     return pl.pallas_call(
         body,
-        out_shape=[jax.ShapeDtypeStruct((tokens // 2, cols), BF16)] * 2,
+        out_shape=[jax.ShapeDtypeStruct((tokens // 2, cols), BF16)] * 2
+        + [jax.ShapeDtypeStruct((tokens, cols), BF16)],
         grid_spec=pltpu.PrefetchScalarGridSpec(
             num_scalar_prefetch=1,
             grid=(heads, steps),
@@ -122,7 +140,7 @@
                 pl.BlockSpec((2, 1, rows, HDIM), lambda h, i, r: (i, 0, 0, h)),
                 pl.BlockSpec((n, 1, rows, HDIM), lambda h, i, r: (0, 1, 0, h)),
                 pl.BlockSpec((n, 1, rows, HDIM), lambda h, i, r: (0, 2, 0, h)),
-                pl.BlockSpec((1, 1, tiles, tokens), lambda h, i, r: (h, i, 0, 0)),
+                pl.BlockSpec((1, tokens, HDIM), lambda h, i, r: (h, 0, 0)),
             ],
             out_specs=[
                 pl.BlockSpec(
@@ -133,34 +151,48 @@
                     (q_rows, HDIM),
                     lambda h, i, r: (jnp.clip(i - (1 - r[0]) * half_steps, 0, half_steps - 1), h),
                 ),
+                pl.BlockSpec((q_rows, HDIM), lambda h, i, r: (i, h)),
             ],
+            scratch_shapes=[pltpu.VMEM((tokens, 2 * HDIM), BF16)],
         ),
         compiler_params=params(),
         cost_estimate=cost(4 * tokens**2 * cols, 8 * tokens * cols, heads * tokens**2),
         name="attention_forward",
-    )(half, packed, packed, packed, bias)
-
-
-def attention_backward(packed, bias, half, grad_own, grad_mirror, head):
+    )(half, packed, packed, packed, mask)
+
+
+def attention_backward(packed, mask, half, extra, attn_own, attn_send, grad_own, grad_mirror, head):
     n, _, rows, cols = packed.shape
     tokens = n * rows
     q_rows = 2 * rows
     steps = n // 2
     half_steps = steps // 2
-    tiles = q_rows // TILE
-
-    def body(half_ref, q_ref, k_ref, v_ref, bias_ref, g0_ref, g1_ref, out_ref, dk_ref, dv_ref):
+
+    def body(half_ref, q_ref, k_ref, v_ref, mask_ref, extra_ref, *refs):
+        a0_ref, a1_ref, g0_ref, g1_ref, out_ref, dk_ref, dv_ref, wide_ref, wide_v_ref = refs
         i = pl.program_id(0)
+
+        @pl.when(i == 0)
+        def _():
+            wide_ref[:, :HDIM] = k_ref[...].reshape(tokens, HDIM)
+            wide_ref[:, HDIM:] = mask_ref[0]
+            wide_v_ref[:, :HDIM] = v_ref[...].reshape(tokens, HDIM)
+            lane = lax.broadcasted_iota(jnp.int32, (tokens, HDIM), 1)
+            wide_v_ref[:, HDIM:] = jnp.where(lane >= EXTRA, F32(-1), F32(0)).astype(BF16)
+
         q = q_ref[...].reshape(q_rows, HDIM)
-        k = k_ref[...].reshape(tokens, HDIM)
-        v = v_ref[...].reshape(tokens, HDIM)
         own = (i // half_steps) == half_ref[0]
         grad = jnp.where(own, g0_ref[...], g1_ref[...])
-        probs = masked_probs(q, k, bias_ref[0, 0])
-        grad_probs = dot_nt(grad, v)
-        row_dot = jnp.sum(probs * grad_probs, axis=1, keepdims=True)
-        grad_scores = (probs * (grad_probs - row_dot)).astype(BF16)
-        grad_q = dot_nn(grad_scores, k) * SCALE
+        attn = jnp.where(own, a0_ref[...], a1_ref[...])
+        row_dot = jnp.sum(grad.astype(F32) * attn.astype(F32), axis=1, keepdims=True)
+        zeros = jnp.zeros((q_rows, HDIM), F32)
+        wide_grad = jnp.concatenate(
+            [grad, put_columns(zeros, split3(row_dot)).astype(BF16)], axis=1
+        )
+        wide_q = jnp.concatenate([q, extra_ref[...]], axis=1)
+        probs = jnp.exp2(dot_nt(wide_q, wide_ref[...]) * EXP2_SCALE)
+        grad_scores = (probs * dot_nt(wide_grad, wide_v_ref[...])).astype(BF16)
+        grad_q = dot_nn(grad_scores, wide_ref[:, :HDIM]) * SCALE
         out_ref[pl.ds(2 * i, 2), 0] = grad_q.astype(BF16).reshape(2, rows, HDIM)
         dk_t = dot_nn(q.T, grad_scores)
         dv_t = dot_nn(grad.T, probs.astype(BF16))
@@ -190,17 +222,18 @@
                 pl.BlockSpec((2, 1, rows, HDIM), lambda i, r: (i, 0, 0, head)),
                 pl.BlockSpec((n, 1, rows, HDIM), lambda i, r: (0, 1, 0, head)),
                 pl.BlockSpec((n, 1, rows, HDIM), lambda i, r: (0, 2, 0, head)),
-                pl.BlockSpec((1, 1, tiles, tokens), lambda i, r: (head, i, 0, 0)),
-                pl.BlockSpec((q_rows, HDIM), lambda i, r: (i % half_steps, head)),
-                pl.BlockSpec((q_rows, HDIM), lambda i, r: (i % half_steps, head)),
-            ],
+                pl.BlockSpec((1, tokens, HDIM), lambda i, r: (head, 0, 0)),
+                pl.BlockSpec((q_rows, HDIM), lambda i, r: (i, head)),
+            ]
+            + [pl.BlockSpec((q_rows, HDIM), lambda i, r: (i % half_steps, head))] * 4,
             out_specs=pl.BlockSpec((n, 3, rows, HDIM), lambda i, r: (0, 0, 0, 0)),
-            scratch_shapes=[pltpu.VMEM((HDIM, tokens), F32), pltpu.VMEM((HDIM, tokens), F32)],
+            scratch_shapes=[pltpu.VMEM((HDIM, tokens), F32)] * 2
+            + [pltpu.VMEM((tokens, 2 * HDIM), BF16)] * 2,
         ),
         compiler_params=params(),
         cost_estimate=cost(10 * tokens**2 * HDIM, 14 * tokens * HDIM, tokens**2),
         name="attention_backward",
-    )(half, packed, packed, packed, bias, grad_own, grad_mirror)
+    )(half, packed, packed, packed, mask, extra, attn_own, attn_send, grad_own, grad_mirror)
 
 
 def attention_grad(cot_blocks, w_own, w_mirror, rank):
@@ -332,14 +365,18 @@
     return joined.reshape(parts * rows, width)
 
 
-def mask_bias(my_tiles, my_counts, tokens, q_rows):
+def key_mask(my_tiles, my_counts, tokens):
     heads, blocks, slots = my_tiles.shape
-    key_tile = lax.broadcasted_iota(jnp.int32, (1, 1, tokens, 1), 2) // TILE
+    key_tile = lax.broadcasted_iota(jnp.int32, (1, blocks, 1, 1), 1)
     slot = lax.broadcasted_iota(jnp.int32, (1, 1, 1, slots), 3)
-    seen = (my_tiles[:, :, None, :] == key_tile) & (slot < my_counts[:, :, None, None])
-    bias = jnp.where(jnp.any(seen, axis=3), F32(0.0), F32(NEG))
-    tiles = q_rows // TILE
-    return bias.reshape(heads, blocks // tiles, tiles, tokens)
+    seen = (my_tiles[:, None] == key_tile) & (slot < my_counts[:, None, :, None])
+    mask = jnp.where(jnp.any(seen, axis=3), F32(0), F32(NEG))
+    mask = jnp.pad(mask, ((0, 0), (0, 0), (0, HDIM - blocks)))
+    lane = lax.broadcasted_iota(jnp.int32, mask.shape, 2)
+    mask = jnp.where(lane >= EXTRA, F32(-1), mask).astype(BF16)
+    return jnp.broadcast_to(mask[:, :, None], (heads, blocks, TILE, HDIM)).reshape(
+        heads, tokens, HDIM
+    )
 
 
 def shards(queries, key_rows, value_rows, out_weight, cotangent, tile_lists, live_counts):
@@ -368,12 +405,12 @@
 
     my_tiles = lax.dynamic_slice_in_dim(tile_lists, s * heads, heads, 0)
     my_counts = lax.dynamic_slice_in_dim(live_counts, s * heads, heads, 0)
-    bias = mask_bias(my_tiles, my_counts, n * rows, 2 * rows)
+    mask = key_mask(my_tiles, my_counts, n * rows)
 
     packed = pack_heads([queries[0], key_rows[0], value_rows[0]], n)
     packed = lax.all_to_all(packed, "seq", split_axis=0, concat_axis=0, tiled=True)
 
-    attn_own, attn_send = attention_forward(packed, bias, half)
+    attn_own, attn_sent, extra = attention_forward(packed, mask, half)
 
     piece = cols // dp
     w_piece = xor(lax.dynamic_slice_in_dim(out_weight, d * piece, piece, 0), m)
@@ -382,10 +419,13 @@
     if bit > 1:
         cot_at[1] = xor(cotangent[0], 1)
     attn_send, w_piece, cot_at[bit] = lax.optimization_barrier(
-        (attn_send, w_piece, cot_at[bit])
+        (attn_sent, w_piece, cot_at[bit])
     )
     attn_mirror = xor(attn_send, m)
-    w_pieces = gather_parts(w_piece)
+
+    w_pieces = [w_piece] + [dp_xor(w_piece, j) for j in range(1, dp)]
+    w_pieces, attn_mirror = lax.optimization_barrier((w_pieces, attn_mirror))
+    w_mirror = join_parts(w_pieces, place, BF16)
 
     while bit > 1:
         bit //= 2
@@ -394,16 +434,23 @@
                 cot_at[j | bit] = xor(cot_at[j], bit)
     cot_blocks = [cot_at[j] for j in range(m)]
 
-    w_mirror = join_parts(w_pieces, place, BF16)
+    partials = output_partial(attn_own, attn_mirror, out_weight, w_mirror, rank, m)
+    partials, cot_blocks = lax.optimization_barrier((partials, cot_blocks))
+    partials = dict(enumerate(partials))
+
+    def halve(bit):
+        for j in [j for j in sorted(partials, reverse=True) if j & bit and j > bit]:
+            got = xor(partials.pop(j), bit).astype(F32)
+            partials[j ^ bit] = (partials[j ^ bit].astype(F32) + got).astype(BF16)
+
+    halve(1)
     grad_own, grad_send = attention_grad(cot_blocks, out_weight, w_mirror, rank)
     grad_mirror = xor(grad_send, m)
     attn_mirror, grad_send = lax.optimization_barrier((attn_mirror, grad_send))
-    partials = output_partial(attn_own, attn_mirror, out_weight, w_mirror, rank, m)
     keep, send = weight_grad_partial(attn_own, attn_mirror, cot_blocks, rank, place, dp)
-    grad_mirror, partials, keep, send = lax.optimization_barrier(
-        (grad_mirror, partials, keep, send)
+    grad_mirror, keep, send, partials = lax.optimization_barrier(
+        (grad_mirror, keep, send, partials)
     )
-    sums = [partials[0]] + [xor(partials[j], j) for j in range(1, m)]
 
     gw = keep.astype(F32) + dp_xor(send, 1).astype(F32)
     bit = 2
@@ -412,21 +459,26 @@
         bit *= 2
     gw_own, gw_send = gw[0, 0], gw[0, 1].astype(BF16)
 
+    bit = 2
+    while bit < m:
+        halve(bit)
+        bit *= 2
+    got = [xor(partials[j], j) for j in sorted(partials) if j]
     grads = []
     for head in range(heads):
         if head == 1:
             gw_send, grad_own = lax.optimization_barrier((gw_send, grad_own))
-        got = attention_backward(packed, bias, half, grad_own, grad_mirror, head)
-        if head == 0:
-            got, sums[1:3] = lax.optimization_barrier((got, sums[1:3]))
-        else:
-            got, sums[3:] = lax.optimization_barrier((got, sums[3:]))
-        grads.append(got)
+        grads.append(
+            attention_backward(
+                packed, mask, half, extra, attn_own, attn_sent, grad_own, grad_mirror, head
+            )
+        )
+    grads[0], got = lax.optimization_barrier((grads[0], got))
     gw = (gw_own + xor(gw_send, m).astype(F32)).astype(BF16)
     grads = [lax.all_to_all(x, "seq", split_axis=0, concat_axis=0, tiled=True) for x in grads]
     back_q, back_k, back_v = unpack_heads(grads)
 
-    block_out = sum(x.astype(F32) for x in sums).astype(BF16)
+    block_out = sum(x.astype(F32) for x in [partials[0]] + got).astype(BF16)
     pieces = gather_parts(gw)
     grad_weight = join_parts(pieces, place, F32)
     return (block_out[None], back_q[None], back_k[None], back_v[None], grad_weight)

time: 268 us -> 257 us (0.959)
  Pallas kernels: 68.9 us -> 63.6 us
  starting transfers between devices: 38.5 us -> 34.1 us
  other arithmetic: 10.3 us -> 7.42 us
    ppermute x10, waiting for transfers between devices: 58.1 us -> 32 us  [shards(): lax.ppermute(x, 'seq', [(i, i ^ bit) for i in range(n)])]
    all_to_all x2, waiting for transfers between devices: 10.6 us -> 30.2 us  [shards(): lax.all_to_all(x, 'seq', split_axis=0, concat_axis=0, tiled=True)]
    ppermute x8, waiting for transfers between devices: 19.5 us -> 24.1 us  [shards(): lax.ppermute(x, 'dp', [(i, i ^ bit) for i in range(dp)])]
    ppermute x10, starting transfers between devices: 18.6 us -> 14.4 us  [shards(): lax.ppermute(x, 'seq', [(i, i ^ bit) for i in range(n)])]
    unnamed x38 -> x48, local copies, waits for them, and re-layouts: 9.95 us -> 12.8 us
  transfers between devices with their start and end apart: 21 -> 21, of which waited for: 13 -> 13; matrix products, arithmetic and copies ran while one was open for 6% -> 5% of each run, Pallas kernels for 23% -> 23%
where the time goes in v3:
time: 257 us
  waiting for transfers between devices  133 us (52%)
  Pallas kernels  63.6 us (25%)
  starting transfers between devices  34.1 us (13%)
  local copies, waits for them, and re-layouts  17.2 us (7%)
  other arithmetic  7.42 us (3%)
    all_to_all x1, waiting for transfers between devices, shards(): lax.all_to_all(packed, 'seq', split_axis=0, concat_axis=0, tiled=True)  46.9 us
    ppermute x10, waiting for transfers between devices, shards(): lax.ppermute(x, 'seq', [(i, i ^ bit) for i in range(n)])  32 us
    all_to_all x2, waiting for transfers between devices, shards(): lax.all_to_all(x, 'seq', split_axis=0, concat_axis=0, tiled=True)  30.2 us
    ppermute x8, waiting for transfers between devices, shards(): lax.ppermute(x, 'dp', [(i, i ^ bit) for i in range(dp)])  24.1 us
    pallas_call x2, Pallas kernels, attention_backward(): pl.pallas_call(body, out_shape=jax.ShapeDtypeStruct((n, 3, rows, HDIM), B...  18.7 us
    pallas_call x1, Pallas kernels, attention_forward(): pl.pallas_call(body, out_shape=[jax.ShapeDtypeStruct((tokens // 2, cols),...  15.9 us
    ppermute x10, starting transfers between devices, shards(): lax.ppermute(x, 'seq', [(i, i ^ bit) for i in range(n)])  14.4 us
    unnamed x48, local copies, waits for them, and re-layouts  12.8 us
  transfers between devices with their start and end apart: 21, of which 13 were waited for; matrix products, arithmetic and copies ran while one was open for 5% of the time, Pallas kernels for 23%

profile of v3, /device:TPU:0, one launch (start us, length us, event | category | flops | bytes accessed | tf_op | source)
XLA Modules:
  0.0 256.5 jit_solution(211955130741234292)
XLA Ops:
  0.7 1.2 copy-done.15
  1.8 1.1 copy-done.16
  3.0 1.1 copy-done.17
  4.8 1.4 copy-done.2
  6.2 7.3 %all-to-all-start = ((bf16[8,3,192,256]{3,2,1,0:T(8,128)(2,1)}), bf16[8,3,192,256]{3,2,1,0:T(8,128)(2,1)S(1)}, u32[]{:S(2)}, u32[]{:S(2)}) async-start(bf16[8,3,192,256]{3,2,1,0:T(8,128)(2,1)} %copy-done.2), calls=%async_computation | async-start | bytes 4718592 | tf_op jit(solution)/shard_map/all_to_all | solution.py:411
  13.4 2.0 collective-permute-start.1
  15.5 1.5 collective-permute-start.6
  16.9 1.8 constant_dynamic-slice_fusion
  18.7 2.4 collective-permute-start
  21.9 46.9 %all-to-all-done.q_ref.k_ref.v_ref = bf16[8,3,192,256]{3,2,1,0:T(8,128)(2,1)S(1)} async-done(((bf16[8,3,192,256]{3,2,1,0:T(8,128)(2,1)}), bf16[8,3,192,256]{3,2,1,0:T(8,128)(2,1)S(1)}, u32[]{:S(2)}, u32[]{:S(2)}) %all-to-all-start) | async-done | bytes 2359328 | tf_op jit(solution)/shard_map/all_to_all | solution.py:411
  68.9 15.9 %attention_forward.1 = (bf16[768,256]{1,0:T(8,128)(2,1)S(1)}, bf16[768,256]{1,0:T(8,128)(2,1)}, bf16[1536,256]{1,0:T(8,128)(2,1)S(1)}) custom-call(s32[1]{0:T(128)} %bitcast.1.half_ref, bf16[8,3,192,256]{3,2,1,0:T(8,128)(2,1)S(1)} %all-to-all-done.q_ref.k_ref.v_ref, bf16[8,3,192,256]{3,2,1,0:T(8,128)(2,1)S(1)} %all-to-all-done.q_ref.k_ref.v_ref, ...), custom_call_target="tpu_custom_call" | custom-call | flops 2415919104 | bytes 3145728 | tf_op jit(solution)/shard_map/attention_forward/pallas_call | solution.py:132
  86.4 1.1 collective-permute-done.1.refs_2_.refs_4_
  87.6 1.5 collective-permute-start.7
  89.0 1.5 collective-permute-start.3
  91.0 2.1 collective-permute-start.5
  93.0 8.1 %collective-permute-done.3.refs_2_ = bf16[64,3072]{1,0:T(8,128)(2,1)S(1)} collective-permute-done((bf16[64,3072]{1,0:T(8,128)(2,1)}, bf16[64,3072]{1,0:T(8,128)(2,1)S(1)}, u32[]{:S(2)}, u32[]{:S(2)}) %collective-permute-start.3) | collective-permute-done | bytes 393248 | tf_op jit(solution)/shard_map/ppermute | solution.py:404
  101.2 7.7 %collective-permute-done.4.refs_3_ = bf16[64,3072]{1,0:T(8,128)(2,1)S(1)} collective-permute-done((bf16[64,3072]{1,0:T(8,128)(2,1)}, bf16[64,3072]{1,0:T(8,128)(2,1)S(1)}, u32[]{:S(2)}, u32[]{:S(2)}) %collective-permute-start.4) | collective-permute-done | bytes 393248 | tf_op jit(solution)/shard_map/ppermute | solution.py:404
  108.8 2.9 %collective-permute-done.5.a1_ref.refs_1_ = bf16[768,256]{1,0:T(8,128)(2,1)S(1)} collective-permute-done((bf16[768,256]{1,0:T(8,128)(2,1)}, bf16[768,256]{1,0:T(8,128)(2,1)S(1)}, u32[]{:S(2)}, u32[]{:S(2)}) %collective-permute-start.5) | collective-permute-done | bytes 393248 | tf_op jit(solution)/shard_map/ppermute | solution.py:394
  111.7 2.0 join_parts.2
  113.8 1.1 copy-done.12
  114.9 5.8 %output_partial.1 = (bf16[192,3072]{1,0:T(8,128)(2,1)S(1)}, bf16[192,3072]{1,0:T(8,128)(2,1)S(1)}, bf16[192,3072]{1,0:T(8,128)(2,1)S(1)}, bf16[192,3072]{1,0:T(8,128)(2,1)S(1)}) custom-call(s32[1]{0:T(128)} %bitcast.rank_ref, bf16[768,256]{1,0:T(8,128)(2,1)S(1)} %copy-done.7, bf16[768,256]{1,0:T(8,128)(2,1)S(1)} %collective-permute-done.5.a1_ref.refs_1_, ...), custom_call_target="tpu_custom_call" | custom-call | flops 2415919104 | bytes 7864320 | tf_op jit(solution)/shard_map/output_partial/pallas_call | solution.py:279
  120.8 1.0 copy-done.13
  122.4 7.2 %attention_grad.1 = (bf16[768,256]{1,0:T(8,128)(2,1)S(1)}, bf16[768,256]{1,0:T(8,128)(2,1)S(1)}) custom-call(s32[1]{0:T(128)} %bitcast.rank_ref, bf16[192,3072]{1,0:T(8,128)(2,1)S(1)} %bitcast.33, bf16[192,3072]{1,0:T(8,128)(2,1)} %collective-permute-done.6.refs_1_.refs_3_, bf16[192,3072]{1,0:T(8,128)(2,1)} %collective-permute-done.1.refs_2_.refs_4_, ...), custom_call_target="tpu_custom_call" | custom-call | flops 2415919104 | bytes 7864320 | tf_op jit(solution)/shard_map/attention_grad/pallas_call | solution.py:252
  129.7 7.9 %weight_grad_partial.1 = (bf16[2,2,64,3072]{3,2,1,0:T(8,128)(2,1)}, bf16[2,2,64,3072]{3,2,1,0:T(8,128)(2,1)}) custom-call(s32[1]{0:T(128)} %bitcast.rank_ref, s32[1]{0:T(128)} %bitcast.7.place_ref, bf16[768,256]{1,0:T(8,128)(2,1)S(1)} %copy-done.7, bf16[768,256]{1,0:T(8,128)(2,1)S(1)} %collective-permute-done.5.a1_ref.refs_1_, ...), custom_call_target="tpu_custom_call" | custom-call | flops 2415919104 | bytes 7864320 | tf_op jit(solution)/shard_map/weight_grad_partial/pallas_call | solution.py:323
  137.6 11.5 %collective-permute-done.9 = bf16[192,3072]{1,0:T(8,128)(2,1)S(1)} collective-permute-done((bf16[192,3072]{1,0:T(8,128)(2,1)S(1)}, bf16[192,3072]{1,0:T(8,128)(2,1)S(1)}, u32[]{:S(2)}, u32[]{:S(2)}) %collective-permute-start.9) | collective-permute-done | bytes 1179680 | tf_op jit(solution)/shard_map/ppermute | solution.py:394
  149.6 1.1 collective-permute-start.10
  151.1 2.0 collective-permute-done.12
  153.6 1.7 copy-done.19
  155.2 1.0 slice.34
  156.2 1.5 collective-permute-start.13
  157.7 9.9 %attention_backward.2 = bf16[8,3,192,128]{3,2,1,0:T(8,128)(2,1)} custom-call(s32[1]{0:T(128)} %bitcast.1.half_ref, bf16[8,3,192,256]{3,2,1,0:T(8,128)(2,1)} %copy-done.1, bf16[8,3,192,256]{3,2,1,0:T(8,128)(2,1)} %copy-done.1, bf16[8,3,192,256]{3,2,1,0:T(8,128)(2,1)} %copy-done.1, bf16[2,1536,128]{2,1,0:T(8,128)(2,1)S(1)} %bitcast.24, ...), custom_call_target="tpu_custom_call" | custom-call | flops 3019898880 | bytes 2752512 | tf_op jit(solution)/shard_map/attention_backward/pallas_call | solution.py:215
  167.6 10.4 %collective-permute-done.10 = bf16[192,3072]{1,0:T(8,128)(2,1)S(1)} collective-permute-done((bf16[192,3072]{1,0:T(8,128)(2,1)S(1)}, bf16[192,3072]{1,0:T(8,128)(2,1)S(1)}, u32[]{:S(2)}, u32[]{:S(2)}) %collective-permute-start.10) | collective-permute-done | bytes 1179680 | tf_op jit(solution)/shard_map/ppermute | solution.py:394
  178.0 1.0 copy-done.22
  179.0 4.0 %all-to-all-start.1 = ((bf16[8,3,192,128]{3,2,1,0:T(8,128)(2,1)}), bf16[8,3,192,128]{3,2,1,0:T(8,128)(2,1)S(1)}, u32[]{:S(2)}, u32[]{:S(2)}) async-start(bf16[8,3,192,128]{3,2,1,0:T(8,128)(2,1)} %attention_backward.2), calls=%async_computation.1 | async-start | bytes 2359296 | tf_op jit(solution)/shard_map/all_to_all | solution.py:478
  183.0 1.8 slice_add_fusion
  186.1 2.9 %collective-permute-start.14 = (bf16[64,3072]{1,0:T(8,128)(2,1)}, bf16[64,3072]{1,0:T(8,128)(2,1)}, u32[]{:S(2)}, u32[]{:S(2)}) collective-permute-start(bf16[64,3072]{1,0:T(8,128)(2,1)} %fusion.3), channel_id=1, source_target_pairs={{0,4},{1,5},{2,6},{3,7},{4,0},{5,1},{6,2},{7,3},{8,12},{9,13},{10,... | collective-permute-start | bytes 1179656 | tf_op jit(solution)/shard_map/ppermute | solution.py:394
  189.0 8.9 %attention_backward.3 = bf16[8,3,192,128]{3,2,1,0:T(8,128)(2,1)S(1)} custom-call(s32[1]{0:T(128)} %bitcast.1.half_ref, bf16[8,3,192,256]{3,2,1,0:T(8,128)(2,1)} %copy-done.1, bf16[8,3,192,256]{3,2,1,0:T(8,128)(2,1)} %copy-done.1, bf16[8,3,192,256]{3,2,1,0:T(8,128)(2,1)} %copy-done.1, bf16[2,1536,128]{2,1,0:T(8,128)(2,1)S(1)} %bitcast.25, ...), custom_call_target="tpu_custom_call" | custom-call | flops 3019898880 | bytes 2752512 | tf_op jit(solution)/shard_map/attention_backward/pallas_call | solution.py:215
  197.9 1.1 copy-done.3
  199.0 22.4 %all-to-all-done.1.refs_0_ = bf16[8,3,192,128]{3,2,1,0:T(8,128)(2,1)S(1)} async-done(((bf16[8,3,192,128]{3,2,1,0:T(8,128)(2,1)}), bf16[8,3,192,128]{3,2,1,0:T(8,128)(2,1)S(1)}, u32[]{:S(2)}, u32[]{:S(2)}) %all-to-all-start.1) | async-done | bytes 1179680 | tf_op jit(solution)/shard_map/all_to_all | solution.py:478
  221.4 3.6 %all-to-all-start.2 = ((bf16[8,3,192,128]{3,2,1,0:T(8,128)(2,1)}), bf16[8,3,192,128]{3,2,1,0:T(8,128)(2,1)S(1)}, u32[]{:S(2)}, u32[]{:S(2)}) async-start(bf16[8,3,192,128]{3,2,1,0:T(8,128)(2,1)} %copy-done.3), calls=%async_computation.2 | async-start | bytes 2359296 | tf_op jit(solution)/shard_map/all_to_all | solution.py:478
  225.0 6.1 %collective-permute-done.14 = bf16[64,3072]{1,0:T(8,128)(2,1)} collective-permute-done((bf16[64,3072]{1,0:T(8,128)(2,1)}, bf16[64,3072]{1,0:T(8,128)(2,1)}, u32[]{:S(2)}, u32[]{:S(2)}) %collective-permute-start.14) | collective-permute-done | bytes 393248 | tf_op jit(solution)/shard_map/ppermute | solution.py:394
  231.1 1.3 fusion.2.refs_0_
  232.4 1.5 collective-permute-start.16
  233.9 6.3 %collective-permute-done.16.refs_2_ = bf16[64,3072]{1,0:T(8,128)(2,1)S(1)} collective-permute-done((bf16[64,3072]{1,0:T(8,128)(2,1)S(1)}, bf16[64,3072]{1,0:T(8,128)(2,1)S(1)}, u32[]{:S(2)}, u32[]{:S(2)}) %collective-permute-start.16) | collective-permute-done | bytes 393248 | tf_op jit(solution)/shard_map/ppermute | solution.py:404
  240.2 3.2 %fusion = bf16[1,192,3072]{2,1,0:T(8,128)(2,1)} fusion(bf16[192,3072]{1,0:T(8,128)(2,1)} %collective-permute-done.11, bf16[192,3072]{1,0:T(8,128)(2,1)} %copy-done.22, bf16[192,3072]{1,0:T(8,128)(2,1)S(1)} %copy-done.14), kind=kLoop, calls=%fused_computation.5 | loop fusion | flops 3538944 | bytes 4718592 | tf_op jit(solution)/shard_map/broadcast_in_dim | solution.py:484
  243.4 2.2 join_parts.3
  245.6 7.8 %all-to-all-done.2.refs_1_ = bf16[8,3,192,128]{3,2,1,0:T(8,128)(2,1)S(1)} async-done(((bf16[8,3,192,128]{3,2,1,0:T(8,128)(2,1)}), bf16[8,3,192,128]{3,2,1,0:T(8,128)(2,1)S(1)}, u32[]{:S(2)}, u32[]{:S(2)}) %all-to-all-start.2) | async-done | bytes 1179680 | tf_op jit(solution)/shard_map/all_to_all | solution.py:478
  253.4 3.1 %unpack_heads.1 = (bf16[192,2048]{1,0:T(8,128)(2,1)}, bf16[192,2048]{1,0:T(8,128)(2,1)}, bf16[192,2048]{1,0:T(8,128)(2,1)}) custom-call(bf16[8,3,192,128]{3,2,1,0:T(8,128)(2,1)S(1)} %all-to-all-done.1.refs_0_, bf16[8,3,192,128]{3,2,1,0:T(8,128)(2,1)S(1)} %all-to-all-done.2.refs_1_), custom_call_target="tpu_custom_call" | custom-call | bytes 4718592 | tf_op jit(solution)/shard_map/unpack_heads/pallas_call | solution.py:66
  (68 shorter events, 7.0 us)
Async XLA Ops:
  0.6 21.1 %copy-start = (s32[16,24,16]{1,2,0:T(8,128)S(1)}, s32[16,24,16]{1,2,0:T(8,128)}, u32[]{:S(2)}) copy-start(s32[16,24,16]{1,2,0:T(8,128)} %param.12) | copy-start | bytes 73732
  0.6 1.2 copy-start.15
  1.8 1.1 copy-start.16
  3.0 1.1 copy-start.17
  4.8 1.4 copy-start.2
  6.2 62.7 %all-to-all-start = ((bf16[8,3,192,256]{3,2,1,0:T(8,128)(2,1)}), bf16[8,3,192,256]{3,2,1,0:T(8,128)(2,1)S(1)}, u32[]{:S(2)}, u32[]{:S(2)}) async-start(bf16[8,3,192,256]{3,2,1,0:T(8,128)(2,1)} %copy-done.2), calls=%async_computation | async-start | bytes 4718592 | tf_op jit(solution)/shard_map/all_to_all | solution.py:411
  13.4 74.1 %collective-permute-start.1 = (bf16[192,3072]{1,0:T(8,128)(2,1)}, bf16[192,3072]{1,0:T(8,128)(2,1)}, u32[]{:S(2)}, u32[]{:S(2)}) collective-permute-start(bf16[192,3072]{1,0:T(8,128)(2,1)} %bitcast.31), channel_id=1, source_target_pairs={{0,2},{1,3},{2,0},{3,1},{4,6},{5,7},{6,4},{7,5},{8,10},{9,11},{10,... | collective-permute-start | bytes 3538952 | tf_op jit(solution)/shard_map/ppermute | solution.py:394
  15.5 106.4 %collective-permute-start.6 = (bf16[192,3072]{1,0:T(8,128)(2,1)}, bf16[192,3072]{1,0:T(8,128)(2,1)}, u32[]{:S(2)}, u32[]{:S(2)}) collective-permute-start(bf16[192,3072]{1,0:T(8,128)(2,1)} %bitcast.32), channel_id=1, source_target_pairs={{0,1},{1,0},{2,3},{3,2},{4,5},{5,4},{6,7},{7,6},{8,9},{9,8},{10,11... | collective-permute-start | bytes 3538952 | tf_op jit(solution)/shard_map/ppermute | solution.py:394
  18.7 67.7 %collective-permute-start = (bf16[64,3072]{1,0:T(8,128)(2,1)}, bf16[64,3072]{1,0:T(8,128)(2,1)}, u32[]{:S(2)}, u32[]{:S(2)}) collective-permute-start(bf16[64,3072]{1,0:T(8,128)(2,1)} %constant_dynamic-slice_fusion), channel_id=1, source_target_pairs={{0,4},{1,5},{2,6},{3,7},{4,0},{5,1},{6,2},{7,3},{8,12},{9,13},{10,... | collective-permute-start | bytes 1179656 | tf_op jit(solution)/shard_map/ppermute | solution.py:394
  68.8 16.0 %copy-start.1 = (bf16[8,3,192,256]{3,2,1,0:T(8,128)(2,1)}, bf16[8,3,192,256]{3,2,1,0:T(8,128)(2,1)S(1)}, u32[]{:S(2)}) copy-start(bf16[8,3,192,256]{3,2,1,0:T(8,128)(2,1)S(1)} %all-to-all-done.q_ref.k_ref.v_ref) | copy-start | bytes 7077892
  84.8 0.9 copy-start.4
  85.7 0.7 copy-start.6
  87.6 34.3 %collective-permute-start.7 = (bf16[192,3072]{1,0:T(8,128)(2,1)}, bf16[192,3072]{1,0:T(8,128)(2,1)}, u32[]{:S(2)}, u32[]{:S(2)}) collective-permute-start(bf16[192,3072]{1,0:T(8,128)(2,1)} %collective-permute-done.1.refs_2_.refs_4_), channel_id=1, source_target_pairs={{0,1},{1,0},{2,3},{3,2},{4,5},{5,4},{6,7},{7,6},{8,9},{9,8},{10,11... | collective-permute-start | bytes 3538952 | tf_op jit(solution)/shard_map/ppermute | solution.py:394
  89.0 1.9 collective-permute-start.2
  89.0 12.1 %collective-permute-start.3 = (bf16[64,3072]{1,0:T(8,128)(2,1)}, bf16[64,3072]{1,0:T(8,128)(2,1)S(1)}, u32[]{:S(2)}, u32[]{:S(2)}) collective-permute-start(bf16[64,3072]{1,0:T(8,128)(2,1)} %collective-permute-done.refs_0_), channel_id=1, source_target_pairs={{0,16},{8,24},{16,0},{24,8},{1,17},{9,25},{17,1},{25,9},{2,18},{10... | collective-permute-start | bytes 1179656 | tf_op jit(solution)/shard_map/ppermute | solution.py:404
  90.5 18.3 %collective-permute-start.4 = (bf16[64,3072]{1,0:T(8,128)(2,1)}, bf16[64,3072]{1,0:T(8,128)(2,1)S(1)}, u32[]{:S(2)}, u32[]{:S(2)}) collective-permute-start(bf16[64,3072]{1,0:T(8,128)(2,1)} %collective-permute-done.refs_0_), channel_id=1, source_target_pairs={{0,24},{8,16},{16,8},{24,0},{1,25},{9,17},{17,9},{25,1},{2,26},{10... | collective-permute-start | bytes 1179656 | tf_op jit(solution)/shard_map/ppermute | solution.py:404
  91.0 20.8 %collective-permute-start.5 = (bf16[768,256]{1,0:T(8,128)(2,1)}, bf16[768,256]{1,0:T(8,128)(2,1)S(1)}, u32[]{:S(2)}, u32[]{:S(2)}) collective-permute-start(bf16[768,256]{1,0:T(8,128)(2,1)} %get-tuple-element.50.refs_1_), channel_id=1, source_target_pairs={{0,4},{1,5},{2,6},{3,7},{4,0},{5,1},{6,2},{7,3},{8,12},{9,13},{10,... | collective-permute-start | bytes 1179656 | tf_op jit(solution)/shard_map/ppermute | solution.py:394
  111.7 3.2 %copy-start.7 = (bf16[768,256]{1,0:T(8,128)(2,1)S(1)}, bf16[768,256]{1,0:T(8,128)(2,1)}, u32[]{:S(2)}) copy-start(bf16[768,256]{1,0:T(8,128)(2,1)} %copy-done.6) | copy-start | bytes 1179652
  113.8 1.1 copy-start.12
  114.9 7.5 %copy-start.18 = (bf16[1,192,3072]{2,1,0:T(8,128)(2,1)S(1)}, bf16[1,192,3072]{2,1,0:T(8,128)(2,1)}, u32[]{:S(2)}) copy-start(bf16[1,192,3072]{2,1,0:T(8,128)(2,1)} %param.11) | copy-start | bytes 3538948
  120.8 1.1 copy-start.13
  121.8 27.3 %collective-permute-start.9 = (bf16[192,3072]{1,0:T(8,128)(2,1)S(1)}, bf16[192,3072]{1,0:T(8,128)(2,1)S(1)}, u32[]{:S(2)}, u32[]{:S(2)}) collective-permute-start(bf16[192,3072]{1,0:T(8,128)(2,1)S(1)} %get-tuple-element.72), channel_id=1, source_target_pairs={{0,1},{1,0},{2,3},{3,2},{4,5},{5,4},{6,7},{7,6},{8,9},{9,8},{10,11... | collective-permute-start | bytes 3538952 | tf_op jit(solution)/shard_map/ppermute | solution.py:394
  129.6 28.1 %copy-start.8 = (bf16[768,256]{1,0:T(8,128)(2,1)}, bf16[768,256]{1,0:T(8,128)(2,1)S(1)}, u32[]{:S(2)}) copy-start(bf16[768,256]{1,0:T(8,128)(2,1)S(1)} %get-tuple-element.84.refs_2_) | copy-start | bytes 1179652
  129.6 19.9 %collective-permute-start.8 = (bf16[768,256]{1,0:T(8,128)(2,1)S(1)}, bf16[768,256]{1,0:T(8,128)(2,1)S(1)}, u32[]{:S(2)}, u32[]{:S(2)}) collective-permute-start(bf16[768,256]{1,0:T(8,128)(2,1)S(1)} %get-tuple-element.65), channel_id=1, source_target_pairs={{0,4},{1,5},{2,6},{3,7},{4,0},{5,1},{6,2},{7,3},{8,12},{9,13},{10,... | collective-permute-start | bytes 1179656 | tf_op jit(solution)/shard_map/ppermute | solution.py:394
  137.6 11.9 %copy-start.23 = (bf16[2,2,64,3072]{3,2,1,0:T(8,128)(2,1)S(1)}, bf16[2,2,64,3072]{3,2,1,0:T(8,128)(2,1)}, u32[]{:S(2)}) copy-start(bf16[2,2,64,3072]{3,2,1,0:T(8,128)(2,1)} %get-tuple-element.83) | copy-start | bytes 4718596
  137.6 15.4 %copy-start.21 = (bf16[2,2,64,3072]{3,2,1,0:T(8,128)(2,1)S(1)}, bf16[2,2,64,3072]{3,2,1,0:T(8,128)(2,1)}, u32[]{:S(2)}) copy-start(bf16[2,2,64,3072]{3,2,1,0:T(8,128)(2,1)} %get-tuple-element.82) | copy-start | bytes 4718596
  149.5 8.2 %copy-start.10 = (bf16[768,256]{1,0:T(8,128)(2,1)}, bf16[768,256]{1,0:T(8,128)(2,1)S(1)}, u32[]{:S(2)}) copy-start(bf16[768,256]{1,0:T(8,128)(2,1)S(1)} %collective-permute-done.8.refs_3_) | copy-start | bytes 1179652
  149.5 3.5 %collective-permute-start.12 = (bf16[2,2,64,3072]{3,2,1,0:T(8,128)(2,1)S(1)}, bf16[2,2,64,3072]{3,2,1,0:T(8,128)(2,1)S(1)}, u32[]{:S(2)}, u32[]{:S(2)}) collective-permute-start(bf16[2,2,64,3072]{3,2,1,0:T(8,128)(2,1)S(1)} %copy-done.23), channel_id=1, source_target_pairs={{0,8},{8,0},{16,24},{24,16},{1,9},{9,1},{17,25},{25,17},{2,10},{10... | collective-permute-start | bytes 4718600 | tf_op jit(solution)/shard_map/ppermute | solution.py:404
  149.6 28.4 %collective-permute-start.10 = (bf16[192,3072]{1,0:T(8,128)(2,1)S(1)}, bf16[192,3072]{1,0:T(8,128)(2,1)S(1)}, u32[]{:S(2)}, u32[]{:S(2)}) collective-permute-start(bf16[192,3072]{1,0:T(8,128)(2,1)S(1)} %get-tuple-element.77), channel_id=1, source_target_pairs={{0,1},{1,0},{2,3},{3,2},{4,5},{5,4},{6,7},{7,6},{8,9},{9,8},{10,11... | collective-permute-start | bytes 3538952 | tf_op jit(solution)/shard_map/ppermute | solution.py:394
  150.7 28.3 %collective-permute-start.11 = (bf16[192,3072]{1,0:T(8,128)(2,1)S(1)}, bf16[192,3072]{1,0:T(8,128)(2,1)}, u32[]{:S(2)}, u32[]{:S(2)}) collective-permute-start(bf16[192,3072]{1,0:T(8,128)(2,1)S(1)} %add_convert_fusion.1), channel_id=1, source_target_pairs={{0,2},{1,3},{2,0},{3,1},{4,6},{5,7},{6,4},{7,5},{8,10},{9,11},{10,... | collective-permute-start | bytes 3538952 | tf_op jit(solution)/shard_map/ppermute | solution.py:394
  153.5 1.7 copy-start.19
  155.2 2.5 copy-start.5
  156.2 26.8 %collective-permute-start.13 = (bf16[1,2,64,3072]{3,2,1,0:T(8,128)(2,1)}, bf16[1,2,64,3072]{3,2,1,0:T(8,128)(2,1)}, u32[]{:S(2)}, u32[]{:S(2)}) collective-permute-start(bf16[1,2,64,3072]{3,2,1,0:T(8,128)(2,1)} %slice.34), channel_id=1, source_target_pairs={{0,16},{8,24},{16,0},{24,8},{1,17},{9,25},{17,1},{25,9},{2,18},{10... | collective-permute-start | bytes 2359304 | tf_op jit(solution)/shard_map/ppermute | solution.py:404
  178.0 1.0 copy-start.22
  179.0 42.4 %all-to-all-start.1 = ((bf16[8,3,192,128]{3,2,1,0:T(8,128)(2,1)}), bf16[8,3,192,128]{3,2,1,0:T(8,128)(2,1)S(1)}, u32[]{:S(2)}, u32[]{:S(2)}) async-start(bf16[8,3,192,128]{3,2,1,0:T(8,128)(2,1)} %attention_backward.2), calls=%async_computation.1 | async-start | bytes 2359296 | tf_op jit(solution)/shard_map/all_to_all | solution.py:478
  183.0 6.1 %copy-start.9 = (bf16[768,256]{1,0:T(8,128)(2,1)S(1)}, bf16[768,256]{1,0:T(8,128)(2,1)}, u32[]{:S(2)}) copy-start(bf16[768,256]{1,0:T(8,128)(2,1)} %copy-done.8) | copy-start | bytes 1179652
  183.0 6.1 %copy-start.11 = (bf16[768,256]{1,0:T(8,128)(2,1)S(1)}, bf16[768,256]{1,0:T(8,128)(2,1)}, u32[]{:S(2)}) copy-start(bf16[768,256]{1,0:T(8,128)(2,1)} %copy-done.10) | copy-start | bytes 1179652
  184.9 1.3 copy-start.20
  186.1 44.9 %collective-permute-start.14 = (bf16[64,3072]{1,0:T(8,128)(2,1)}, bf16[64,3072]{1,0:T(8,128)(2,1)}, u32[]{:S(2)}, u32[]{:S(2)}) collective-permute-start(bf16[64,3072]{1,0:T(8,128)(2,1)} %fusion.3), channel_id=1, source_target_pairs={{0,4},{1,5},{2,6},{3,7},{4,0},{5,1},{6,2},{7,3},{8,12},{9,13},{10,... | collective-permute-start | bytes 1179656 | tf_op jit(solution)/shard_map/ppermute | solution.py:394
  197.9 1.1 copy-start.3
  221.4 32.0 %all-to-all-start.2 = ((bf16[8,3,192,128]{3,2,1,0:T(8,128)(2,1)}), bf16[8,3,192,128]{3,2,1,0:T(8,128)(2,1)S(1)}, u32[]{:S(2)}, u32[]{:S(2)}) async-start(bf16[8,3,192,128]{3,2,1,0:T(8,128)(2,1)} %copy-done.3), calls=%async_computation.2 | async-start | bytes 2359296 | tf_op jit(solution)/shard_map/all_to_all | solution.py:478
  225.0 15.2 %copy-start.14 = (bf16[192,3072]{1,0:T(8,128)(2,1)S(1)}, bf16[192,3072]{1,0:T(8,128)(2,1)}, u32[]{:S(2)}) copy-start(bf16[192,3072]{1,0:T(8,128)(2,1)} %copy-done.13) | copy-start | bytes 3538948
  232.4 7.8 %collective-permute-start.16 = (bf16[64,3072]{1,0:T(8,128)(2,1)S(1)}, bf16[64,3072]{1,0:T(8,128)(2,1)S(1)}, u32[]{:S(2)}, u32[]{:S(2)}) collective-permute-start(bf16[64,3072]{1,0:T(8,128)(2,1)S(1)} %fusion.2.refs_0_), channel_id=1, source_target_pairs={{0,16},{8,24},{16,0},{24,8},{1,17},{9,25},{17,1},{25,9},{2,18},{10... | collective-permute-start | bytes 1179656 | tf_op jit(solution)/shard_map/ppermute | solution.py:404
  233.9 9.5 %collective-permute-start.15 = (bf16[64,3072]{1,0:T(8,128)(2,1)S(1)}, bf16[64,3072]{1,0:T(8,128)(2,1)S(1)}, u32[]{:S(2)}, u32[]{:S(2)}) collective-permute-start(bf16[64,3072]{1,0:T(8,128)(2,1)S(1)} %fusion.2.refs_0_), channel_id=1, source_target_pairs={{0,8},{8,0},{16,24},{24,16},{1,9},{9,1},{17,25},{25,17},{2,10},{10... | collective-permute-start | bytes 1179656 | tf_op jit(solution)/shard_map/ppermute | solution.py:404
  240.2 3.2 %collective-permute-start.17 = (bf16[64,3072]{1,0:T(8,128)(2,1)S(1)}, bf16[64,3072]{1,0:T(8,128)(2,1)S(1)}, u32[]{:S(2)}, u32[]{:S(2)}) collective-permute-start(bf16[64,3072]{1,0:T(8,128)(2,1)S(1)} %collective-permute-done.16.refs_2_), channel_id=1, source_target_pairs={{0,8},{8,0},{16,24},{24,16},{1,9},{9,1},{17,25},{25,17},{2,10},{10... | collective-permute-start | bytes 1179656 | tf_op jit(solution)/shard_map/ppermute | solution.py:404

commit v4 on v3

--- a/solution.py
+++ b/solution.py
@@ -111,12 +111,17 @@
         tile = lax.broadcasted_iota(jnp.int32, shape, 0) // TILE + i * tiles
         ones = jnp.where(tile == lax.broadcasted_iota(jnp.int32, shape, 1), F32(1), F32(0))
         q = jnp.concatenate([q_ref[...].reshape(shape), ones.astype(BF16)], axis=1)
-        s = dot_nt(q, wide_ref[...])
-        top = jnp.max(s, axis=1, keepdims=True)
-        e = jnp.exp2((s - top) * EXP2_SCALE)
-        total = jnp.sum(e, axis=1, keepdims=True)
-        attn = dot_nn(e.astype(BF16), v_ref[...].reshape(tokens, HDIM)) * (1.0 / total)
-        attn = attn.astype(BF16)
+        v = v_ref[...].reshape(tokens, HDIM)
+        sub = q_rows // 2
+        starts = range(0, q_rows, sub)
+        scores = [dot_nt(q[at : at + sub], wide_ref[...]) for at in starts]
+        tops = [jnp.max(s, axis=1, keepdims=True) for s in scores]
+        exps = [jnp.exp2((s - top) * EXP2_SCALE) for s, top in zip(scores, tops)]
+        totals = [jnp.sum(e, axis=1, keepdims=True) for e in exps]
+        attn = [dot_nn(e.astype(BF16), v) * (1.0 / t) for e, t in zip(exps, totals)]
+        attn = jnp.concatenate(attn, axis=0).astype(BF16)
+        top = jnp.concatenate(tops, axis=0)
+        total = jnp.concatenate(totals, axis=0)
         log_sum = top + jnp.log2(total) * (1.0 / EXP2_SCALE)
         extra_ref[...] = put_columns(ones, split3(log_sum)).astype(BF16)
         own = (i // half_steps) == half_ref[0]
@@ -164,8 +169,8 @@
 def attention_backward(packed, mask, half, extra, attn_own, attn_send, grad_own, grad_mirror, head):
     n, _, rows, cols = packed.shape
     tokens = n * rows
-    q_rows = 2 * rows
-    steps = n // 2
+    q_rows = 4 * rows
+    steps = n // 4
     half_steps = steps // 2
 
     def body(half_ref, q_ref, k_ref, v_ref, mask_ref, extra_ref, *refs):
@@ -193,7 +198,7 @@
         probs = jnp.exp2(dot_nt(wide_q, wide_ref[...]) * EXP2_SCALE)
         grad_scores = (probs * dot_nt(wide_grad, wide_v_ref[...])).astype(BF16)
         grad_q = dot_nn(grad_scores, wide_ref[:, :HDIM]) * SCALE
-        out_ref[pl.ds(2 * i, 2), 0] = grad_q.astype(BF16).reshape(2, rows, HDIM)
+        out_ref[pl.ds(4 * i, 4), 0] = grad_q.astype(BF16).reshape(4, rows, HDIM)
         dk_t = dot_nn(q.T, grad_scores)
         dv_t = dot_nn(grad.T, probs.astype(BF16))
 
@@ -219,7 +224,7 @@
             num_scalar_prefetch=1,
             grid=(steps,),
             in_specs=[
-                pl.BlockSpec((2, 1, rows, HDIM), lambda i, r: (i, 0, 0, head)),
+                pl.BlockSpec((4, 1, rows, HDIM), lambda i, r: (i, 0, 0, head)),
                 pl.BlockSpec((n, 1, rows, HDIM), lambda i, r: (0, 1, 0, head)),
                 pl.BlockSpec((n, 1, rows, HDIM), lambda i, r: (0, 2, 0, head)),
                 pl.BlockSpec((1, tokens, HDIM), lambda i, r: (head, 0, 0)),
@@ -306,13 +311,11 @@
         @pl.when(pl.program_id(0) == 0)
         def _():
             for j in range(m):
-                start = pl.multiple_of((rank_ref[0] ^ j) * rows, rows)
-                at_ref[j, :cols] = a0_ref[pl.ds(start, rows), :].T
-                at_ref[j, cols:] = a1_ref[pl.ds(start, rows), :].T
-
-        total = dot_nn(at_ref[0], cots[0][...])
-        for j in range(1, m):
-            total += dot_nn(at_ref[j], cots[j][...])
+                at = pl.ds(pl.multiple_of((rank_ref[0] ^ j) * rows, rows), rows)
+                at_ref[:cols, j * rows : (j + 1) * rows] = a0_ref[at, :].T
+                at_ref[cols:, j * rows : (j + 1) * rows] = a1_ref[at, :].T
+
+        total = dot_nn(at_ref[...], jnp.concatenate([c[...] for c in cots], axis=0))
         sum_ref[...] = total.astype(BF16).reshape(2 * parts, piece, step)
         for j in range(parts):
             out_ref = send_ref if j % 2 else keep_ref
@@ -330,7 +333,7 @@
             + [pl.BlockSpec((rows, step), lambda i, r, p: (0, i))] * m,
             out_specs=[pl.BlockSpec(shape[:3] + (step,), lambda i, r, p: (0, 0, 0, i))] * 2,
             scratch_shapes=[
-                pltpu.VMEM((m, 2 * cols, rows), BF16),
+                pltpu.VMEM((2 * cols, m * rows), BF16),
                 pltpu.VMEM((2 * parts, piece, step), BF16),
             ],
         ),

time: 257 us -> 257 us (level)
  Pallas kernels: 63.6 us -> 56.6 us
  waiting for transfers between devices: 133 us -> 140 us
    ppermute x10, waiting for transfers between devices: 32 us -> 37.7 us  [shards(): lax.ppermute(x, 'seq', [(i, i ^ bit) for i in range(n)])]
    pallas_call x1, Pallas kernels: 15.9 us -> 11.8 us  [attention_forward(): pl.pallas_call(body, out_shape=[jax.ShapeDtypeStruct((tokens // 2, cols),...]
  transfers between devices with their start and end apart: 21 -> 21, of which waited for: 13 -> 14; matrix products, arithmetic and copies ran while one was open for 5% -> 5% of each run, Pallas kernels for 23% -> 21%
where the time goes in v4:
time: 257 us
  waiting for transfers between devices  140 us (54%)
  Pallas kernels  56.6 us (22%)
  starting transfers between devices  34.1 us (13%)
  local copies, waits for them, and re-layouts  17.2 us (7%)
  other arithmetic  7.42 us (3%)
    all_to_all x1, waiting for transfers between devices, shards(): lax.all_to_all(packed, 'seq', split_axis=0, concat_axis=0, tiled=True)  46.9 us
    ppermute x10, waiting for transfers between devices, shards(): lax.ppermute(x, 'seq', [(i, i ^ bit) for i in range(n)])  37.7 us
    all_to_all x2, waiting for transfers between devices, shards(): lax.all_to_all(x, 'seq', split_axis=0, concat_axis=0, tiled=True)  31.5 us
    ppermute x8, waiting for transfers between devices, shards(): lax.ppermute(x, 'dp', [(i, i ^ bit) for i in range(dp)])  24.1 us
    pallas_call x2, Pallas kernels, attention_backward(): pl.pallas_call(body, out_shape=jax.ShapeDtypeStruct((n, 3, rows, HDIM), B...  16.2 us
    ppermute x10, starting transfers between devices, shards(): lax.ppermute(x, 'seq', [(i, i ^ bit) for i in range(n)])  14.4 us
    unnamed x48, local copies, waits for them, and re-layouts  12.8 us
    pallas_call x1, Pallas kernels, attention_forward(): pl.pallas_call(body, out_shape=[jax.ShapeDtypeStruct((tokens // 2, cols),...  11.8 us
  transfers between devices with their start and end apart: 21, of which 14 were waited for; matrix products, arithmetic and copies ran while one was open for 5% of the time, Pallas kernels for 21%

profile of v4, /device:TPU:0, one launch (start us, length us, event | category | flops | bytes accessed | tf_op | source)
XLA Modules:
  0.0 256.5 jit_solution(5195461420110946360)
XLA Ops:
  0.7 1.2 copy-done.15
  1.8 1.1 copy-done.16
  3.0 1.1 copy-done.17
  4.8 1.4 copy-done.2
  6.2 7.3 %all-to-all-start = ((bf16[8,3,192,256]{3,2,1,0:T(8,128)(2,1)}), bf16[8,3,192,256]{3,2,1,0:T(8,128)(2,1)S(1)}, u32[]{:S(2)}, u32[]{:S(2)}) async-start(bf16[8,3,192,256]{3,2,1,0:T(8,128)(2,1)} %copy-done.2), calls=%async_computation | async-start | bytes 4718592 | tf_op jit(solution)/shard_map/all_to_all | solution.py:414
  13.4 2.0 collective-permute-start.1
  15.5 1.5 collective-permute-start.6
  16.9 1.8 constant_dynamic-slice_fusion
  18.7 2.4 collective-permute-start
  21.9 46.9 %all-to-all-done.q_ref.k_ref.v_ref = bf16[8,3,192,256]{3,2,1,0:T(8,128)(2,1)S(1)} async-done(((bf16[8,3,192,256]{3,2,1,0:T(8,128)(2,1)}), bf16[8,3,192,256]{3,2,1,0:T(8,128)(2,1)S(1)}, u32[]{:S(2)}, u32[]{:S(2)}) %all-to-all-start) | async-done | bytes 2359328 | tf_op jit(solution)/shard_map/all_to_all | solution.py:414
  68.9 11.8 %attention_forward.1 = (bf16[768,256]{1,0:T(8,128)(2,1)S(1)}, bf16[768,256]{1,0:T(8,128)(2,1)}, bf16[1536,256]{1,0:T(8,128)(2,1)S(1)}) custom-call(s32[1]{0:T(128)} %bitcast.1.half_ref, bf16[8,3,192,256]{3,2,1,0:T(8,128)(2,1)S(1)} %all-to-all-done.q_ref.k_ref.v_ref, bf16[8,3,192,256]{3,2,1,0:T(8,128)(2,1)S(1)} %all-to-all-done.q_ref.k_ref.v_ref, ...), custom_call_target="tpu_custom_call" | custom-call | flops 2415919104 | bytes 3145728 | tf_op jit(solution)/shard_map/attention_forward/pallas_call | solution.py:137
  82.4 4.1 %collective-permute-done.refs_0_ = bf16[64,3072]{1,0:T(8,128)(2,1)} collective-permute-done((bf16[64,3072]{1,0:T(8,128)(2,1)}, bf16[64,3072]{1,0:T(8,128)(2,1)}, u32[]{:S(2)}, u32[]{:S(2)}) %collective-permute-start) | collective-permute-done | bytes 393248 | tf_op jit(solution)/shard_map/ppermute | solution.py:397
  86.4 1.1 collective-permute-done.1.refs_2_.refs_4_
  87.6 1.5 collective-permute-start.7
  89.0 1.5 collective-permute-start.3
  91.0 2.1 collective-permute-start.5
  93.0 8.1 %collective-permute-done.3.refs_2_ = bf16[64,3072]{1,0:T(8,128)(2,1)S(1)} collective-permute-done((bf16[64,3072]{1,0:T(8,128)(2,1)}, bf16[64,3072]{1,0:T(8,128)(2,1)S(1)}, u32[]{:S(2)}, u32[]{:S(2)}) %collective-permute-start.3) | collective-permute-done | bytes 393248 | tf_op jit(solution)/shard_map/ppermute | solution.py:407
  101.2 7.7 %collective-permute-done.4.refs_3_ = bf16[64,3072]{1,0:T(8,128)(2,1)S(1)} collective-permute-done((bf16[64,3072]{1,0:T(8,128)(2,1)}, bf16[64,3072]{1,0:T(8,128)(2,1)S(1)}, u32[]{:S(2)}, u32[]{:S(2)}) %collective-permute-start.4) | collective-permute-done | bytes 393248 | tf_op jit(solution)/shard_map/ppermute | solution.py:407
  108.8 2.9 %collective-permute-done.5.a1_ref.refs_1_ = bf16[768,256]{1,0:T(8,128)(2,1)S(1)} collective-permute-done((bf16[768,256]{1,0:T(8,128)(2,1)}, bf16[768,256]{1,0:T(8,128)(2,1)S(1)}, u32[]{:S(2)}, u32[]{:S(2)}) %collective-permute-start.5) | collective-permute-done | bytes 393248 | tf_op jit(solution)/shard_map/ppermute | solution.py:397
  111.7 2.0 join_parts.2
  113.8 1.1 copy-done.12
  114.9 5.8 %output_partial.1 = (bf16[192,3072]{1,0:T(8,128)(2,1)S(1)}, bf16[192,3072]{1,0:T(8,128)(2,1)S(1)}, bf16[192,3072]{1,0:T(8,128)(2,1)S(1)}, bf16[192,3072]{1,0:T(8,128)(2,1)S(1)}) custom-call(s32[1]{0:T(128)} %bitcast.rank_ref, bf16[768,256]{1,0:T(8,128)(2,1)S(1)} %copy-done.7, bf16[768,256]{1,0:T(8,128)(2,1)S(1)} %collective-permute-done.5.a1_ref.refs_1_, ...), custom_call_target="tpu_custom_call" | custom-call | flops 2415919104 | bytes 7864320 | tf_op jit(solution)/shard_map/output_partial/pallas_call | solution.py:284
  120.8 1.0 copy-done.13
  122.4 7.2 %attention_grad.1 = (bf16[768,256]{1,0:T(8,128)(2,1)S(1)}, bf16[768,256]{1,0:T(8,128)(2,1)S(1)}) custom-call(s32[1]{0:T(128)} %bitcast.rank_ref, bf16[192,3072]{1,0:T(8,128)(2,1)S(1)} %bitcast.33, bf16[192,3072]{1,0:T(8,128)(2,1)} %collective-permute-done.6.refs_1_.refs_3_, bf16[192,3072]{1,0:T(8,128)(2,1)} %collective-permute-done.1.refs_2_.refs_4_, ...), custom_call_target="tpu_custom_call" | custom-call | flops 2415919104 | bytes 7864320 | tf_op jit(solution)/shard_map/attention_grad/pallas_call | solution.py:257
  129.7 7.6 %weight_grad_partial.1 = (bf16[2,2,64,3072]{3,2,1,0:T(8,128)(2,1)}, bf16[2,2,64,3072]{3,2,1,0:T(8,128)(2,1)}) custom-call(s32[1]{0:T(128)} %bitcast.rank_ref, s32[1]{0:T(128)} %bitcast.7.place_ref, bf16[768,256]{1,0:T(8,128)(2,1)S(1)} %copy-done.7, bf16[768,256]{1,0:T(8,128)(2,1)S(1)} %collective-permute-done.5.a1_ref.refs_1_, ...), custom_call_target="tpu_custom_call" | custom-call | flops 2415919104 | bytes 7864320 | tf_op jit(solution)/shard_map/weight_grad_partial/pallas_call | solution.py:326
  137.3 11.8 %collective-permute-done.9 = bf16[192,3072]{1,0:T(8,128)(2,1)S(1)} collective-permute-done((bf16[192,3072]{1,0:T(8,128)(2,1)S(1)}, bf16[192,3072]{1,0:T(8,128)(2,1)S(1)}, u32[]{:S(2)}, u32[]{:S(2)}) %collective-permute-start.9) | collective-permute-done | bytes 1179680 | tf_op jit(solution)/shard_map/ppermute | solution.py:397
  149.6 1.1 collective-permute-start.10
  151.1 2.0 collective-permute-done.12
  153.6 1.7 copy-done.19
  156.2 1.5 collective-permute-start.13
  157.7 8.6 %attention_backward.2 = bf16[8,3,192,128]{3,2,1,0:T(8,128)(2,1)} custom-call(s32[1]{0:T(128)} %bitcast.1.half_ref, bf16[8,3,192,256]{3,2,1,0:T(8,128)(2,1)} %copy-done.1, bf16[8,3,192,256]{3,2,1,0:T(8,128)(2,1)} %copy-done.1, bf16[8,3,192,256]{3,2,1,0:T(8,128)(2,1)} %copy-done.1, bf16[2,1536,128]{2,1,0:T(8,128)(2,1)S(1)} %bitcast.24, ...), custom_call_target="tpu_custom_call" | custom-call | flops 3019898880 | bytes 2752512 | tf_op jit(solution)/shard_map/attention_backward/pallas_call | solution.py:220
  166.3 11.7 %collective-permute-done.10 = bf16[192,3072]{1,0:T(8,128)(2,1)S(1)} collective-permute-done((bf16[192,3072]{1,0:T(8,128)(2,1)S(1)}, bf16[192,3072]{1,0:T(8,128)(2,1)S(1)}, u32[]{:S(2)}, u32[]{:S(2)}) %collective-permute-start.10) | collective-permute-done | bytes 1179680 | tf_op jit(solution)/shard_map/ppermute | solution.py:397
  178.0 1.0 copy-done.22
  179.0 4.0 %all-to-all-start.1 = ((bf16[8,3,192,128]{3,2,1,0:T(8,128)(2,1)}), bf16[8,3,192,128]{3,2,1,0:T(8,128)(2,1)S(1)}, u32[]{:S(2)}, u32[]{:S(2)}) async-start(bf16[8,3,192,128]{3,2,1,0:T(8,128)(2,1)} %attention_backward.2), calls=%async_computation.1 | async-start | bytes 2359296 | tf_op jit(solution)/shard_map/all_to_all | solution.py:481
  183.0 1.8 slice_add_fusion
  186.1 2.9 %collective-permute-start.14 = (bf16[64,3072]{1,0:T(8,128)(2,1)}, bf16[64,3072]{1,0:T(8,128)(2,1)}, u32[]{:S(2)}, u32[]{:S(2)}) collective-permute-start(bf16[64,3072]{1,0:T(8,128)(2,1)} %fusion.3), channel_id=1, source_target_pairs={{0,4},{1,5},{2,6},{3,7},{4,0},{5,1},{6,2},{7,3},{8,12},{9,13},{10,... | collective-permute-start | bytes 1179656 | tf_op jit(solution)/shard_map/ppermute | solution.py:397
  189.0 7.6 %attention_backward.3 = bf16[8,3,192,128]{3,2,1,0:T(8,128)(2,1)S(1)} custom-call(s32[1]{0:T(128)} %bitcast.1.half_ref, bf16[8,3,192,256]{3,2,1,0:T(8,128)(2,1)} %copy-done.1, bf16[8,3,192,256]{3,2,1,0:T(8,128)(2,1)} %copy-done.1, bf16[8,3,192,256]{3,2,1,0:T(8,128)(2,1)} %copy-done.1, bf16[2,1536,128]{2,1,0:T(8,128)(2,1)S(1)} %bitcast.25, ...), custom_call_target="tpu_custom_call" | custom-call | flops 3019898880 | bytes 2752512 | tf_op jit(solution)/shard_map/attention_backward/pallas_call | solution.py:220
  196.7 1.1 copy-done.3
  197.7 23.7 %all-to-all-done.1.refs_0_ = bf16[8,3,192,128]{3,2,1,0:T(8,128)(2,1)S(1)} async-done(((bf16[8,3,192,128]{3,2,1,0:T(8,128)(2,1)}), bf16[8,3,192,128]{3,2,1,0:T(8,128)(2,1)S(1)}, u32[]{:S(2)}, u32[]{:S(2)}) %all-to-all-start.1) | async-done | bytes 1179680 | tf_op jit(solution)/shard_map/all_to_all | solution.py:481
  221.4 3.6 %all-to-all-start.2 = ((bf16[8,3,192,128]{3,2,1,0:T(8,128)(2,1)}), bf16[8,3,192,128]{3,2,1,0:T(8,128)(2,1)S(1)}, u32[]{:S(2)}, u32[]{:S(2)}) async-start(bf16[8,3,192,128]{3,2,1,0:T(8,128)(2,1)} %copy-done.3), calls=%async_computation.2 | async-start | bytes 2359296 | tf_op jit(solution)/shard_map/all_to_all | solution.py:481
  225.0 6.1 %collective-permute-done.14 = bf16[64,3072]{1,0:T(8,128)(2,1)} collective-permute-done((bf16[64,3072]{1,0:T(8,128)(2,1)}, bf16[64,3072]{1,0:T(8,128)(2,1)}, u32[]{:S(2)}, u32[]{:S(2)}) %collective-permute-start.14) | collective-permute-done | bytes 393248 | tf_op jit(solution)/shard_map/ppermute | solution.py:397
  231.1 1.3 fusion.2.refs_0_
  232.4 1.5 collective-permute-start.16
  233.9 6.3 %collective-permute-done.16.refs_2_ = bf16[64,3072]{1,0:T(8,128)(2,1)S(1)} collective-permute-done((bf16[64,3072]{1,0:T(8,128)(2,1)S(1)}, bf16[64,3072]{1,0:T(8,128)(2,1)S(1)}, u32[]{:S(2)}, u32[]{:S(2)}) %collective-permute-start.16) | collective-permute-done | bytes 393248 | tf_op jit(solution)/shard_map/ppermute | solution.py:407
  240.2 3.2 %fusion = bf16[1,192,3072]{2,1,0:T(8,128)(2,1)} fusion(bf16[192,3072]{1,0:T(8,128)(2,1)} %collective-permute-done.11, bf16[192,3072]{1,0:T(8,128)(2,1)} %copy-done.22, bf16[192,3072]{1,0:T(8,128)(2,1)S(1)} %copy-done.14), kind=kLoop, calls=%fused_computation.5 | loop fusion | flops 3538944 | bytes 4718592 | tf_op jit(solution)/shard_map/broadcast_in_dim | solution.py:487
  243.4 2.2 join_parts.3
  245.6 7.8 %all-to-all-done.2.refs_1_ = bf16[8,3,192,128]{3,2,1,0:T(8,128)(2,1)S(1)} async-done(((bf16[8,3,192,128]{3,2,1,0:T(8,128)(2,1)}), bf16[8,3,192,128]{3,2,1,0:T(8,128)(2,1)S(1)}, u32[]{:S(2)}, u32[]{:S(2)}) %all-to-all-start.2) | async-done | bytes 1179680 | tf_op jit(solution)/shard_map/all_to_all | solution.py:481
  253.4 3.1 %unpack_heads.1 = (bf16[192,2048]{1,0:T(8,128)(2,1)}, bf16[192,2048]{1,0:T(8,128)(2,1)}, bf16[192,2048]{1,0:T(8,128)(2,1)}) custom-call(bf16[8,3,192,128]{3,2,1,0:T(8,128)(2,1)S(1)} %all-to-all-done.1.refs_0_, bf16[8,3,192,128]{3,2,1,0:T(8,128)(2,1)S(1)} %all-to-all-done.2.refs_1_), custom_call_target="tpu_custom_call" | custom-call | bytes 4718592 | tf_op jit(solution)/shard_map/unpack_heads/pallas_call | solution.py:66
  (68 shorter events, 8.0 us)
Async XLA Ops:
  0.6 21.1 %copy-start = (s32[16,24,16]{1,2,0:T(8,128)S(1)}, s32[16,24,16]{1,2,0:T(8,128)}, u32[]{:S(2)}) copy-start(s32[16,24,16]{1,2,0:T(8,128)} %param.12) | copy-start | bytes 73732
  0.6 1.2 copy-start.15
  1.8 1.1 copy-start.16
  3.0 1.1 copy-start.17
  4.8 1.4 copy-start.2
  6.2 62.7 %all-to-all-start = ((bf16[8,3,192,256]{3,2,1,0:T(8,128)(2,1)}), bf16[8,3,192,256]{3,2,1,0:T(8,128)(2,1)S(1)}, u32[]{:S(2)}, u32[]{:S(2)}) async-start(bf16[8,3,192,256]{3,2,1,0:T(8,128)(2,1)} %copy-done.2), calls=%async_computation | async-start | bytes 4718592 | tf_op jit(solution)/shard_map/all_to_all | solution.py:414
  13.4 74.1 %collective-permute-start.1 = (bf16[192,3072]{1,0:T(8,128)(2,1)}, bf16[192,3072]{1,0:T(8,128)(2,1)}, u32[]{:S(2)}, u32[]{:S(2)}) collective-permute-start(bf16[192,3072]{1,0:T(8,128)(2,1)} %bitcast.31), channel_id=1, source_target_pairs={{0,2},{1,3},{2,0},{3,1},{4,6},{5,7},{6,4},{7,5},{8,10},{9,11},{10,... | collective-permute-start | bytes 3538952 | tf_op jit(solution)/shard_map/ppermute | solution.py:397
  15.5 106.4 %collective-permute-start.6 = (bf16[192,3072]{1,0:T(8,128)(2,1)}, bf16[192,3072]{1,0:T(8,128)(2,1)}, u32[]{:S(2)}, u32[]{:S(2)}) collective-permute-start(bf16[192,3072]{1,0:T(8,128)(2,1)} %bitcast.32), channel_id=1, source_target_pairs={{0,1},{1,0},{2,3},{3,2},{4,5},{5,4},{6,7},{7,6},{8,9},{9,8},{10,11... | collective-permute-start | bytes 3538952 | tf_op jit(solution)/shard_map/ppermute | solution.py:397
  18.7 67.7 %collective-permute-start = (bf16[64,3072]{1,0:T(8,128)(2,1)}, bf16[64,3072]{1,0:T(8,128)(2,1)}, u32[]{:S(2)}, u32[]{:S(2)}) collective-permute-start(bf16[64,3072]{1,0:T(8,128)(2,1)} %constant_dynamic-slice_fusion), channel_id=1, source_target_pairs={{0,4},{1,5},{2,6},{3,7},{4,0},{5,1},{6,2},{7,3},{8,12},{9,13},{10,... | collective-permute-start | bytes 1179656 | tf_op jit(solution)/shard_map/ppermute | solution.py:397
  68.8 11.9 %copy-start.1 = (bf16[8,3,192,256]{3,2,1,0:T(8,128)(2,1)}, bf16[8,3,192,256]{3,2,1,0:T(8,128)(2,1)S(1)}, u32[]{:S(2)}) copy-start(bf16[8,3,192,256]{3,2,1,0:T(8,128)(2,1)S(1)} %all-to-all-done.q_ref.k_ref.v_ref) | copy-start | bytes 7077892
  80.8 0.9 copy-start.4
  81.6 0.7 copy-start.6
  87.6 34.3 %collective-permute-start.7 = (bf16[192,3072]{1,0:T(8,128)(2,1)}, bf16[192,3072]{1,0:T(8,128)(2,1)}, u32[]{:S(2)}, u32[]{:S(2)}) collective-permute-start(bf16[192,3072]{1,0:T(8,128)(2,1)} %collective-permute-done.1.refs_2_.refs_4_), channel_id=1, source_target_pairs={{0,1},{1,0},{2,3},{3,2},{4,5},{5,4},{6,7},{7,6},{8,9},{9,8},{10,11... | collective-permute-start | bytes 3538952 | tf_op jit(solution)/shard_map/ppermute | solution.py:397
  89.0 1.9 collective-permute-start.2
  89.0 12.1 %collective-permute-start.3 = (bf16[64,3072]{1,0:T(8,128)(2,1)}, bf16[64,3072]{1,0:T(8,128)(2,1)S(1)}, u32[]{:S(2)}, u32[]{:S(2)}) collective-permute-start(bf16[64,3072]{1,0:T(8,128)(2,1)} %collective-permute-done.refs_0_), channel_id=1, source_target_pairs={{0,16},{8,24},{16,0},{24,8},{1,17},{9,25},{17,1},{25,9},{2,18},{10... | collective-permute-start | bytes 1179656 | tf_op jit(solution)/shard_map/ppermute | solution.py:407
  90.5 18.3 %collective-permute-start.4 = (bf16[64,3072]{1,0:T(8,128)(2,1)}, bf16[64,3072]{1,0:T(8,128)(2,1)S(1)}, u32[]{:S(2)}, u32[]{:S(2)}) collective-permute-start(bf16[64,3072]{1,0:T(8,128)(2,1)} %collective-permute-done.refs_0_), channel_id=1, source_target_pairs={{0,24},{8,16},{16,8},{24,0},{1,25},{9,17},{17,9},{25,1},{2,26},{10... | collective-permute-start | bytes 1179656 | tf_op jit(solution)/shard_map/ppermute | solution.py:407
  91.0 20.8 %collective-permute-start.5 = (bf16[768,256]{1,0:T(8,128)(2,1)}, bf16[768,256]{1,0:T(8,128)(2,1)S(1)}, u32[]{:S(2)}, u32[]{:S(2)}) collective-permute-start(bf16[768,256]{1,0:T(8,128)(2,1)} %get-tuple-element.50.refs_1_), channel_id=1, source_target_pairs={{0,4},{1,5},{2,6},{3,7},{4,0},{5,1},{6,2},{7,3},{8,12},{9,13},{10,... | collective-permute-start | bytes 1179656 | tf_op jit(solution)/shard_map/ppermute | solution.py:397
  111.7 3.2 %copy-start.7 = (bf16[768,256]{1,0:T(8,128)(2,1)S(1)}, bf16[768,256]{1,0:T(8,128)(2,1)}, u32[]{:S(2)}) copy-start(bf16[768,256]{1,0:T(8,128)(2,1)} %copy-done.6) | copy-start | bytes 1179652
  113.8 1.1 copy-start.12
  114.9 7.5 %copy-start.18 = (bf16[1,192,3072]{2,1,0:T(8,128)(2,1)S(1)}, bf16[1,192,3072]{2,1,0:T(8,128)(2,1)}, u32[]{:S(2)}) copy-start(bf16[1,192,3072]{2,1,0:T(8,128)(2,1)} %param.11) | copy-start | bytes 3538948
  120.8 1.1 copy-start.13
  121.8 27.3 %collective-permute-start.9 = (bf16[192,3072]{1,0:T(8,128)(2,1)S(1)}, bf16[192,3072]{1,0:T(8,128)(2,1)S(1)}, u32[]{:S(2)}, u32[]{:S(2)}) collective-permute-start(bf16[192,3072]{1,0:T(8,128)(2,1)S(1)} %get-tuple-element.72), channel_id=1, source_target_pairs={{0,1},{1,0},{2,3},{3,2},{4,5},{5,4},{6,7},{7,6},{8,9},{9,8},{10,11... | collective-permute-start | bytes 3538952 | tf_op jit(solution)/shard_map/ppermute | solution.py:397
  129.6 28.1 %copy-start.8 = (bf16[768,256]{1,0:T(8,128)(2,1)}, bf16[768,256]{1,0:T(8,128)(2,1)S(1)}, u32[]{:S(2)}) copy-start(bf16[768,256]{1,0:T(8,128)(2,1)S(1)} %get-tuple-element.84.refs_2_) | copy-start | bytes 1179652
  129.6 19.9 %collective-permute-start.8 = (bf16[768,256]{1,0:T(8,128)(2,1)S(1)}, bf16[768,256]{1,0:T(8,128)(2,1)S(1)}, u32[]{:S(2)}, u32[]{:S(2)}) collective-permute-start(bf16[768,256]{1,0:T(8,128)(2,1)S(1)} %get-tuple-element.65), channel_id=1, source_target_pairs={{0,4},{1,5},{2,6},{3,7},{4,0},{5,1},{6,2},{7,3},{8,12},{9,13},{10,... | collective-permute-start | bytes 1179656 | tf_op jit(solution)/shard_map/ppermute | solution.py:397
  137.3 12.3 %copy-start.23 = (bf16[2,2,64,3072]{3,2,1,0:T(8,128)(2,1)S(1)}, bf16[2,2,64,3072]{3,2,1,0:T(8,128)(2,1)}, u32[]{:S(2)}) copy-start(bf16[2,2,64,3072]{3,2,1,0:T(8,128)(2,1)} %get-tuple-element.83) | copy-start | bytes 4718596
  137.3 15.8 %copy-start.21 = (bf16[2,2,64,3072]{3,2,1,0:T(8,128)(2,1)S(1)}, bf16[2,2,64,3072]{3,2,1,0:T(8,128)(2,1)}, u32[]{:S(2)}) copy-start(bf16[2,2,64,3072]{3,2,1,0:T(8,128)(2,1)} %get-tuple-element.82) | copy-start | bytes 4718596
  149.5 8.2 %copy-start.10 = (bf16[768,256]{1,0:T(8,128)(2,1)}, bf16[768,256]{1,0:T(8,128)(2,1)S(1)}, u32[]{:S(2)}) copy-start(bf16[768,256]{1,0:T(8,128)(2,1)S(1)} %collective-permute-done.8.refs_3_) | copy-start | bytes 1179652
  149.5 3.5 %collective-permute-start.12 = (bf16[2,2,64,3072]{3,2,1,0:T(8,128)(2,1)S(1)}, bf16[2,2,64,3072]{3,2,1,0:T(8,128)(2,1)S(1)}, u32[]{:S(2)}, u32[]{:S(2)}) collective-permute-start(bf16[2,2,64,3072]{3,2,1,0:T(8,128)(2,1)S(1)} %copy-done.23), channel_id=1, source_target_pairs={{0,8},{8,0},{16,24},{24,16},{1,9},{9,1},{17,25},{25,17},{2,10},{10... | collective-permute-start | bytes 4718600 | tf_op jit(solution)/shard_map/ppermute | solution.py:407
  149.6 28.4 %collective-permute-start.10 = (bf16[192,3072]{1,0:T(8,128)(2,1)S(1)}, bf16[192,3072]{1,0:T(8,128)(2,1)S(1)}, u32[]{:S(2)}, u32[]{:S(2)}) collective-permute-start(bf16[192,3072]{1,0:T(8,128)(2,1)S(1)} %get-tuple-element.77), channel_id=1, source_target_pairs={{0,1},{1,0},{2,3},{3,2},{4,5},{5,4},{6,7},{7,6},{8,9},{9,8},{10,11... | collective-permute-start | bytes 3538952 | tf_op jit(solution)/shard_map/ppermute | solution.py:397
  150.7 28.3 %collective-permute-start.11 = (bf16[192,3072]{1,0:T(8,128)(2,1)S(1)}, bf16[192,3072]{1,0:T(8,128)(2,1)}, u32[]{:S(2)}, u32[]{:S(2)}) collective-permute-start(bf16[192,3072]{1,0:T(8,128)(2,1)S(1)} %add_convert_fusion.1), channel_id=1, source_target_pairs={{0,2},{1,3},{2,0},{3,1},{4,6},{5,7},{6,4},{7,5},{8,10},{9,11},{10,... | collective-permute-start | bytes 3538952 | tf_op jit(solution)/shard_map/ppermute | solution.py:397
  153.5 1.7 copy-start.19
  155.2 2.5 copy-start.5
  156.2 26.8 %collective-permute-start.13 = (bf16[1,2,64,3072]{3,2,1,0:T(8,128)(2,1)}, bf16[1,2,64,3072]{3,2,1,0:T(8,128)(2,1)}, u32[]{:S(2)}, u32[]{:S(2)}) collective-permute-start(bf16[1,2,64,3072]{3,2,1,0:T(8,128)(2,1)} %slice.34), channel_id=1, source_target_pairs={{0,16},{8,24},{16,0},{24,8},{1,17},{9,25},{17,1},{25,9},{2,18},{10... | collective-permute-start | bytes 2359304 | tf_op jit(solution)/shard_map/ppermute | solution.py:407
  178.0 1.0 copy-start.22
  179.0 42.4 %all-to-all-start.1 = ((bf16[8,3,192,128]{3,2,1,0:T(8,128)(2,1)}), bf16[8,3,192,128]{3,2,1,0:T(8,128)(2,1)S(1)}, u32[]{:S(2)}, u32[]{:S(2)}) async-start(bf16[8,3,192,128]{3,2,1,0:T(8,128)(2,1)} %attention_backward.2), calls=%async_computation.1 | async-start | bytes 2359296 | tf_op jit(solution)/shard_map/all_to_all | solution.py:481
  183.0 6.1 %copy-start.9 = (bf16[768,256]{1,0:T(8,128)(2,1)S(1)}, bf16[768,256]{1,0:T(8,128)(2,1)}, u32[]{:S(2)}) copy-start(bf16[768,256]{1,0:T(8,128)(2,1)} %copy-done.8) | copy-start | bytes 1179652
  183.0 6.1 %copy-start.11 = (bf16[768,256]{1,0:T(8,128)(2,1)S(1)}, bf16[768,256]{1,0:T(8,128)(2,1)}, u32[]{:S(2)}) copy-start(bf16[768,256]{1,0:T(8,128)(2,1)} %copy-done.10) | copy-start | bytes 1179652
  184.9 1.3 copy-start.20
  186.1 44.9 %collective-permute-start.14 = (bf16[64,3072]{1,0:T(8,128)(2,1)}, bf16[64,3072]{1,0:T(8,128)(2,1)}, u32[]{:S(2)}, u32[]{:S(2)}) collective-permute-start(bf16[64,3072]{1,0:T(8,128)(2,1)} %fusion.3), channel_id=1, source_target_pairs={{0,4},{1,5},{2,6},{3,7},{4,0},{5,1},{6,2},{7,3},{8,12},{9,13},{10,... | collective-permute-start | bytes 1179656 | tf_op jit(solution)/shard_map/ppermute | solution.py:397
  196.7 1.1 copy-start.3
  221.4 32.0 %all-to-all-start.2 = ((bf16[8,3,192,128]{3,2,1,0:T(8,128)(2,1)}), bf16[8,3,192,128]{3,2,1,0:T(8,128)(2,1)S(1)}, u32[]{:S(2)}, u32[]{:S(2)}) async-start(bf16[8,3,192,128]{3,2,1,0:T(8,128)(2,1)} %copy-done.3), calls=%async_computation.2 | async-start | bytes 2359296 | tf_op jit(solution)/shard_map/all_to_all | solution.py:481
  225.0 15.2 %copy-start.14 = (bf16[192,3072]{1,0:T(8,128)(2,1)S(1)}, bf16[192,3072]{1,0:T(8,128)(2,1)}, u32[]{:S(2)}) copy-start(bf16[192,3072]{1,0:T(8,128)(2,1)} %copy-done.13) | copy-start | bytes 3538948
  232.4 7.8 %collective-permute-start.16 = (bf16[64,3072]{1,0:T(8,128)(2,1)S(1)}, bf16[64,3072]{1,0:T(8,128)(2,1)S(1)}, u32[]{:S(2)}, u32[]{:S(2)}) collective-permute-start(bf16[64,3072]{1,0:T(8,128)(2,1)S(1)} %fusion.2.refs_0_), channel_id=1, source_target_pairs={{0,16},{8,24},{16,0},{24,8},{1,17},{9,25},{17,1},{25,9},{2,18},{10... | collective-permute-start | bytes 1179656 | tf_op jit(solution)/shard_map/ppermute | solution.py:407
  233.9 9.5 %collective-permute-start.15 = (bf16[64,3072]{1,0:T(8,128)(2,1)S(1)}, bf16[64,3072]{1,0:T(8,128)(2,1)S(1)}, u32[]{:S(2)}, u32[]{:S(2)}) collective-permute-start(bf16[64,3072]{1,0:T(8,128)(2,1)S(1)} %fusion.2.refs_0_), channel_id=1, source_target_pairs={{0,8},{8,0},{16,24},{24,16},{1,9},{9,1},{17,25},{25,17},{2,10},{10... | collective-permute-start | bytes 1179656 | tf_op jit(solution)/shard_map/ppermute | solution.py:407
  240.2 3.2 %collective-permute-start.17 = (bf16[64,3072]{1,0:T(8,128)(2,1)S(1)}, bf16[64,3072]{1,0:T(8,128)(2,1)S(1)}, u32[]{:S(2)}, u32[]{:S(2)}) collective-permute-start(bf16[64,3072]{1,0:T(8,128)(2,1)S(1)} %collective-permute-done.16.refs_2_), channel_id=1, source_target_pairs={{0,8},{8,0},{16,24},{24,16},{1,9},{9,1},{17,25},{25,17},{2,10},{10... | collective-permute-start | bytes 1179656 | tf_op jit(solution)/shard_map/ppermute | solution.py:407

commit v5 on v3

--- a/solution.py
+++ b/solution.py
@@ -53,26 +53,25 @@
     )(*arrays)
 
 
-def unpack_heads(packed):
-    heads = len(packed)
-    n, count, rows, width = packed[0].shape
-    cols = heads * width
+def unpack_head(packed, head, heads, outs):
+    n, count, rows, width = packed.shape
 
     def body(*refs):
         for a in range(count):
-            for h in range(heads):
-                refs[heads + a][:, h * width : (h + 1) * width] = refs[h][0, a]
-
-    return pl.pallas_call(
-        body,
-        out_shape=[jax.ShapeDtypeStruct((rows, n * cols), BF16)] * count,
+            refs[1 + len(outs) + a][...] = refs[0][0, a]
+
+    return pl.pallas_call(
+        body,
+        out_shape=[jax.ShapeDtypeStruct((rows, n * heads * width), BF16)] * count,
         grid=(n,),
-        in_specs=[pl.BlockSpec((1, count, rows, width), lambda j: (j, 0, 0, 0))] * heads,
-        out_specs=[pl.BlockSpec((rows, cols), lambda j: (0, j))] * count,
-        compiler_params=params(),
-        cost_estimate=cost(0, 4 * n * count * rows * cols),
-        name="unpack_heads",
-    )(*packed)
+        in_specs=[pl.BlockSpec((1, count, rows, width), lambda j: (j, 0, 0, 0))]
+        + [pl.BlockSpec(memory_space=pl.ANY)] * len(outs),
+        out_specs=[pl.BlockSpec((rows, width), lambda j: (0, j * heads + head))] * count,
+        input_output_aliases={1 + a: a for a in range(len(outs))},
+        compiler_params=params(),
+        cost_estimate=cost(0, 4 * n * count * rows * width),
+        name="unpack_head",
+    )(packed, *outs)
 
 
 def split3(x):
@@ -476,7 +475,10 @@
     grads[0], got = lax.optimization_barrier((grads[0], got))
     gw = (gw_own + xor(gw_send, m).astype(F32)).astype(BF16)
     grads = [lax.all_to_all(x, "seq", split_axis=0, concat_axis=0, tiled=True) for x in grads]
-    back_q, back_k, back_v = unpack_heads(grads)
+    back = []
+    for head in range(heads):
+        back = unpack_head(grads[head], head, heads, back)
+    back_q, back_k, back_v = back
 
     block_out = sum(x.astype(F32) for x in [partials[0]] + got).astype(BF16)
     pieces = gather_parts(gw)

time: 257 us -> 257 us (level)
    all_to_all x2, waiting for transfers between devices: 30.2 us -> 27.5 us  [shards(): lax.all_to_all(x, 'seq', split_axis=0, concat_axis=0, tiled=True)]
    pallas_call x1 -> x2, Pallas kernels: 3.12 us -> 5.38 us  [unpack_head(): pl.pallas_call(body, out_shape=[jax.ShapeDtypeStruct((rows, n * heads * w...]
  transfers between devices with their start and end apart: 21 -> 21, of which waited for: 13 -> 13; matrix products, arithmetic and copies ran while one was open for 5% -> 5% of each run, Pallas kernels for 23% -> 24%
where the time goes in v5:
time: 257 us; the launch traced here: 256 us
  waiting for transfers between devices  131 us (51%)
  Pallas kernels  65.8 us (26%)
  starting transfers between devices  34.1 us (13%)
  local copies, waits for them, and re-layouts  17.2 us (7%)
  other arithmetic  7.42 us (3%)
    all_to_all x1, waiting for transfers between devices, shards(): lax.all_to_all(packed, 'seq', split_axis=0, concat_axis=0, tiled=True)  46.9 us
    ppermute x10, waiting for transfers between devices, shards(): lax.ppermute(x, 'seq', [(i, i ^ bit) for i in range(n)])  32.1 us
    all_to_all x2, waiting for transfers between devices, shards(): lax.all_to_all(x, 'seq', split_axis=0, concat_axis=0, tiled=True)  27.5 us
    ppermute x8, waiting for transfers between devices, shards(): lax.ppermute(x, 'dp', [(i, i ^ bit) for i in range(dp)])  24.1 us
    pallas_call x2, Pallas kernels, attention_backward(): pl.pallas_call(body, out_shape=jax.ShapeDtypeStruct((n, 3, rows, HDIM), B...  18.7 us
    pallas_call x1, Pallas kernels, attention_forward(): pl.pallas_call(body, out_shape=[jax.ShapeDtypeStruct((tokens // 2, cols),...  15.9 us
    ppermute x10, starting transfers between devices, shards(): lax.ppermute(x, 'seq', [(i, i ^ bit) for i in range(n)])  14.4 us
    unnamed x48, local copies, waits for them, and re-layouts  12.8 us
  transfers between devices with their start and end apart: 21, of which 13 were waited for; matrix products, arithmetic and copies ran while one was open for 5% of the time, Pallas kernels for 24%

profile of v5, /device:TPU:0, one launch (start us, length us, event | category | flops | bytes accessed | tf_op | source)
XLA Modules:
  0.0 256.1 jit_solution(12968778757319973606)
XLA Ops:
  0.7 1.2 copy-done.15
  1.8 1.1 copy-done.16
  3.0 1.1 copy-done.17
  4.8 1.4 copy-done.2
  6.2 7.3 %all-to-all-start = ((bf16[8,3,192,256]{3,2,1,0:T(8,128)(2,1)}), bf16[8,3,192,256]{3,2,1,0:T(8,128)(2,1)S(1)}, u32[]{:S(2)}, u32[]{:S(2)}) async-start(bf16[8,3,192,256]{3,2,1,0:T(8,128)(2,1)} %copy-done.2), calls=%async_computation | async-start | bytes 4718592 | tf_op jit(solution)/shard_map/all_to_all | solution.py:410
  13.4 2.0 collective-permute-start.1
  15.5 1.5 collective-permute-start.6
  16.9 1.8 constant_dynamic-slice_fusion
  18.7 2.4 collective-permute-start
  21.9 46.9 %all-to-all-done.q_ref.k_ref.v_ref = bf16[8,3,192,256]{3,2,1,0:T(8,128)(2,1)S(1)} async-done(((bf16[8,3,192,256]{3,2,1,0:T(8,128)(2,1)}), bf16[8,3,192,256]{3,2,1,0:T(8,128)(2,1)S(1)}, u32[]{:S(2)}, u32[]{:S(2)}) %all-to-all-start) | async-done | bytes 2359328 | tf_op jit(solution)/shard_map/all_to_all | solution.py:410
  68.9 15.9 %attention_forward.1 = (bf16[768,256]{1,0:T(8,128)(2,1)S(1)}, bf16[768,256]{1,0:T(8,128)(2,1)}, bf16[1536,256]{1,0:T(8,128)(2,1)S(1)}) custom-call(s32[1]{0:T(128)} %bitcast.1.half_ref, bf16[8,3,192,256]{3,2,1,0:T(8,128)(2,1)S(1)} %all-to-all-done.q_ref.k_ref.v_ref, bf16[8,3,192,256]{3,2,1,0:T(8,128)(2,1)S(1)} %all-to-all-done.q_ref.k_ref.v_ref, ...), custom_call_target="tpu_custom_call" | custom-call | flops 2415919104 | bytes 3145728 | tf_op jit(solution)/shard_map/attention_forward/pallas_call | solution.py:131
  86.4 1.1 collective-permute-done.1.refs_2_.refs_4_
  87.6 1.5 collective-permute-start.7
  89.0 1.5 collective-permute-start.3
  91.0 2.1 collective-permute-start.5
  93.0 8.1 %collective-permute-done.3.refs_2_ = bf16[64,3072]{1,0:T(8,128)(2,1)S(1)} collective-permute-done((bf16[64,3072]{1,0:T(8,128)(2,1)}, bf16[64,3072]{1,0:T(8,128)(2,1)S(1)}, u32[]{:S(2)}, u32[]{:S(2)}) %collective-permute-start.3) | collective-permute-done | bytes 393248 | tf_op jit(solution)/shard_map/ppermute | solution.py:403
  101.2 7.7 %collective-permute-done.4.refs_3_ = bf16[64,3072]{1,0:T(8,128)(2,1)S(1)} collective-permute-done((bf16[64,3072]{1,0:T(8,128)(2,1)}, bf16[64,3072]{1,0:T(8,128)(2,1)S(1)}, u32[]{:S(2)}, u32[]{:S(2)}) %collective-permute-start.4) | collective-permute-done | bytes 393248 | tf_op jit(solution)/shard_map/ppermute | solution.py:403
  108.8 2.9 %collective-permute-done.5.a1_ref.refs_1_ = bf16[768,256]{1,0:T(8,128)(2,1)S(1)} collective-permute-done((bf16[768,256]{1,0:T(8,128)(2,1)}, bf16[768,256]{1,0:T(8,128)(2,1)S(1)}, u32[]{:S(2)}, u32[]{:S(2)}) %collective-permute-start.5) | collective-permute-done | bytes 393248 | tf_op jit(solution)/shard_map/ppermute | solution.py:393
  111.7 2.0 join_parts.2
  113.8 1.1 copy-done.12
  114.9 5.8 %output_partial.1 = (bf16[192,3072]{1,0:T(8,128)(2,1)S(1)}, bf16[192,3072]{1,0:T(8,128)(2,1)S(1)}, bf16[192,3072]{1,0:T(8,128)(2,1)S(1)}, bf16[192,3072]{1,0:T(8,128)(2,1)S(1)}) custom-call(s32[1]{0:T(128)} %bitcast.rank_ref, bf16[768,256]{1,0:T(8,128)(2,1)S(1)} %copy-done.7, bf16[768,256]{1,0:T(8,128)(2,1)S(1)} %collective-permute-done.5.a1_ref.refs_1_, ...), custom_call_target="tpu_custom_call" | custom-call | flops 2415919104 | bytes 7864320 | tf_op jit(solution)/shard_map/output_partial/pallas_call | solution.py:278
  120.8 1.0 copy-done.13
  122.4 7.2 %attention_grad.1 = (bf16[768,256]{1,0:T(8,128)(2,1)S(1)}, bf16[768,256]{1,0:T(8,128)(2,1)S(1)}) custom-call(s32[1]{0:T(128)} %bitcast.rank_ref, bf16[192,3072]{1,0:T(8,128)(2,1)S(1)} %bitcast.33, bf16[192,3072]{1,0:T(8,128)(2,1)} %collective-permute-done.6.refs_1_.refs_3_, bf16[192,3072]{1,0:T(8,128)(2,1)} %collective-permute-done.1.refs_2_.refs_4_, ...), custom_call_target="tpu_custom_call" | custom-call | flops 2415919104 | bytes 7864320 | tf_op jit(solution)/shard_map/attention_grad/pallas_call | solution.py:251
  129.7 7.9 %weight_grad_partial.1 = (bf16[2,2,64,3072]{3,2,1,0:T(8,128)(2,1)}, bf16[2,2,64,3072]{3,2,1,0:T(8,128)(2,1)}) custom-call(s32[1]{0:T(128)} %bitcast.rank_ref, s32[1]{0:T(128)} %bitcast.7.place_ref, bf16[768,256]{1,0:T(8,128)(2,1)S(1)} %copy-done.7, bf16[768,256]{1,0:T(8,128)(2,1)S(1)} %collective-permute-done.5.a1_ref.refs_1_, ...), custom_call_target="tpu_custom_call" | custom-call | flops 2415919104 | bytes 7864320 | tf_op jit(solution)/shard_map/weight_grad_partial/pallas_call | solution.py:322
  137.6 11.5 %collective-permute-done.9 = bf16[192,3072]{1,0:T(8,128)(2,1)S(1)} collective-permute-done((bf16[192,3072]{1,0:T(8,128)(2,1)S(1)}, bf16[192,3072]{1,0:T(8,128)(2,1)S(1)}, u32[]{:S(2)}, u32[]{:S(2)}) %collective-permute-start.9) | collective-permute-done | bytes 1179680 | tf_op jit(solution)/shard_map/ppermute | solution.py:393
  149.6 1.1 collective-permute-start.10
  151.1 2.0 collective-permute-done.12
  153.6 1.7 copy-done.19
  156.2 1.5 collective-permute-start.13
  157.7 9.9 %attention_backward.2 = bf16[8,3,192,128]{3,2,1,0:T(8,128)(2,1)} custom-call(s32[1]{0:T(128)} %bitcast.1.half_ref, bf16[8,3,192,256]{3,2,1,0:T(8,128)(2,1)} %copy-done.1, bf16[8,3,192,256]{3,2,1,0:T(8,128)(2,1)} %copy-done.1, bf16[8,3,192,256]{3,2,1,0:T(8,128)(2,1)} %copy-done.1, bf16[2,1536,128]{2,1,0:T(8,128)(2,1)S(1)} %bitcast.24, ...), custom_call_target="tpu_custom_call" | custom-call | flops 3019898880 | bytes 2752512 | tf_op jit(solution)/shard_map/attention_backward/pallas_call | solution.py:214
  167.5 10.5 %collective-permute-done.10 = bf16[192,3072]{1,0:T(8,128)(2,1)S(1)} collective-permute-done((bf16[192,3072]{1,0:T(8,128)(2,1)S(1)}, bf16[192,3072]{1,0:T(8,128)(2,1)S(1)}, u32[]{:S(2)}, u32[]{:S(2)}) %collective-permute-start.10) | collective-permute-done | bytes 1179680 | tf_op jit(solution)/shard_map/ppermute | solution.py:393
  178.0 1.0 copy-done.22
  179.0 4.0 %all-to-all-start.2 = ((bf16[8,3,192,128]{3,2,1,0:T(8,128)(2,1)}), bf16[8,3,192,128]{3,2,1,0:T(8,128)(2,1)S(1)}, u32[]{:S(2)}, u32[]{:S(2)}) async-start(bf16[8,3,192,128]{3,2,1,0:T(8,128)(2,1)} %attention_backward.2), calls=%async_computation.2 | async-start | bytes 2359296 | tf_op jit(solution)/shard_map/all_to_all | solution.py:477
  183.0 1.8 slice_add_fusion
  186.1 2.9 %collective-permute-start.14 = (bf16[64,3072]{1,0:T(8,128)(2,1)}, bf16[64,3072]{1,0:T(8,128)(2,1)}, u32[]{:S(2)}, u32[]{:S(2)}) collective-permute-start(bf16[64,3072]{1,0:T(8,128)(2,1)} %fusion.3), channel_id=1, source_target_pairs={{0,4},{1,5},{2,6},{3,7},{4,0},{5,1},{6,2},{7,3},{8,12},{9,13},{10,... | collective-permute-start | bytes 1179656 | tf_op jit(solution)/shard_map/ppermute | solution.py:393
  189.0 8.9 %attention_backward.3 = bf16[8,3,192,128]{3,2,1,0:T(8,128)(2,1)S(1)} custom-call(s32[1]{0:T(128)} %bitcast.1.half_ref, bf16[8,3,192,256]{3,2,1,0:T(8,128)(2,1)} %copy-done.1, bf16[8,3,192,256]{3,2,1,0:T(8,128)(2,1)} %copy-done.1, bf16[8,3,192,256]{3,2,1,0:T(8,128)(2,1)} %copy-done.1, bf16[2,1536,128]{2,1,0:T(8,128)(2,1)S(1)} %bitcast.25, ...), custom_call_target="tpu_custom_call" | custom-call | flops 3019898880 | bytes 2752512 | tf_op jit(solution)/shard_map/attention_backward/pallas_call | solution.py:214
  197.9 1.1 copy-done.3
  199.0 22.4 %all-to-all-done.2.refs_0_ = bf16[8,3,192,128]{3,2,1,0:T(8,128)(2,1)S(1)} async-done(((bf16[8,3,192,128]{3,2,1,0:T(8,128)(2,1)}), bf16[8,3,192,128]{3,2,1,0:T(8,128)(2,1)S(1)}, u32[]{:S(2)}, u32[]{:S(2)}) %all-to-all-start.2) | async-done | bytes 1179680 | tf_op jit(solution)/shard_map/all_to_all | solution.py:477
  221.4 3.6 %all-to-all-start.1 = ((bf16[8,3,192,128]{3,2,1,0:T(8,128)(2,1)}), bf16[8,3,192,128]{3,2,1,0:T(8,128)(2,1)S(1)}, u32[]{:S(2)}, u32[]{:S(2)}) async-start(bf16[8,3,192,128]{3,2,1,0:T(8,128)(2,1)} %copy-done.3), calls=%async_computation.1 | async-start | bytes 2359296 | tf_op jit(solution)/shard_map/all_to_all | solution.py:477
  225.0 6.1 %collective-permute-done.14 = bf16[64,3072]{1,0:T(8,128)(2,1)} collective-permute-done((bf16[64,3072]{1,0:T(8,128)(2,1)}, bf16[64,3072]{1,0:T(8,128)(2,1)}, u32[]{:S(2)}, u32[]{:S(2)}) %collective-permute-start.14) | collective-permute-done | bytes 393248 | tf_op jit(solution)/shard_map/ppermute | solution.py:393
  231.1 1.3 fusion.2.refs_0_
  232.4 1.5 collective-permute-start.16
  233.9 6.3 %collective-permute-done.16.refs_2_ = bf16[64,3072]{1,0:T(8,128)(2,1)S(1)} collective-permute-done((bf16[64,3072]{1,0:T(8,128)(2,1)S(1)}, bf16[64,3072]{1,0:T(8,128)(2,1)S(1)}, u32[]{:S(2)}, u32[]{:S(2)}) %collective-permute-start.16) | collective-permute-done | bytes 393248 | tf_op jit(solution)/shard_map/ppermute | solution.py:403
  240.2 3.2 %fusion = bf16[1,192,3072]{2,1,0:T(8,128)(2,1)} fusion(bf16[192,3072]{1,0:T(8,128)(2,1)} %collective-permute-done.11, bf16[192,3072]{1,0:T(8,128)(2,1)} %copy-done.22, bf16[192,3072]{1,0:T(8,128)(2,1)S(1)} %copy-done.14), kind=kLoop, calls=%fused_computation.5 | loop fusion | flops 3538944 | bytes 4718592 | tf_op jit(solution)/shard_map/broadcast_in_dim | solution.py:486
  243.4 2.7 %unpack_head.2 = (bf16[192,2048]{1,0:T(8,128)(2,1)}, bf16[192,2048]{1,0:T(8,128)(2,1)}, bf16[192,2048]{1,0:T(8,128)(2,1)}) custom-call(bf16[8,3,192,128]{3,2,1,0:T(8,128)(2,1)S(1)} %all-to-all-done.2.refs_0_), custom_call_target="tpu_custom_call" | custom-call | bytes 2359296 | tf_op jit(solution)/shard_map/unpack_head/pallas_call | solution.py:63
  246.1 2.2 join_parts.3
  248.3 5.1 %all-to-all-done.1.refs_0_ = bf16[8,3,192,128]{3,2,1,0:T(8,128)(2,1)S(1)} async-done(((bf16[8,3,192,128]{3,2,1,0:T(8,128)(2,1)}), bf16[8,3,192,128]{3,2,1,0:T(8,128)(2,1)S(1)}, u32[]{:S(2)}, u32[]{:S(2)}) %all-to-all-start.1) | async-done | bytes 1179680 | tf_op jit(solution)/shard_map/all_to_all | solution.py:477
  253.4 2.7 %unpack_head.3 = (bf16[192,2048]{1,0:T(8,128)(2,1)}, bf16[192,2048]{1,0:T(8,128)(2,1)}, bf16[192,2048]{1,0:T(8,128)(2,1)}) custom-call(bf16[8,3,192,128]{3,2,1,0:T(8,128)(2,1)S(1)} %all-to-all-done.1.refs_0_, bf16[192,2048]{1,0:T(8,128)(2,1)} %get-tuple-element.88.refs_1_, ...), custom_call_target="tpu_custom_call", output_to_operand_aliasing={{0}: (1, {}), {1}: (2, {}), {2}: (3, {})} | custom-call | bytes 2359296 | tf_op jit(solution)/shard_map/unpack_head/pallas_call | solution.py:63
  (69 shorter events, 8.0 us)
Async XLA Ops:
  0.6 21.1 %copy-start = (s32[16,24,16]{1,2,0:T(8,128)S(1)}, s32[16,24,16]{1,2,0:T(8,128)}, u32[]{:S(2)}) copy-start(s32[16,24,16]{1,2,0:T(8,128)} %param.12) | copy-start | bytes 73732
  0.6 1.2 copy-start.15
  1.8 1.1 copy-start.16
  3.0 1.1 copy-start.17
  4.8 1.4 copy-start.2
  6.2 62.7 %all-to-all-start = ((bf16[8,3,192,256]{3,2,1,0:T(8,128)(2,1)}), bf16[8,3,192,256]{3,2,1,0:T(8,128)(2,1)S(1)}, u32[]{:S(2)}, u32[]{:S(2)}) async-start(bf16[8,3,192,256]{3,2,1,0:T(8,128)(2,1)} %copy-done.2), calls=%async_computation | async-start | bytes 4718592 | tf_op jit(solution)/shard_map/all_to_all | solution.py:410
  13.4 74.1 %collective-permute-start.1 = (bf16[192,3072]{1,0:T(8,128)(2,1)}, bf16[192,3072]{1,0:T(8,128)(2,1)}, u32[]{:S(2)}, u32[]{:S(2)}) collective-permute-start(bf16[192,3072]{1,0:T(8,128)(2,1)} %bitcast.31), channel_id=1, source_target_pairs={{0,2},{1,3},{2,0},{3,1},{4,6},{5,7},{6,4},{7,5},{8,10},{9,11},{10,... | collective-permute-start | bytes 3538952 | tf_op jit(solution)/shard_map/ppermute | solution.py:393
  15.5 106.4 %collective-permute-start.6 = (bf16[192,3072]{1,0:T(8,128)(2,1)}, bf16[192,3072]{1,0:T(8,128)(2,1)}, u32[]{:S(2)}, u32[]{:S(2)}) collective-permute-start(bf16[192,3072]{1,0:T(8,128)(2,1)} %bitcast.32), channel_id=1, source_target_pairs={{0,1},{1,0},{2,3},{3,2},{4,5},{5,4},{6,7},{7,6},{8,9},{9,8},{10,11... | collective-permute-start | bytes 3538952 | tf_op jit(solution)/shard_map/ppermute | solution.py:393
  18.7 67.7 %collective-permute-start = (bf16[64,3072]{1,0:T(8,128)(2,1)}, bf16[64,3072]{1,0:T(8,128)(2,1)}, u32[]{:S(2)}, u32[]{:S(2)}) collective-permute-start(bf16[64,3072]{1,0:T(8,128)(2,1)} %constant_dynamic-slice_fusion), channel_id=1, source_target_pairs={{0,4},{1,5},{2,6},{3,7},{4,0},{5,1},{6,2},{7,3},{8,12},{9,13},{10,... | collective-permute-start | bytes 1179656 | tf_op jit(solution)/shard_map/ppermute | solution.py:393
  68.8 16.0 %copy-start.1 = (bf16[8,3,192,256]{3,2,1,0:T(8,128)(2,1)}, bf16[8,3,192,256]{3,2,1,0:T(8,128)(2,1)S(1)}, u32[]{:S(2)}) copy-start(bf16[8,3,192,256]{3,2,1,0:T(8,128)(2,1)S(1)} %all-to-all-done.q_ref.k_ref.v_ref) | copy-start | bytes 7077892
  84.8 0.9 copy-start.4
  85.7 0.7 copy-start.6
  87.6 34.3 %collective-permute-start.7 = (bf16[192,3072]{1,0:T(8,128)(2,1)}, bf16[192,3072]{1,0:T(8,128)(2,1)}, u32[]{:S(2)}, u32[]{:S(2)}) collective-permute-start(bf16[192,3072]{1,0:T(8,128)(2,1)} %collective-permute-done.1.refs_2_.refs_4_), channel_id=1, source_target_pairs={{0,1},{1,0},{2,3},{3,2},{4,5},{5,4},{6,7},{7,6},{8,9},{9,8},{10,11... | collective-permute-start | bytes 3538952 | tf_op jit(solution)/shard_map/ppermute | solution.py:393
  89.0 1.9 collective-permute-start.2
  89.0 12.1 %collective-permute-start.3 = (bf16[64,3072]{1,0:T(8,128)(2,1)}, bf16[64,3072]{1,0:T(8,128)(2,1)S(1)}, u32[]{:S(2)}, u32[]{:S(2)}) collective-permute-start(bf16[64,3072]{1,0:T(8,128)(2,1)} %collective-permute-done.refs_0_), channel_id=1, source_target_pairs={{0,16},{8,24},{16,0},{24,8},{1,17},{9,25},{17,1},{25,9},{2,18},{10... | collective-permute-start | bytes 1179656 | tf_op jit(solution)/shard_map/ppermute | solution.py:403
  90.5 18.3 %collective-permute-start.4 = (bf16[64,3072]{1,0:T(8,128)(2,1)}, bf16[64,3072]{1,0:T(8,128)(2,1)S(1)}, u32[]{:S(2)}, u32[]{:S(2)}) collective-permute-start(bf16[64,3072]{1,0:T(8,128)(2,1)} %collective-permute-done.refs_0_), channel_id=1, source_target_pairs={{0,24},{8,16},{16,8},{24,0},{1,25},{9,17},{17,9},{25,1},{2,26},{10... | collective-permute-start | bytes 1179656 | tf_op jit(solution)/shard_map/ppermute | solution.py:403
  91.0 20.8 %collective-permute-start.5 = (bf16[768,256]{1,0:T(8,128)(2,1)}, bf16[768,256]{1,0:T(8,128)(2,1)S(1)}, u32[]{:S(2)}, u32[]{:S(2)}) collective-permute-start(bf16[768,256]{1,0:T(8,128)(2,1)} %get-tuple-element.53.refs_1_), channel_id=1, source_target_pairs={{0,4},{1,5},{2,6},{3,7},{4,0},{5,1},{6,2},{7,3},{8,12},{9,13},{10,... | collective-permute-start | bytes 1179656 | tf_op jit(solution)/shard_map/ppermute | solution.py:393
  111.7 3.2 %copy-start.7 = (bf16[768,256]{1,0:T(8,128)(2,1)S(1)}, bf16[768,256]{1,0:T(8,128)(2,1)}, u32[]{:S(2)}) copy-start(bf16[768,256]{1,0:T(8,128)(2,1)} %copy-done.6) | copy-start | bytes 1179652
  113.8 1.1 copy-start.12
  114.9 7.5 %copy-start.18 = (bf16[1,192,3072]{2,1,0:T(8,128)(2,1)S(1)}, bf16[1,192,3072]{2,1,0:T(8,128)(2,1)}, u32[]{:S(2)}) copy-start(bf16[1,192,3072]{2,1,0:T(8,128)(2,1)} %param.11) | copy-start | bytes 3538948
  120.8 1.1 copy-start.13
  121.8 27.3 %collective-permute-start.9 = (bf16[192,3072]{1,0:T(8,128)(2,1)S(1)}, bf16[192,3072]{1,0:T(8,128)(2,1)S(1)}, u32[]{:S(2)}, u32[]{:S(2)}) collective-permute-start(bf16[192,3072]{1,0:T(8,128)(2,1)S(1)} %get-tuple-element.75), channel_id=1, source_target_pairs={{0,1},{1,0},{2,3},{3,2},{4,5},{5,4},{6,7},{7,6},{8,9},{9,8},{10,11... | collective-permute-start | bytes 3538952 | tf_op jit(solution)/shard_map/ppermute | solution.py:393
  129.6 28.1 %copy-start.8 = (bf16[768,256]{1,0:T(8,128)(2,1)}, bf16[768,256]{1,0:T(8,128)(2,1)S(1)}, u32[]{:S(2)}) copy-start(bf16[768,256]{1,0:T(8,128)(2,1)S(1)} %get-tuple-element.86.refs_2_) | copy-start | bytes 1179652
  129.6 19.9 %collective-permute-start.8 = (bf16[768,256]{1,0:T(8,128)(2,1)S(1)}, bf16[768,256]{1,0:T(8,128)(2,1)S(1)}, u32[]{:S(2)}, u32[]{:S(2)}) collective-permute-start(bf16[768,256]{1,0:T(8,128)(2,1)S(1)} %get-tuple-element.68), channel_id=1, source_target_pairs={{0,4},{1,5},{2,6},{3,7},{4,0},{5,1},{6,2},{7,3},{8,12},{9,13},{10,... | collective-permute-start | bytes 1179656 | tf_op jit(solution)/shard_map/ppermute | solution.py:393
  137.6 11.9 %copy-start.23 = (bf16[2,2,64,3072]{3,2,1,0:T(8,128)(2,1)S(1)}, bf16[2,2,64,3072]{3,2,1,0:T(8,128)(2,1)}, u32[]{:S(2)}) copy-start(bf16[2,2,64,3072]{3,2,1,0:T(8,128)(2,1)} %get-tuple-element.85) | copy-start | bytes 4718596
  137.6 15.4 %copy-start.21 = (bf16[2,2,64,3072]{3,2,1,0:T(8,128)(2,1)S(1)}, bf16[2,2,64,3072]{3,2,1,0:T(8,128)(2,1)}, u32[]{:S(2)}) copy-start(bf16[2,2,64,3072]{3,2,1,0:T(8,128)(2,1)} %get-tuple-element.84) | copy-start | bytes 4718596
  149.5 8.2 %copy-start.10 = (bf16[768,256]{1,0:T(8,128)(2,1)}, bf16[768,256]{1,0:T(8,128)(2,1)S(1)}, u32[]{:S(2)}) copy-start(bf16[768,256]{1,0:T(8,128)(2,1)S(1)} %collective-permute-done.8.refs_3_) | copy-start | bytes 1179652
  149.5 3.5 %collective-permute-start.12 = (bf16[2,2,64,3072]{3,2,1,0:T(8,128)(2,1)S(1)}, bf16[2,2,64,3072]{3,2,1,0:T(8,128)(2,1)S(1)}, u32[]{:S(2)}, u32[]{:S(2)}) collective-permute-start(bf16[2,2,64,3072]{3,2,1,0:T(8,128)(2,1)S(1)} %copy-done.23), channel_id=1, source_target_pairs={{0,8},{8,0},{16,24},{24,16},{1,9},{9,1},{17,25},{25,17},{2,10},{10... | collective-permute-start | bytes 4718600 | tf_op jit(solution)/shard_map/ppermute | solution.py:403
  149.6 28.4 %collective-permute-start.10 = (bf16[192,3072]{1,0:T(8,128)(2,1)S(1)}, bf16[192,3072]{1,0:T(8,128)(2,1)S(1)}, u32[]{:S(2)}, u32[]{:S(2)}) collective-permute-start(bf16[192,3072]{1,0:T(8,128)(2,1)S(1)} %get-tuple-element.80), channel_id=1, source_target_pairs={{0,1},{1,0},{2,3},{3,2},{4,5},{5,4},{6,7},{7,6},{8,9},{9,8},{10,11... | collective-permute-start | bytes 3538952 | tf_op jit(solution)/shard_map/ppermute | solution.py:393
  150.7 28.3 %collective-permute-start.11 = (bf16[192,3072]{1,0:T(8,128)(2,1)S(1)}, bf16[192,3072]{1,0:T(8,128)(2,1)}, u32[]{:S(2)}, u32[]{:S(2)}) collective-permute-start(bf16[192,3072]{1,0:T(8,128)(2,1)S(1)} %add_convert_fusion.1), channel_id=1, source_target_pairs={{0,2},{1,3},{2,0},{3,1},{4,6},{5,7},{6,4},{7,5},{8,10},{9,11},{10,... | collective-permute-start | bytes 3538952 | tf_op jit(solution)/shard_map/ppermute | solution.py:393
  153.5 1.7 copy-start.19
  155.2 2.5 copy-start.5
  156.2 26.8 %collective-permute-start.13 = (bf16[1,2,64,3072]{3,2,1,0:T(8,128)(2,1)}, bf16[1,2,64,3072]{3,2,1,0:T(8,128)(2,1)}, u32[]{:S(2)}, u32[]{:S(2)}) collective-permute-start(bf16[1,2,64,3072]{3,2,1,0:T(8,128)(2,1)} %slice.34), channel_id=1, source_target_pairs={{0,16},{8,24},{16,0},{24,8},{1,17},{9,25},{17,1},{25,9},{2,18},{10... | collective-permute-start | bytes 2359304 | tf_op jit(solution)/shard_map/ppermute | solution.py:403
  178.0 1.0 copy-start.22
  179.0 42.4 %all-to-all-start.2 = ((bf16[8,3,192,128]{3,2,1,0:T(8,128)(2,1)}), bf16[8,3,192,128]{3,2,1,0:T(8,128)(2,1)S(1)}, u32[]{:S(2)}, u32[]{:S(2)}) async-start(bf16[8,3,192,128]{3,2,1,0:T(8,128)(2,1)} %attention_backward.2), calls=%async_computation.2 | async-start | bytes 2359296 | tf_op jit(solution)/shard_map/all_to_all | solution.py:477
  183.0 6.1 %copy-start.9 = (bf16[768,256]{1,0:T(8,128)(2,1)S(1)}, bf16[768,256]{1,0:T(8,128)(2,1)}, u32[]{:S(2)}) copy-start(bf16[768,256]{1,0:T(8,128)(2,1)} %copy-done.8) | copy-start | bytes 1179652
  183.0 6.1 %copy-start.11 = (bf16[768,256]{1,0:T(8,128)(2,1)S(1)}, bf16[768,256]{1,0:T(8,128)(2,1)}, u32[]{:S(2)}) copy-start(bf16[768,256]{1,0:T(8,128)(2,1)} %copy-done.10) | copy-start | bytes 1179652
  184.9 1.3 copy-start.20
  186.1 44.9 %collective-permute-start.14 = (bf16[64,3072]{1,0:T(8,128)(2,1)}, bf16[64,3072]{1,0:T(8,128)(2,1)}, u32[]{:S(2)}, u32[]{:S(2)}) collective-permute-start(bf16[64,3072]{1,0:T(8,128)(2,1)} %fusion.3), channel_id=1, source_target_pairs={{0,4},{1,5},{2,6},{3,7},{4,0},{5,1},{6,2},{7,3},{8,12},{9,13},{10,... | collective-permute-start | bytes 1179656 | tf_op jit(solution)/shard_map/ppermute | solution.py:393
  197.9 1.1 copy-start.3
  221.4 32.0 %all-to-all-start.1 = ((bf16[8,3,192,128]{3,2,1,0:T(8,128)(2,1)}), bf16[8,3,192,128]{3,2,1,0:T(8,128)(2,1)S(1)}, u32[]{:S(2)}, u32[]{:S(2)}) async-start(bf16[8,3,192,128]{3,2,1,0:T(8,128)(2,1)} %copy-done.3), calls=%async_computation.1 | async-start | bytes 2359296 | tf_op jit(solution)/shard_map/all_to_all | solution.py:477
  225.0 15.2 %copy-start.14 = (bf16[192,3072]{1,0:T(8,128)(2,1)S(1)}, bf16[192,3072]{1,0:T(8,128)(2,1)}, u32[]{:S(2)}) copy-start(bf16[192,3072]{1,0:T(8,128)(2,1)} %copy-done.13) | copy-start | bytes 3538948
  232.4 7.8 %collective-permute-start.16 = (bf16[64,3072]{1,0:T(8,128)(2,1)S(1)}, bf16[64,3072]{1,0:T(8,128)(2,1)S(1)}, u32[]{:S(2)}, u32[]{:S(2)}) collective-permute-start(bf16[64,3072]{1,0:T(8,128)(2,1)S(1)} %fusion.2.refs_0_), channel_id=1, source_target_pairs={{0,16},{8,24},{16,0},{24,8},{1,17},{9,25},{17,1},{25,9},{2,18},{10... | collective-permute-start | bytes 1179656 | tf_op jit(solution)/shard_map/ppermute | solution.py:403
  233.9 12.2 %collective-permute-start.15 = (bf16[64,3072]{1,0:T(8,128)(2,1)S(1)}, bf16[64,3072]{1,0:T(8,128)(2,1)S(1)}, u32[]{:S(2)}, u32[]{:S(2)}) collective-permute-start(bf16[64,3072]{1,0:T(8,128)(2,1)S(1)} %fusion.2.refs_0_), channel_id=1, source_target_pairs={{0,8},{8,0},{16,24},{24,16},{1,9},{9,1},{17,25},{25,17},{2,10},{10... | collective-permute-start | bytes 1179656 | tf_op jit(solution)/shard_map/ppermute | solution.py:403
  240.2 5.9 %collective-permute-start.17 = (bf16[64,3072]{1,0:T(8,128)(2,1)S(1)}, bf16[64,3072]{1,0:T(8,128)(2,1)S(1)}, u32[]{:S(2)}, u32[]{:S(2)}) collective-permute-start(bf16[64,3072]{1,0:T(8,128)(2,1)S(1)} %collective-permute-done.16.refs_2_), channel_id=1, source_target_pairs={{0,8},{8,0},{16,24},{24,16},{1,9},{9,1},{17,25},{25,17},{2,10},{10... | collective-permute-start | bytes 1179656 | tf_op jit(solution)/shard_map/ppermute | solution.py:403
